TPU v7x, 512 devices: a whole 4x8x8 slice. The times are simulated.
512 devices in a mesh: tile: 128 (over z_lo, y, x, core), layer: 4 (over z_hi).
Axes of the slice: x: 4, y: 8, z: 8 (z_hi: 4, z_lo: 2; z = z_hi * 2 + z_lo), core: 2. Of those that a mesh axis runs over, the one named last changes fastest.
Arguments:
- rand_vectors: bfloat16 [4, 16, 1572864], P(None, None, ('tile', 'layer')), may hold values from -4 to 4
- onsite: bfloat16 [12288, 128, 128], P(('tile', 'layer')), as said below
- down_hop: bfloat16 [12288, 128, 128], P(('tile', 'layer')), may hold values from -0.1875 to 0.1875
- right_hop: bfloat16 [12288, 128, 128], P(('tile', 'layer')), may hold values from -0.1875 to 0.1875
- pattern: int32 [12288, 2], P(('tile', 'layer')), may hold values 0 or 1
- pairing: float32 [1572864], P(('tile', 'layer')), may hold values from 0.1 to 1
- link_rows: int32 [65536, 8], P(('tile', 'layer')), may hold values from 0 to 3071
- link_target: int32 [65536, 8], P(('tile', 'layer')), may hold values from 0 to 3071
- link_weight: bfloat16 [65536, 8], P(('tile', 'layer')), may hold values from -3 to 3
- link_count: int32 [65536], P(('tile', 'layer')), may hold values from 0 to 8, as said below
Outputs:
- cheb_one: float32 [4, 16, 1572864], P(None, None, ('tile', 'layer'))
- cheb_two: float32 [4, 16, 1572864], P(None, None, ('tile', 'layer'))
- moments: float32 [3, 4, 1572864], P(None, None, ('tile', 'layer'))
Inputs may be any that keep to these rules, and one draw needn't show every extreme that they name: `onsite`: every tile is symmetric. `link_rows`: a local site of the sending device. `link_target`: a local site of the receiving device. `link_count`: the number of used slots from one source tile row index to one receiving device; loads differ strongly between receiving tile row indices.
All inputs are finite; a program needn't handle non-finite values. No bound on the sum of `pattern` on one device may be relied on, other than what follows from the above.
Results may differ from a plain program's by a relative error of at most 0.0025.
Values may be sent and summed in bfloat16 or wider, within the bound.
No kernel may reach another device: no remote copies, remote signals or barrier semaphores. Data moves between devices by JAX's collectives and lax.ppermute only.
A program may use at most 64 MiB of HBM per device.

v0:
```python
import jax
import jax.numpy as jnp
from jax import lax
from jax.sharding import PartitionSpec as P

TILE = 128
TR = 4
TC = 6


def passed_along(value, axis, by):
    length = lax.axis_size(axis)
    pairs = [(i, i + by) for i in range(length) if 0 <= i + by < length]
    return lax.ppermute(value, axis, pairs)


def partner_2(value, axis, bit):
    return lax.ppermute(value, axis, [(i, i ^ 1 << bit) for i in range(lax.axis_size(axis))])


def with_halo(block, sides, width):
    for axis, dim in sides:
        count = lax.axis_size(axis)
        forward = [(i, i + 1) for i in range(count - 1)]
        backward = [(target, source) for source, target in forward]
        low = lax.ppermute(
            lax.slice_in_dim(block, block.shape[dim] - width, None, axis=dim), axis, forward
        )
        high = lax.ppermute(lax.slice_in_dim(block, 0, width, axis=dim), axis, backward)
        block = jnp.concatenate([low, block, high], axis=dim)
    return block


def hop_forward(tiles, field_grid):
    return jnp.einsum("rkij,nrkj->nrki", tiles, field_grid, preferred_element_type=jnp.float32)


def hop_transposed(tiles, field_grid):
    return jnp.einsum("rkji,nrkj->nrki", tiles, field_grid, preferred_element_type=jnp.float32)


def shards(
    rand_vectors,
    onsite,
    down_hop,
    right_hop,
    pattern,
    pairing,
    link_rows,
    link_target,
    link_weight,
    link_count,
):
    components, vectors, sites_dev = rand_vectors.shape
    field_rows = components * vectors
    tile_count = lax.axis_size("tile")
    slot_count = link_rows.shape[1]
    self_tiles = onsite.reshape(TR, TC, TILE, TILE)
    down_mask = (down_hop * pattern[:, 0][:, None, None].astype(jnp.bfloat16)).reshape(
        TR, TC, TILE, TILE
    )
    right_mask = (right_hop * pattern[:, 1][:, None, None].astype(jnp.bfloat16)).reshape(
        TR, TC, TILE, TILE
    )
    is_left = lax.axis_index("layer") % 2 == 0
    slot_live = jnp.arange(slot_count, dtype=jnp.int32)[None, :] < link_count[:, None]
    slot_weight = jnp.where(slot_live, link_weight.astype(jnp.float32), 0.0).reshape(-1)
    send_rows = link_rows.reshape(-1)
    recv_sites = link_target.reshape(-1)
    upper_blocks = passed_along(down_mask[TR - 1], "tile", 1)
    shifted_down = jnp.concatenate([upper_blocks[None], down_mask[:-1]], axis=0)
    weight_table = slot_weight.reshape(tile_count, slot_count).astype(jnp.bfloat16)
    weight_spread = lax.all_to_all(weight_table, "tile", split_axis=0, concat_axis=0, tiled=True)
    sender_weight = partner_2(weight_spread, "layer", 1).astype(jnp.float32).reshape(-1)

    def apply_hop(field_b):
        field_grid = field_b.reshape(field_rows, TR, TC, TILE)
        accumulated = hop_forward(self_tiles, field_grid)
        padded = with_halo(field_grid, (("tile", 1),), 1)
        accumulated = (
            accumulated
            + hop_forward(down_mask, padded[:, 2:])
            + hop_transposed(shifted_down, padded[:, :-2])
        )
        leftward = hop_transposed(right_mask, field_grid)
        payload = jnp.where(
            is_left, leftward[:, :, TC - 1], field_grid[:, :, 0].astype(jnp.float32)
        )
        partner = partner_2(payload, "layer", 0)
        right_edge = jnp.where(is_left, partner, 0.0).astype(jnp.bfloat16)
        accumulated = accumulated + hop_forward(
            right_mask, jnp.concatenate([field_grid[:, :, 1:], right_edge[:, :, None]], axis=2)
        )
        left_edge = jnp.where(is_left, 0.0, partner)
        accumulated = accumulated + jnp.concatenate(
            [left_edge[:, :, None], leftward[:, :, :-1]], axis=2
        )
        accumulated = accumulated.reshape(field_rows, sites_dev)
        flat_field = field_b.reshape(field_rows, sites_dev)
        outgoing = jnp.take(flat_field, send_rows, axis=1).reshape(
            field_rows, tile_count, slot_count
        )
        own_ends = jnp.take(flat_field, recv_sites, axis=1).reshape(
            field_rows, tile_count, slot_count
        )
        paired = jnp.concatenate([outgoing, own_ends], axis=2)
        paired_spread = lax.all_to_all(paired, "tile", split_axis=1, concat_axis=1, tiled=True)
        landed = partner_2(paired_spread, "layer", 1)
        arrived_terms = (
            landed[:, :, :slot_count].reshape(field_rows, -1).astype(jnp.float32)
            * slot_weight[None, :]
        )
        accumulated = accumulated.at[:, recv_sites].add(arrived_terms)
        returned_terms = (
            landed[:, :, slot_count:].reshape(field_rows, -1).astype(jnp.float32)
            * sender_weight[None, :]
        )
        accumulated = accumulated.at[:, send_rows].add(returned_terms)
        return accumulated.reshape(components, vectors, sites_dev)

    nambu_sign = jnp.array([1.0, 1.0, -1.0, -1.0], dtype=jnp.float32)[:, None, None]
    initial = rand_vectors.astype(jnp.float32)
    cheb_one = nambu_sign * apply_hop(rand_vectors) + pairing * jnp.roll(initial, 2, axis=0)
    one_rounded = cheb_one.astype(jnp.bfloat16)
    cheb_two = (
        2.0 * (nambu_sign * apply_hop(one_rounded) + pairing * jnp.roll(cheb_one, 2, axis=0))
        - initial
    )
    moments = jnp.stack(
        [
            jnp.mean(initial * initial, axis=1),
            jnp.mean(initial * cheb_one, axis=1),
            jnp.mean(initial * cheb_two, axis=1),
        ]
    )
    return (cheb_one, cheb_two, moments)


def solution(mesh):
    in_specs = (
        P(None, None, ("tile", "layer")),
        P(("tile", "layer"), None, None),
        P(("tile", "layer"), None, None),
        P(("tile", "layer"), None, None),
        P(("tile", "layer"), None),
        P(("tile", "layer")),
        P(("tile", "layer"), None),
        P(("tile", "layer"), None),
        P(("tile", "layer"), None),
        P(("tile", "layer")),
    )
    out_specs = (
        P(None, None, ("tile", "layer")),
        P(None, None, ("tile", "layer")),
        P(None, None, ("tile", "layer")),
    )
    return jax.shard_map(shards, mesh=mesh, in_specs=in_specs, out_specs=out_specs, check_vma=False)
```

profile of v0, /device:TPU:7, one launch (start us, length us, event | category | flops | bytes accessed | tf_op | source)
XLA Modules:
  0.0 250.8 jit_solution(17171188428479891034)
XLA Ops:
  3.7 5.8 %collective-permute-start.3 = (f32[64,4,128]{2,0,1:T(8,128)}, f32[64,4,128]{2,0,1:T(8,128)}, u32[]{:S(2)}, u32[]{:S(2)}) collective-permute-start(f32[64,4,128]{2,0,1:T(8,128)} %fusion.54), channel_id=1, source_target_pairs={{0,1},{1,0},{2,3},{3,2},{4,5},{5,4},{6,7},{7,6},{8,9},{9,8},{10,11... | collective-permute-start | bytes 393224 | tf_op jit(solution)/shard_map/ppermute | solution.py:18
  10.2 2.9 %collective-permute-start = (bf16[64,1,6,128]{3,0,2,1:T(8,128)(2,1)}, bf16[64,1,6,128]{3,0,2,1:T(8,128)(2,1)}, u32[]{:S(2)}, u32[]{:S(2)}) collective-permute-start(bf16[64,1,6,128]{3,0,2,1:T(8,128)(2,1)} %get-tuple-element.17), channel_id=1, source_target_pairs={{4,0},{8,4},{12,8},{16,12},{20,16},{24,20},{28,24},{32,28},{36,32}... | collective-permute-start | bytes 294920 | tf_op jit(solution)/shard_map/ppermute | solution.py:29
  13.1 4.8 %collective-permute-start.1 = (bf16[64,1,6,128]{3,0,2,1:T(8,128)(2,1)}, bf16[64,1,6,128]{3,0,2,1:T(8,128)(2,1)}, u32[]{:S(2)}, u32[]{:S(2)}) collective-permute-start(bf16[64,1,6,128]{3,0,2,1:T(8,128)(2,1)} %get-tuple-element.16), channel_id=1, source_target_pairs={{0,4},{4,8},{8,12},{12,16},{16,20},{20,24},{24,28},{28,32},{32,36}... | collective-permute-start | bytes 294920 | tf_op jit(solution)/shard_map/ppermute | solution.py:26
  22.3 13.1 %all-to-all-start.1 = ((bf16[128,1,8]{2,1,0:T(2,128)(2,1)}), bf16[128,1,8]{2,1,0:T(2,128)(2,1)S(1)}, u32[]{:S(2)}, u32[]{:S(2)}) async-start(bf16[128,1,8]{2,1,0:T(2,128)(2,1)} %copy.130), calls=%async_computation.1 | async-start | bytes 131072 | tf_op jit(solution)/shard_map/all_to_all | solution.py:73
  39.9 3.2 %gather_fusion = bf16[1024,64]{1,0:T(8,128)(2,1)S(1)} fusion(bf16[64,3072]{0,1:T(8,128)(2,1)S(1)} %copy.124, s32[1024]{0:T(1024)S(1)} %fusion.57), kind=kCustom, calls=%fused_computation.clone | custom fusion | bytes 266240 | tf_op jit(solution)/shard_map/jit(_take)/gather | solution.py:100
  43.2 4.3 %gather_fusion.1 = bf16[1024,64]{1,0:T(8,128)(2,1)} fusion(bf16[64,3072]{0,1:T(8,128)(2,1)S(1)} %copy.124, s32[1024]{0:T(1024)S(1)} %fusion.58), kind=kCustom, calls=%fused_computation.1.clone | custom fusion | bytes 266240 | tf_op jit(solution)/shard_map/jit(_take)/gather | solution.py:103
  52.5 12.9 %all-to-all-start = ((bf16[128,2,512]{2,1,0:T(2,128)(2,1)}), bf16[128,2,512]{2,1,0:T(2,128)(2,1)}, u32[]{:S(2)}, u32[]{:S(2)}) async-start(bf16[128,2,512]{2,1,0:T(2,128)(2,1)} %reshape.304), calls=%async_computation | async-start | bytes 524288 | tf_op jit(solution)/shard_map/all_to_all | solution.py:107
  66.1 7.9 %collective-permute-start.5 = (bf16[128,8]{0,1:T(8,128)(2,1)}, bf16[128,8]{0,1:T(8,128)(2,1)}, u32[]{:S(2)}, u32[]{:S(2)}) collective-permute-start(bf16[128,8]{0,1:T(8,128)(2,1)} %bitcast.27), channel_id=1, source_target_pairs={{0,2},{1,3},{2,0},{3,1},{4,6},{5,7},{6,4},{7,5},{8,10},{9,11},{10,... | collective-permute-start | bytes 6152 | tf_op jit(solution)/shard_map/ppermute | solution.py:18
  79.1 2.7 %convolution_add_fusion.3 = f32[4,6,64,128]{3,2,1,0:T(8,128)} fusion(f32[4,6,64,128]{3,2,1,0:T(8,128)} %fusion.72, bf16[4,6,128,128]{3,2,1,0:T(8,128)(2,1)S(1)} %bitcast.133, bf16[64,1,6,128]{3,0,2,1:T(8,128)(2,1)} %collective-permute-done, bf16[64,4,6,128]{3,0,2,1:T(8,128)(2,1)S(1)} %copy.110), kind=kOutput, calls=%fused_computation.20 | convolution fusion | flops 51511296 | bytes 2850816 | tf_op jit(solution)/shard_map/rkij,nrkj->nrki/dot_general | solution.py:35
  86.5 5.1 %collective-permute-start.4 = (bf16[64,128,16]{0,2,1:T(8,128)(2,1)}, bf16[64,128,16]{0,2,1:T(8,128)(2,1)}, u32[]{:S(2)}, u32[]{:S(2)}) collective-permute-start(bf16[64,128,16]{0,2,1:T(8,128)(2,1)} %bitcast.110), channel_id=1, source_target_pairs={{0,2},{1,3},{2,0},{3,1},{4,6},{5,7},{6,4},{7,5},{8,10},{9,11},{10,... | collective-permute-start | bytes 786440 | tf_op jit(solution)/shard_map/ppermute | solution.py:18
  91.7 2.9 %fusion.5 = f32[64,4,6,128]{3,0,2,1:T(8,128)} fusion(f32[4,6,64,128]{3,2,1,0:T(8,128)} %fusion.42, f32[4,6,64,128]{3,2,1,0:T(8,128)} %convolution_add_fusion.3, f32[64,4,5,128]{3,0,2,1:T(8,128)S(1)} %slice-done, f32[64,4,1,128]{3,0,2,1:T(8,128)S(1)} %select_bitcast_fusion.5, bf16[64,4,6,128]{3,0,2,1:T(8,128)(2,1)S(1)} %copy.110, ...), kind=kOutput, calls=%fused_computation.19 | convolution fusion | flops 53673984 | bytes 4423680 | tf_op jit(solution)/shard_map/rkji,nrkj->nrki/dot_general | solution.py:39
  96.2 20.6 %collective-permute-done.4 = bf16[64,128,16]{0,2,1:T(8,128)(2,1)} collective-permute-done((bf16[64,128,16]{0,2,1:T(8,128)(2,1)}, bf16[64,128,16]{0,2,1:T(8,128)(2,1)}, u32[]{:S(2)}, u32[]{:S(2)}) %collective-permute-start.4) | collective-permute-done | bytes 262176 | tf_op jit(solution)/shard_map/ppermute | solution.py:18
  116.8 7.1 %scatter_custom_fusion = f32[64,3072]{0,1:T(8,128)S(1)} fusion(f32[64,3072]{0,1:T(8,128)S(1)} %bitcast.126, s32[1024]{0:T(1024)} %bitcast.140, bf16[64,128,16]{0,2,1:T(8,128)(2,1)} %collective-permute-done.4, f32[1024]{0:T(1024)S(1)} %mul.125), kind=kCustom, calls=%fused_computation.54 | custom fusion | flops 196608 | bytes 1052672 | tf_op jit(solution)/shard_map/scatter-add | solution.py:113
  123.9 7.5 %scatter_custom_fusion.1 = f32[64,3072]{0,1:T(8,128)S(1)} fusion(f32[64,3072]{0,1:T(8,128)S(1)} %scatter_custom_fusion, s32[1024]{0:T(1024)} %bitcast.142, bf16[64,128,16]{0,2,1:T(8,128)(2,1)} %collective-permute-done.4, f32[1024]{0:T(1024)} %reshape.217), kind=kCustom, calls=%fused_computation.51 | custom fusion | flops 196608 | bytes 1052672 | tf_op jit(solution)/shard_map/scatter-add | solution.py:118
  135.3 2.8 %copy.149 = f32[64,3072]{0,1:T(8,128)} copy(f32[64,3072]{1,0:T(8,128)} %bitcast.135) | data formatting | bytes 1572864 | tf_op jit(solution)/shard_map/jit(_roll_static)/concatenate | solution.py:123
  138.1 2.8 %add_convert_fusion = bf16[64,3072]{0,1:T(8,128)(2,1)} fusion(f32[64,3072]{0,1:T(8,128)} %copy.149, f32[64,3072]{0,1:T(8,128)S(1)} %scatter_custom_fusion.1, f32[3072]{0:T(1024)S(1)} %copy-done.13, f32[64]{0:T(128)} %mul.136), kind=kLoop, calls=%fused_computation.8 | loop fusion | flops 786432 | bytes 1978624 | tf_op jit(solution)/shard_map/convert_element_type | solution.py:124
  140.9 5.6 %gather_fusion.2 = bf16[1024,64]{1,0:T(8,128)(2,1)} fusion(bf16[64,3072]{0,1:T(8,128)(2,1)} %add_convert_fusion, s32[1024]{0:T(1024)} %copy-done.16), kind=kCustom, calls=%fused_computation.2.clone | custom fusion | bytes 266240 | tf_op jit(solution)/shard_map/jit(_take)/gather | solution.py:100
  146.5 5.6 %gather_fusion.3 = bf16[1024,64]{1,0:T(8,128)(2,1)} fusion(bf16[64,3072]{0,1:T(8,128)(2,1)} %add_convert_fusion, s32[1024]{0:T(1024)} %copy-done.15), kind=kCustom, calls=%fused_computation.3.clone | custom fusion | bytes 266240 | tf_op jit(solution)/shard_map/jit(_take)/gather | solution.py:103
  163.4 13.8 %all-to-all-start.2 = ((bf16[128,2,512]{2,1,0:T(2,128)(2,1)}), bf16[128,2,512]{2,1,0:T(2,128)(2,1)}, u32[]{:S(2)}, u32[]{:S(2)}) async-start(bf16[128,2,512]{2,1,0:T(2,128)(2,1)} %reshape.306), calls=%async_computation.2 | async-start | bytes 524288 | tf_op jit(solution)/shard_map/all_to_all | solution.py:107
  182.4 5.6 %collective-permute-start.7 = (bf16[64,1,6,128]{3,0,1,2:T(8,128)(2,1)}, bf16[64,1,6,128]{3,0,1,2:T(8,128)(2,1)}, u32[]{:S(2)}, u32[]{:S(2)}) collective-permute-start(bf16[64,1,6,128]{3,0,1,2:T(8,128)(2,1)} %get-tuple-element.12), channel_id=1, source_target_pairs={{0,4},{4,8},{8,12},{12,16},{16,20},{20,24},{24,28},{28,32},{32,36}... | collective-permute-start | bytes 294920 | tf_op jit(solution)/shard_map/ppermute | solution.py:26
  196.7 4.8 %collective-permute-start.9 = (bf16[64,128,16]{0,2,1:T(8,128)(2,1)}, bf16[64,128,16]{0,2,1:T(8,128)(2,1)}, u32[]{:S(2)}, u32[]{:S(2)}) collective-permute-start(bf16[64,128,16]{0,2,1:T(8,128)(2,1)} %bitcast.112), channel_id=1, source_target_pairs={{0,2},{1,3},{2,0},{3,1},{4,6},{5,7},{6,4},{7,5},{8,10},{9,11},{10,... | collective-permute-start | bytes 786440 | tf_op jit(solution)/shard_map/ppermute | solution.py:18
  205.5 22.5 %collective-permute-done.9 = bf16[64,128,16]{0,2,1:T(8,128)(2,1)} collective-permute-done((bf16[64,128,16]{0,2,1:T(8,128)(2,1)}, bf16[64,128,16]{0,2,1:T(8,128)(2,1)}, u32[]{:S(2)}, u32[]{:S(2)}) %collective-permute-start.9) | collective-permute-done | bytes 262176 | tf_op jit(solution)/shard_map/ppermute | solution.py:18
  228.0 9.4 %scatter_custom_fusion.2 = f32[64,3072]{0,1:T(8,128)} fusion(f32[64,3072]{0,1:T(8,128)} %bitcast.136, s32[1024]{0:T(1024)} %bitcast.141, bf16[64,128,16]{0,2,1:T(8,128)(2,1)} %collective-permute-done.9, f32[1024]{0:T(1024)S(1)} %mul.125), kind=kCustom, calls=%fused_computation.48 | custom fusion | flops 196608 | bytes 1052672 | tf_op jit(solution)/shard_map/scatter-add | solution.py:113
  237.4 9.4 %scatter_custom_fusion.3 = f32[64,3072]{0,1:T(8,128)} fusion(f32[64,3072]{0,1:T(8,128)} %scatter_custom_fusion.2, s32[1024]{0:T(1024)} %bitcast.143, bf16[64,128,16]{0,2,1:T(8,128)(2,1)} %collective-permute-done.9, f32[1024]{0:T(1024)S(1)} %copy-done.14), kind=kCustom, calls=%fused_computation.45 | custom fusion | flops 196608 | bytes 1052672 | tf_op jit(solution)/shard_map/scatter-add | solution.py:118
  (141 shorter events, 66.3 us)
Async XLA Ops:
  0.6 37.4 %copy-start = (bf16[24,128,128]{2,1,0:T(8,128)(2,1)S(1)}, bf16[24,128,128]{2,1,0:T(8,128)(2,1)}, u32[]{:S(2)}) copy-start(bf16[24,128,128]{2,1,0:T(8,128)(2,1)} %param.14) | copy-start | bytes 2359300
  2.6 15.3 %copy-start.10 = (bf16[24,128,128]{2,1,0:T(8,128)(2,1)S(1)}, bf16[24,128,128]{2,1,0:T(8,128)(2,1)}, u32[]{:S(2)}) copy-start(bf16[24,128,128]{2,1,0:T(8,128)(2,1)} %param.15) | copy-start | bytes 2359300
  3.0 14.9 %copy-start.6 = (f32[64,4,6,128]{3,0,2,1:T(8,128)}, f32[64,4,6,128]{3,0,2,1:T(8,128)S(1)}, u32[]{:S(2)}) copy-start(f32[64,4,6,128]{3,0,2,1:T(8,128)S(1)} %convolution_bitcast_fusion) | copy-start | bytes 2359300
  3.0 18.6 %copy-start.22 = (bf16[128,8]{0,1:T(8,128)(2,1)S(1)}, bf16[128,8]{0,1:T(8,128)(2,1)}, u32[]{:S(2)}) copy-start(bf16[128,8]{0,1:T(8,128)(2,1)} %param.21) | copy-start | bytes 6148
  3.0 18.6 %copy-start.23 = (s32[128]{0:T(128)S(1)}, s32[128]{0:T(128)}, u32[]{:S(2)}) copy-start(s32[128]{0:T(128)} %param.22) | copy-start | bytes 1540
  3.0 32.4 %copy-start.20 = (s32[128,8]{0,1:T(8,128)S(1)}, s32[128,8]{0,1:T(8,128)}, u32[]{:S(2)}) copy-start(s32[128,8]{0,1:T(8,128)} %param.20) | copy-start | bytes 12292
  3.0 33.2 %copy-start.21 = (s32[128,8]{0,1:T(8,128)S(1)}, s32[128,8]{0,1:T(8,128)}, u32[]{:S(2)}) copy-start(s32[128,8]{0,1:T(8,128)} %param.19) | copy-start | bytes 12292
  3.0 34.1 %copy-start.1 = (bf16[4,16,3072]{2,1,0:T(8,128)(2,1)S(1)}, bf16[4,16,3072]{2,1,0:T(8,128)(2,1)}, u32[]{:S(2)}) copy-start(bf16[4,16,3072]{2,1,0:T(8,128)(2,1)} %param.13) | copy-start | bytes 1179652
  3.7 78.1 %collective-permute-start.3 = (f32[64,4,128]{2,0,1:T(8,128)}, f32[64,4,128]{2,0,1:T(8,128)}, u32[]{:S(2)}, u32[]{:S(2)}) collective-permute-start(f32[64,4,128]{2,0,1:T(8,128)} %fusion.54), channel_id=1, source_target_pairs={{0,1},{1,0},{2,3},{3,2},{4,5},{5,4},{6,7},{7,6},{8,9},{9,8},{10,11... | collective-permute-start | bytes 393224 | tf_op jit(solution)/shard_map/ppermute | solution.py:18
  10.2 68.9 %collective-permute-start = (bf16[64,1,6,128]{3,0,2,1:T(8,128)(2,1)}, bf16[64,1,6,128]{3,0,2,1:T(8,128)(2,1)}, u32[]{:S(2)}, u32[]{:S(2)}) collective-permute-start(bf16[64,1,6,128]{3,0,2,1:T(8,128)(2,1)} %get-tuple-element.17), channel_id=1, source_target_pairs={{4,0},{8,4},{12,8},{16,12},{20,16},{24,20},{28,24},{32,28},{36,32}... | collective-permute-start | bytes 294920 | tf_op jit(solution)/shard_map/ppermute | solution.py:29
  13.1 78.6 %collective-permute-start.1 = (bf16[64,1,6,128]{3,0,2,1:T(8,128)(2,1)}, bf16[64,1,6,128]{3,0,2,1:T(8,128)(2,1)}, u32[]{:S(2)}, u32[]{:S(2)}) collective-permute-start(bf16[64,1,6,128]{3,0,2,1:T(8,128)(2,1)} %get-tuple-element.16), channel_id=1, source_target_pairs={{0,4},{4,8},{8,12},{12,16},{16,20},{20,24},{24,28},{28,32},{32,36}... | collective-permute-start | bytes 294920 | tf_op jit(solution)/shard_map/ppermute | solution.py:26
  19.6 72.0 %collective-permute-start.2 = (bf16[6,128,128]{2,1,0:T(8,128)(2,1)}, bf16[6,128,128]{2,1,0:T(8,128)(2,1)}, u32[]{:S(2)}, u32[]{:S(2)}) collective-permute-start(bf16[6,128,128]{2,1,0:T(8,128)(2,1)} %slice.135), channel_id=1, source_target_pairs={{0,4},{4,8},{8,12},{12,16},{16,20},{20,24},{24,28},{28,32},{32,36}... | collective-permute-start | bytes 589832 | tf_op jit(solution)/shard_map/ppermute | solution.py:14
  22.3 30.2 %all-to-all-start.1 = ((bf16[128,1,8]{2,1,0:T(2,128)(2,1)}), bf16[128,1,8]{2,1,0:T(2,128)(2,1)S(1)}, u32[]{:S(2)}, u32[]{:S(2)}) async-start(bf16[128,1,8]{2,1,0:T(2,128)(2,1)} %copy.130), calls=%async_computation.1 | async-start | bytes 131072 | tf_op jit(solution)/shard_map/all_to_all | solution.py:73
  50.4 24.3 %copy-start.3 = (bf16[24,128,128]{2,1,0:T(8,128)(2,1)S(1)}, bf16[24,128,128]{2,1,0:T(8,128)(2,1)}, u32[]{:S(2)}) copy-start(bf16[24,128,128]{2,1,0:T(8,128)(2,1)} %copy-done.2) | copy-start | bytes 2359300
  52.5 31.8 %all-to-all-start = ((bf16[128,2,512]{2,1,0:T(2,128)(2,1)}), bf16[128,2,512]{2,1,0:T(2,128)(2,1)}, u32[]{:S(2)}, u32[]{:S(2)}) async-start(bf16[128,2,512]{2,1,0:T(2,128)(2,1)} %reshape.304), calls=%async_computation | async-start | bytes 524288 | tf_op jit(solution)/shard_map/all_to_all | solution.py:107
  66.1 11.6 %collective-permute-start.5 = (bf16[128,8]{0,1:T(8,128)(2,1)}, bf16[128,8]{0,1:T(8,128)(2,1)}, u32[]{:S(2)}, u32[]{:S(2)}) collective-permute-start(bf16[128,8]{0,1:T(8,128)(2,1)} %bitcast.27), channel_id=1, source_target_pairs={{0,2},{1,3},{2,0},{3,1},{4,6},{5,7},{6,4},{7,5},{8,10},{9,11},{10,... | collective-permute-start | bytes 6152 | tf_op jit(solution)/shard_map/ppermute | solution.py:18
  86.5 30.3 %collective-permute-start.4 = (bf16[64,128,16]{0,2,1:T(8,128)(2,1)}, bf16[64,128,16]{0,2,1:T(8,128)(2,1)}, u32[]{:S(2)}, u32[]{:S(2)}) collective-permute-start(bf16[64,128,16]{0,2,1:T(8,128)(2,1)} %bitcast.110), channel_id=1, source_target_pairs={{0,2},{1,3},{2,0},{3,1},{4,6},{5,7},{6,4},{7,5},{8,10},{9,11},{10,... | collective-permute-start | bytes 786440 | tf_op jit(solution)/shard_map/ppermute | solution.py:18
  160.2 27.8 %copy-start.5 = (f32[4,16,3072]{2,1,0:T(8,128)S(1)}, f32[4,16,3072]{2,1,0:T(8,128)}, u32[]{:S(2)}) copy-start(f32[4,16,3072]{2,1,0:T(8,128)} %get-tuple-element.9) | copy-start | bytes 2359300
  163.4 31.2 %all-to-all-start.2 = ((bf16[128,2,512]{2,1,0:T(2,128)(2,1)}), bf16[128,2,512]{2,1,0:T(2,128)(2,1)}, u32[]{:S(2)}, u32[]{:S(2)}) async-start(bf16[128,2,512]{2,1,0:T(2,128)(2,1)} %reshape.306), calls=%async_computation.2 | async-start | bytes 524288 | tf_op jit(solution)/shard_map/all_to_all | solution.py:107
  177.2 13.6 %collective-permute-start.6 = (bf16[64,1,6,128]{3,0,1,2:T(8,128)(2,1)}, bf16[64,1,6,128]{3,0,1,2:T(8,128)(2,1)S(1)}, u32[]{:S(2)}, u32[]{:S(2)}) collective-permute-start(bf16[64,1,6,128]{3,0,1,2:T(8,128)(2,1)} %get-tuple-element.13), channel_id=1, source_target_pairs={{4,0},{8,4},{12,8},{16,12},{20,16},{24,20},{28,24},{32,28},{36,32}... | collective-permute-start | bytes 294920 | tf_op jit(solution)/shard_map/ppermute | solution.py:29
  180.4 11.9 %collective-permute-start.8 = (f32[64,4,128]{2,0,1:T(8,128)S(1)}, f32[64,4,128]{2,0,1:T(8,128)S(1)}, u32[]{:S(2)}, u32[]{:S(2)}) collective-permute-start(f32[64,4,128]{2,0,1:T(8,128)S(1)} %fusion.53), channel_id=1, source_target_pairs={{0,1},{1,0},{2,3},{3,2},{4,5},{5,4},{6,7},{7,6},{8,9},{9,8},{10,11... | collective-permute-start | bytes 393224 | tf_op jit(solution)/shard_map/ppermute | solution.py:18
  182.4 19.2 %collective-permute-start.7 = (bf16[64,1,6,128]{3,0,1,2:T(8,128)(2,1)}, bf16[64,1,6,128]{3,0,1,2:T(8,128)(2,1)}, u32[]{:S(2)}, u32[]{:S(2)}) collective-permute-start(bf16[64,1,6,128]{3,0,1,2:T(8,128)(2,1)} %get-tuple-element.12), channel_id=1, source_target_pairs={{0,4},{4,8},{8,12},{12,16},{16,20},{20,24},{24,28},{28,32},{32,36}... | collective-permute-start | bytes 294920 | tf_op jit(solution)/shard_map/ppermute | solution.py:26
  196.7 31.3 %collective-permute-start.9 = (bf16[64,128,16]{0,2,1:T(8,128)(2,1)}, bf16[64,128,16]{0,2,1:T(8,128)(2,1)}, u32[]{:S(2)}, u32[]{:S(2)}) collective-permute-start(bf16[64,128,16]{0,2,1:T(8,128)(2,1)} %bitcast.112), channel_id=1, source_target_pairs={{0,2},{1,3},{2,0},{3,1},{4,6},{5,7},{6,4},{7,5},{8,10},{9,11},{10,... | collective-permute-start | bytes 786440 | tf_op jit(solution)/shard_map/ppermute | solution.py:18
  203.8 33.6 %copy-start.14 = (f32[1024]{0:T(1024)S(1)}, f32[1024]{0:T(1024)}, u32[]{:S(2)}) copy-start(f32[1024]{0:T(1024)} %reshape.217) | copy-start | bytes 12292
  (15 other events, 43.1 us)
where the time goes:
time: 252 us; the launch traced here: 251 us
  starting transfers between devices  82.9 us (33%)
  local copies, waits for them, and re-layouts  55.3 us (22%)
  other arithmetic  52.2 us (21%)
  waiting for transfers between devices  43.1 us (17%)
  matrix products  16 us (6%)
    ppermute x5, waiting for transfers between devices, partner_2(): lax.ppermute(value, axis, [(i, i ^ 1 << bit) for i in range(lax.axis_size...  43.1 us
    all_to_all x2, starting transfers between devices, apply_hop(): lax.all_to_all(paired, 'tile', split_axis=1, concat_axis=1, tiled=True)  26.7 us
    ppermute x5, starting transfers between devices, partner_2(): lax.ppermute(value, axis, [(i, i ^ 1 << bit) for i in range(lax.axis_size...  25.6 us
    scatter-add x2, other arithmetic, apply_hop(): accumulated = accumulated.at[:, send_rows].add(returned_terms)  16.9 us
    scatter-add x2, other arithmetic, apply_hop(): accumulated = accumulated.at[:, recv_sites].add(arrived_terms)  16.6 us
    all_to_all x1, starting transfers between devices, shards(): lax.all_to_all(weight_table, 'tile', split_axis=0, concat_axis=0, tiled=T...  13.1 us
    ppermute x2, starting transfers between devices, with_halo(): lax.ppermute(lax.slice_in_dim(block, block.shape[dim] - width, None, axis...  10.4 us
    unnamed x56, local copies, waits for them, and re-layouts  10.2 us
  transfers between devices with their start and end apart: 13, of which 2 were waited for; matrix products, arithmetic and copies ran while one was open for 20% of the time, Pallas kernels for 0%

commit v1 on v0

v1 whole, which is shorter than its diff:
```python
import jax
import jax.numpy as jnp
from jax import lax
from jax.experimental import pallas as pl
from jax.experimental.pallas import tpu as pltpu
from jax.sharding import PartitionSpec as P

TILE = 128
TR = 4
TC = 6
ROWS = 64
SITES_DEV = TR * TC * TILE
PEERS = 128
CAP = 8
SLOTS = PEERS * CAP
SPAN = 256
HI = SITES_DEV // SPAN
F32 = jnp.float32
BF16 = jnp.bfloat16
NT = (((1,), (1,)), ((), ()))
NN = (((1,), (0,)), ((), ()))
VMEM_LIMIT = 56 * 1024 * 1024


def dot(a, b, dims=NN):
    return lax.dot_general(a, b, dims, preferred_element_type=F32)


def per_slot(table):
    spread = jnp.broadcast_to(table.astype(F32)[:, None, :], (PEERS, CAP, CAP)).reshape(SLOTS, CAP)
    own = lax.broadcasted_iota(jnp.int32, (SLOTS, CAP), 0) % CAP == lax.broadcasted_iota(
        jnp.int32, (SLOTS, CAP), 1
    )
    picked = jnp.where(own, spread, 0.0).astype(BF16)
    return dot(picked, jnp.ones((CAP, TILE), BF16))


def gather_into(x, hot_ref, high_ref, out_ref):
    chunk = 256
    lane = lax.broadcasted_iota(jnp.int32, (chunk, TILE), 1)
    half = (lane >= ROWS).astype(F32)
    pieces = []
    for q in range(HI // 2):
        pieces.append(
            jnp.concatenate(
                [x[:, 2 * q * SPAN : (2 * q + 1) * SPAN], x[:, (2 * q + 1) * SPAN : (2 * q + 2) * SPAN]],
                axis=0,
            )
        )
    for start in range(0, SLOTS, chunk):
        ends = []
        for end in range(2):
            hot = hot_ref[end * SLOTS + start : end * SLOTS + start + chunk, :]
            high = high_ref[end * SLOTS + start : end * SLOTS + start + chunk, :] - half
            total = jnp.zeros((chunk, TILE), F32)
            for q in range(HI // 2):
                total = jnp.where(high == 2.0 * q, dot(hot, pieces[q], NT), total)
            ends.append(total + pltpu.roll(total, ROWS, 1))
        out_ref[start : start + chunk, :] = jnp.where(lane < ROWS, ends[0], ends[1]).astype(BF16)


def prepare_kernel(x_ref, rows_ref, target_ref, weight_ref, count_ref, hot_ref, high_ref, out_ref):
    lane = lax.broadcasted_iota(jnp.int32, (SLOTS, SPAN), 1).astype(F32)
    live = lax.broadcasted_iota(jnp.int32, (PEERS, CAP), 1) < count_ref[...]
    weight = per_slot(jnp.where(live, weight_ref[...].astype(F32), 0.0))
    for end, table_ref in ((0, rows_ref), (1, target_ref)):
        table = table_ref[...]
        low = per_slot(table % SPAN)
        high_ref[end * SLOTS : (end + 1) * SLOTS, :] = per_slot(table // SPAN)
        low = jnp.concatenate([low, low], axis=1)
        value = 1.0 if end == 0 else jnp.concatenate([weight, weight], axis=1)
        hot_ref[end * SLOTS : (end + 1) * SLOTS, :] = jnp.where(lane == low, value, 0.0).astype(BF16)
    gather_into(x_ref[...], hot_ref, high_ref, out_ref)


def prepare(x, link_rows, link_target, link_weight, link_count):
    return pl.pallas_call(
        prepare_kernel,
        out_shape=(
            jax.ShapeDtypeStruct((2 * SLOTS, SPAN), BF16),
            jax.ShapeDtypeStruct((2 * SLOTS, TILE), F32),
            jax.ShapeDtypeStruct((SLOTS, 2 * ROWS), BF16),
        ),
        compiler_params=pltpu.CompilerParams(vmem_limit_bytes=VMEM_LIMIT),
        name="prepare",
    )(x, link_rows, link_target, link_weight, link_count.reshape(PEERS, 1))


def edges_kernel(pattern_ref, left_ref, x_ref, down_ref, right_ref, below_ref, side_ref):
    x = x_ref[...]
    for k in range(TC):
        tile = (TR - 1) * TC + k
        keep = pattern_ref[tile, 0].astype(F32)
        below_ref[:, k * TILE : (k + 1) * TILE] = keep * dot(
            x[:, tile * TILE : (tile + 1) * TILE], down_ref[k]
        )
    is_left = left_ref[0] == 1
    for r in range(TR):
        last = r * TC + TC - 1
        keep = pattern_ref[last, 1].astype(F32)
        product = keep * dot(x[:, last * TILE : (last + 1) * TILE], right_ref[r, 0])
        first = x[:, r * TC * TILE : (r * TC + 1) * TILE].astype(F32)
        side_ref[:, r * TILE : (r + 1) * TILE] = jnp.where(is_left, product, first)


def edges(pattern, left_flag, x, down_hop, right_hop):
    return pl.pallas_call(
        edges_kernel,
        grid=(1,),
        in_specs=[
            pl.BlockSpec(memory_space=pltpu.SMEM),
            pl.BlockSpec(memory_space=pltpu.SMEM),
            pl.BlockSpec((ROWS, SITES_DEV), lambda i: (0, 0)),
            pl.BlockSpec((TC, TILE, TILE), lambda i: (TR - 1, 0, 0)),
            pl.BlockSpec((TR, 1, TILE, TILE), lambda i: (0, TC - 1, 0, 0)),
        ],
        out_specs=(
            pl.BlockSpec((ROWS, TC * TILE), lambda i: (0, 0)),
            pl.BlockSpec((ROWS, TR * TILE), lambda i: (0, 0)),
        ),
        out_shape=(
            jax.ShapeDtypeStruct((ROWS, TC * TILE), F32),
            jax.ShapeDtypeStruct((ROWS, TR * TILE), F32),
        ),
        compiler_params=pltpu.CompilerParams(vmem_limit_bytes=VMEM_LIMIT),
        name="edges",
    )(pattern, left_flag, x, down_hop, right_hop.reshape(TR, TC, TILE, TILE))


def intra_kernel(
    pattern_ref, left_ref, x_ref, onsite_ref, down_ref, right_ref, above_ref, below_ref, side_ref, out_ref
):
    is_left = left_ref[0] == 1
    x = x_ref[...]

    def block(tile):
        return x[:, tile * TILE : (tile + 1) * TILE]

    def kept(tile, which, value):
        return jnp.where(pattern_ref[tile, which] == 1, value, jnp.zeros_like(value))

    for r in range(TR):
        for k in range(TC):
            tile = r * TC + k
            fields = [block(tile)]
            tiles = [onsite_ref[tile]]
            if r > 0:
                fields.append(kept(tile - TC, 0, block(tile - TC)))
                tiles.append(down_ref[tile - TC])
            if k > 0:
                fields.append(kept(tile - 1, 1, block(tile - 1)))
                tiles.append(right_ref[tile - 1])
            total = dot(jnp.concatenate(fields, axis=1), jnp.concatenate(tiles, axis=0))
            lower = block(tile + TC) if r < TR - 1 else below_ref[:, k * TILE : (k + 1) * TILE]
            if k < TC - 1:
                righter = block(tile + 1)
            else:
                edge = side_ref[:, r * TILE : (r + 1) * TILE]
                righter = jnp.where(is_left, edge, 0.0).astype(BF16)
            total = total + dot(
                jnp.concatenate([kept(tile, 0, lower), kept(tile, 1, righter)], axis=1),
                jnp.concatenate([down_ref[tile], right_ref[tile]], axis=1),
                NT,
            )
            if r == 0:
                total = total + above_ref[:, k * TILE : (k + 1) * TILE]
            if k == 0:
                edge = side_ref[:, r * TILE : (r + 1) * TILE]
                total = total + jnp.where(is_left, 0.0, edge)
            out_ref[:, tile * TILE : (tile + 1) * TILE] = total


def intra(pattern, left_flag, x, onsite, down_hop, right_hop, above, below, side):
    smem = pl.BlockSpec(memory_space=pltpu.SMEM)
    vmem = pl.BlockSpec(memory_space=pltpu.VMEM)
    return pl.pallas_call(
        intra_kernel,
        in_specs=[smem, smem] + [vmem] * 7,
        out_shape=jax.ShapeDtypeStruct((ROWS, SITES_DEV), F32),
        compiler_params=pltpu.CompilerParams(vmem_limit_bytes=VMEM_LIMIT),
        name="intra",
    )(pattern, left_flag, x, onsite, down_hop, right_hop, above, below, side)


def scatter_into(landed, hot_ref, high_ref, mask_ref, total_ref):
    turned = landed.astype(F32).T.astype(BF16)
    high_send = high_ref[0:SLOTS, :].T.astype(BF16)[:ROWS]
    high_recv = high_ref[SLOTS : 2 * SLOTS, :].T.astype(BF16)[:ROWS]
    zero = jnp.zeros((ROWS, SLOTS), BF16)
    for h in range(HI):
        mask_ref[h * ROWS : (h + 1) * ROWS, 0:SLOTS] = jnp.where(
            high_send == BF16(h), turned[ROWS:], zero
        )
        mask_ref[h * ROWS : (h + 1) * ROWS, SLOTS : 2 * SLOTS] = jnp.where(
            high_recv == BF16(h), turned[:ROWS], zero
        )
    group = 4
    for start in range(0, HI, group):
        total_ref[start * ROWS : (start + group) * ROWS, :] = dot(
            mask_ref[start * ROWS : (start + group) * ROWS, :], hot_ref[...]
        )


def signed(value):
    return jnp.where(lax.broadcasted_iota(jnp.int32, value.shape, 0) < ROWS // 2, value, -value)


def swapped(value):
    return jnp.concatenate([value[ROWS // 2 :], value[: ROWS // 2]], axis=0)


def vector_mean(value):
    comps = value.reshape(4, 16, value.shape[-1])
    return jnp.sum(comps, axis=1) * (1.0 / 16.0)


def first_kernel(
    v0_ref, landed_ref, hot_ref, high_ref, intra_ref, pairing_ref, one_ref, x_ref, mom_ref, out_ref, mask_ref, total_ref
):
    scatter_into(landed_ref[...], hot_ref, high_ref, mask_ref, total_ref)
    for h in range(HI):
        cols = slice(h * SPAN, (h + 1) * SPAN)
        hop = total_ref[h * ROWS : (h + 1) * ROWS, :] + intra_ref[:, cols]
        v0 = v0_ref[:, cols].astype(F32)
        one = signed(hop) + pairing_ref[:, cols] * swapped(v0)
        one_ref[:, cols] = one
        x_ref[:, cols] = one.astype(BF16)
        mom_ref[0:4, cols] = vector_mean(v0 * v0)
        mom_ref[4:8, cols] = vector_mean(v0 * one)
    gather_into(x_ref[...], hot_ref, high_ref, out_ref)


def first(v0, landed, hot, high, intra_part, pairing):
    return pl.pallas_call(
        first_kernel,
        out_shape=(
            jax.ShapeDtypeStruct((ROWS, SITES_DEV), F32),
            jax.ShapeDtypeStruct((ROWS, SITES_DEV), BF16),
            jax.ShapeDtypeStruct((8, SITES_DEV), F32),
            jax.ShapeDtypeStruct((SLOTS, 2 * ROWS), BF16),
        ),
        scratch_shapes=[pltpu.VMEM((HI * ROWS, 2 * SLOTS), BF16), pltpu.VMEM((HI * ROWS, SPAN), F32)],
        compiler_params=pltpu.CompilerParams(vmem_limit_bytes=VMEM_LIMIT),
        name="first",
    )(v0, landed, hot, high, intra_part, pairing)


def second_kernel(
    v0_ref, one_ref, landed_ref, hot_ref, high_ref, intra_ref, pairing_ref, mom_in_ref, two_ref, mom_ref, mask_ref, total_ref
):
    scatter_into(landed_ref[...], hot_ref, high_ref, mask_ref, total_ref)
    mom_ref[0:8, :] = mom_in_ref[...]
    for h in range(HI):
        cols = slice(h * SPAN, (h + 1) * SPAN)
        hop = total_ref[h * ROWS : (h + 1) * ROWS, :] + intra_ref[:, cols]
        v0 = v0_ref[:, cols].astype(F32)
        two = 2.0 * (signed(hop) + pairing_ref[:, cols] * swapped(one_ref[:, cols])) - v0
        two_ref[:, cols] = two
        mom_ref[8:12, cols] = vector_mean(v0 * two)


def second(v0, one, landed, hot, high, intra_part, pairing, mom):
    return pl.pallas_call(
        second_kernel,
        out_shape=(
            jax.ShapeDtypeStruct((ROWS, SITES_DEV), F32),
            jax.ShapeDtypeStruct((12, SITES_DEV), F32),
        ),
        scratch_shapes=[pltpu.VMEM((HI * ROWS, 2 * SLOTS), BF16), pltpu.VMEM((HI * ROWS, SPAN), F32)],
        compiler_params=pltpu.CompilerParams(vmem_limit_bytes=VMEM_LIMIT),
        name="second",
    )(v0, one, landed, hot, high, intra_part, pairing, mom)


def passed_along(value, axis, by):
    length = lax.axis_size(axis)
    pairs = [(i, i + by) for i in range(length) if 0 <= i + by < length]
    return lax.ppermute(value, axis, pairs)


def partner_2(value, axis, bit):
    return lax.ppermute(value, axis, [(i, i ^ 1 << bit) for i in range(lax.axis_size(axis))])


def exchange(payload):
    spread = lax.all_to_all(
        payload.reshape(PEERS, CAP, 2 * ROWS), "tile", split_axis=0, concat_axis=0, tiled=True
    )
    return partner_2(spread, "layer", 1).reshape(SLOTS, 2 * ROWS)


def shards(
    rand_vectors,
    onsite,
    down_hop,
    right_hop,
    pattern,
    pairing,
    link_rows,
    link_target,
    link_weight,
    link_count,
):
    v0 = rand_vectors.reshape(ROWS, SITES_DEV)
    pairing = pairing.reshape(1, SITES_DEV)
    left_flag = (1 - lax.axis_index("layer") % 2).astype(jnp.int32).reshape(1)

    def intra_of(x):
        below_part, side_part = edges(pattern, left_flag, x, down_hop, right_hop)
        above = passed_along(below_part, "tile", 1)
        below = passed_along(x[:, : TC * TILE], "tile", -1)
        side = partner_2(side_part, "layer", 0)
        return intra(pattern, left_flag, x, onsite, down_hop, right_hop, above, below, side)

    hot, high, payload = prepare(v0, link_rows, link_target, link_weight, link_count)
    landed = exchange(payload)
    one, x, mom, payload = first(v0, landed, hot, high, intra_of(v0), pairing)
    landed = exchange(payload)
    two, mom = second(v0, one, landed, hot, high, intra_of(x), pairing, mom)
    shape = rand_vectors.shape
    return one.reshape(shape), two.reshape(shape), mom.reshape(3, 4, SITES_DEV)


def solution(mesh):
    both = ("tile", "layer")
    in_specs = (
        P(None, None, both),
        P(both, None, None),
        P(both, None, None),
        P(both, None, None),
        P(both, None),
        P(both),
        P(both, None),
        P(both, None),
        P(both, None),
        P(both),
    )
    out_specs = (P(None, None, both), P(None, None, both), P(None, None, both))
    return jax.shard_map(shards, mesh=mesh, in_specs=in_specs, out_specs=out_specs, check_vma=False)
```

time: 252 us -> 139 us (0.55)
  the two profiles are of different devices: /device:TPU:7 before, /device:TPU:1 now
where the time goes in v1:
time: 139 us
  blocking collectives  55.4 us (40%)
  starting transfers between devices  27.2 us (20%)
  Pallas kernels  26.1 us (19%)
  waiting for transfers between devices  16.1 us (12%)
  local copies, waits for them, and re-layouts  13.1 us (9%)
    all_to_all x2, blocking collectives, exchange(): lax.all_to_all(payload.reshape(PEERS, CAP, 2 * ROWS), 'tile', split_axis=...  55.4 us
    ppermute x4, starting transfers between devices, partner_2(): lax.ppermute(value, axis, [(i, i ^ 1 << bit) for i in range(lax.axis_size...  18.3 us
    unnamed x28, local copies, waits for them, and re-layouts  8.95 us
    ppermute x4, starting transfers between devices, passed_along(): return lax.ppermute(value, axis, pairs)  8.9 us
    ppermute x4, waiting for transfers between devices, passed_along(): return lax.ppermute(value, axis, pairs)  8.56 us
    ppermute x4, waiting for transfers between devices, partner_2(): lax.ppermute(value, axis, [(i, i ^ 1 << bit) for i in range(lax.axis_size...  7.55 us
    pallas_call x2, Pallas kernels, intra(): pl.pallas_call(intra_kernel, in_specs=[smem, smem] + [vmem] * 7, out_shap...  7.38 us
    pallas_call x1, Pallas kernels, first(): pl.pallas_call(first_kernel, out_shape=(jax.ShapeDtypeStruct((ROWS, SITES...  5.98 us
  transfers between devices with their start and end apart: 8, of which 4 were waited for; matrix products, arithmetic and copies ran while one was open for 2% of the time, Pallas kernels for 8%

profile of v1, /device:TPU:1, one launch (start us, length us, event | category | flops | bytes accessed | tf_op | source)
XLA Modules:
  0.0 138.7 jit_solution(8296837576176071129)
XLA Ops:
  0.6 1.4 %copy.15.weight_ref = bf16[128,8]{1,0:T(8,128)(2,1)} copy(bf16[128,8]{0,1:T(8,128)(2,1)} %param.18) | data formatting | bytes 4096 | tf_op args[8]
  4.9 4.4 %prepare.1 = (bf16[2048,256]{1,0:T(8,128)(2,1)}, f32[2048,128]{1,0:T(8,128)}, bf16[1024,128]{1,0:T(8,128)(2,1)}) custom-call(bf16[64,3072]{1,0:T(8,128)(2,1)} %bitcast.13, s32[128,8]{1,0:T(8,128)} %copy.13.rows_ref, s32[128,8]{1,0:T(8,128)} %copy.14.target_ref, bf16[128,8]{1,0:T(8,128)(2,1)} %copy.15.weight_ref, s32[128,1]{1,0:T(8,128)} %copy.16.count_ref), custom_call_target="tpu_custom_call" | custom-call | tf_op jit(solution)/shard_map/prepare/pallas_call | solution.py:77
  9.3 29.3 %all_to_all.10 = bf16[128,8,128]{2,1,0:T(8,128)(2,1)S(1)} all-to-all(bf16[128,8,128]{2,1,0:T(8,128)(2,1)} %bitcast.21), channel_id=1, replica_groups=mesh['tile'=128,'layer'=4] {'tile'}, dimensions={0} | all-to-all | bytes 524288 | tf_op jit(solution)/shard_map/all_to_all | solution.py:286
  38.6 9.7 %collective-permute-start = (bf16[128,8,128]{2,1,0:T(8,128)(2,1)S(1)}, bf16[128,8,128]{2,1,0:T(8,128)(2,1)S(1)}, u32[]{:S(2)}, u32[]{:S(2)}) collective-permute-start(bf16[128,8,128]{2,1,0:T(8,128)(2,1)S(1)} %all_to_all.10), channel_id=1, source_target_pairs={{0,2},{1,3},{2,0},{3,1},{4,6},{5,7},{6,4},{7,5},{8,10},{9,11},{10,... | collective-permute-start | bytes 786440 | tf_op jit(solution)/shard_map/ppermute | solution.py:282
  49.7 2.0 %edges.2 = (f32[64,768]{1,0:T(8,128)}, f32[64,512]{1,0:T(8,128)}) custom-call(s32[24,2]{1,0:T(8,128)} %copy.18.pattern_ref, s32[1]{0:T(128)} %bitcast.4.left_ref, bf16[64,3072]{1,0:T(8,128)(2,1)} %bitcast.14, bf16[24,128,128]{2,1,0:T(8,128)(2,1)} %down_ref.7, bf16[4,6,128,128]{3,2,1,0:T(8,128)(2,1)} %bitcast.11), custom_call_target="tpu_custom_call" | custom-call | tf_op jit(solution)/shard_map/edges/pallas_call | solution.py:107
  51.7 2.7 %collective-permute-start.1 = (f32[64,768]{1,0:T(8,128)}, f32[64,768]{1,0:T(8,128)S(1)}, u32[]{:S(2)}, u32[]{:S(2)}) collective-permute-start(f32[64,768]{1,0:T(8,128)} %get-tuple-element.19), channel_id=1, source_target_pairs={{0,4},{4,8},{8,12},{12,16},{16,20},{20,24},{24,28},{28,32},{32,36}... | collective-permute-start | bytes 589832 | tf_op jit(solution)/shard_map/ppermute | solution.py:278
  54.4 4.0 %collective-permute-start.3 = (f32[64,512]{1,0:T(8,128)}, f32[64,512]{1,0:T(8,128)S(1)}, u32[]{:S(2)}, u32[]{:S(2)}) collective-permute-start(f32[64,512]{1,0:T(8,128)} %get-tuple-element.20), channel_id=1, source_target_pairs={{0,1},{1,0},{2,3},{3,2},{4,5},{5,4},{6,7},{7,6},{8,9},{9,8},{10,11... | collective-permute-start | bytes 393224 | tf_op jit(solution)/shard_map/ppermute | solution.py:282
  58.4 0.9 slice.8
  59.3 1.9 %collective-permute-start.2 = (bf16[64,768]{1,0:T(8,128)(2,1)S(1)}, bf16[64,768]{1,0:T(8,128)(2,1)S(1)}, u32[]{:S(2)}, u32[]{:S(2)}) collective-permute-start(bf16[64,768]{1,0:T(8,128)(2,1)S(1)} %slice.8), channel_id=1, source_target_pairs={{4,0},{8,4},{12,8},{16,12},{20,16},{24,20},{28,24},{32,28},{36,32}... | collective-permute-start | bytes 294920 | tf_op jit(solution)/shard_map/ppermute | solution.py:278
  61.3 4.3 %collective-permute-done.2.below_ref = bf16[64,768]{1,0:T(8,128)(2,1)S(1)} collective-permute-done((bf16[64,768]{1,0:T(8,128)(2,1)S(1)}, bf16[64,768]{1,0:T(8,128)(2,1)S(1)}, u32[]{:S(2)}, u32[]{:S(2)}) %collective-permute-start.2) | collective-permute-done | bytes 98336 | tf_op jit(solution)/shard_map/ppermute | solution.py:278
  67.5 3.7 %intra.2.intra_ref = f32[64,3072]{1,0:T(8,128)} custom-call(s32[24,2]{1,0:T(8,128)} %copy.18.pattern_ref, s32[1]{0:T(128)} %bitcast.4.left_ref, bf16[64,3072]{1,0:T(8,128)(2,1)} %bitcast.16, bf16[24,128,128]{2,1,0:T(8,128)(2,1)} %onsite_ref.3, bf16[24,128,128]{2,1,0:T(8,128)(2,1)} %down_ref.7, bf16[24,128,128]{2,1,0:T(8,128)(2,1)} %right_ref.3, ...), custom_call_target="tpu_custom_call" | custom-call | tf_op jit(solution)/shard_map/intra/pallas_call | solution.py:176
  71.9 6.0 %first.1 = (f32[64,3072]{1,0:T(8,128)}, bf16[64,3072]{1,0:T(8,128)(2,1)}, f32[8,3072]{1,0:T(8,128)}, bf16[1024,128]{1,0:T(8,128)(2,1)}) custom-call(bf16[64,3072]{1,0:T(8,128)(2,1)} %bitcast.17, bf16[1024,128]{1,0:T(8,128)(2,1)} %bitcast.23, bf16[2048,256]{1,0:T(8,128)(2,1)} %get-tuple-element.17.hot_ref, f32[2048,128]{1,0:T(8,128)} %get-tuple-element.18.high_ref, ...), custom_call_target="tpu_custom_call" | custom-call | tf_op jit(solution)/shard_map/first/pallas_call | solution.py:234
  77.9 26.1 %all_to_all.11 = bf16[128,8,128]{2,1,0:T(8,128)(2,1)S(1)} all-to-all(bf16[128,8,128]{2,1,0:T(8,128)(2,1)} %bitcast.22), channel_id=1, replica_groups=mesh['tile'=128,'layer'=4] {'tile'}, dimensions={0} | all-to-all | bytes 524288 | tf_op jit(solution)/shard_map/all_to_all | solution.py:286
  104.0 1.9 %collective-permute-start.4 = (bf16[128,8,128]{2,1,0:T(8,128)(2,1)S(1)}, bf16[128,8,128]{2,1,0:T(8,128)(2,1)S(1)}, u32[]{:S(2)}, u32[]{:S(2)}) collective-permute-start(bf16[128,8,128]{2,1,0:T(8,128)(2,1)S(1)} %all_to_all.11), channel_id=1, source_target_pairs={{0,2},{1,3},{2,0},{3,1},{4,6},{5,7},{6,4},{7,5},{8,10},{9,11},{10,... | collective-permute-start | bytes 786440 | tf_op jit(solution)/shard_map/ppermute | solution.py:282
  105.9 2.0 %edges.3 = (f32[64,768]{1,0:T(8,128)}, f32[64,512]{1,0:T(8,128)}) custom-call(s32[24,2]{1,0:T(8,128)} %copy.18.pattern_ref, s32[1]{0:T(128)} %bitcast.4.left_ref, bf16[64,3072]{1,0:T(8,128)(2,1)} %get-tuple-element.23.x_ref, bf16[24,128,128]{2,1,0:T(8,128)(2,1)} %down_ref.7, bf16[4,6,128,128]{3,2,1,0:T(8,128)(2,1)} %bitcast.12), custom_call_target="tpu_custom_call" | custom-call | tf_op jit(solution)/shard_map/edges/pallas_call | solution.py:107
  108.0 2.4 %collective-permute-start.5 = (f32[64,768]{1,0:T(8,128)}, f32[64,768]{1,0:T(8,128)S(1)}, u32[]{:S(2)}, u32[]{:S(2)}) collective-permute-start(f32[64,768]{1,0:T(8,128)} %get-tuple-element.24), channel_id=1, source_target_pairs={{0,4},{4,8},{8,12},{12,16},{16,20},{20,24},{24,28},{28,32},{32,36}... | collective-permute-start | bytes 589832 | tf_op jit(solution)/shard_map/ppermute | solution.py:278
  110.3 2.6 %collective-permute-start.7 = (f32[64,512]{1,0:T(8,128)}, f32[64,512]{1,0:T(8,128)S(1)}, u32[]{:S(2)}, u32[]{:S(2)}) collective-permute-start(f32[64,512]{1,0:T(8,128)} %get-tuple-element.25), channel_id=1, source_target_pairs={{0,1},{1,0},{2,3},{3,2},{4,5},{5,4},{6,7},{7,6},{8,9},{9,8},{10,11... | collective-permute-start | bytes 393224 | tf_op jit(solution)/shard_map/ppermute | solution.py:282
  113.0 0.9 slice.7
  113.9 1.9 %collective-permute-start.6 = (bf16[64,768]{1,0:T(8,128)(2,1)S(1)}, bf16[64,768]{1,0:T(8,128)(2,1)S(1)}, u32[]{:S(2)}, u32[]{:S(2)}) collective-permute-start(bf16[64,768]{1,0:T(8,128)(2,1)S(1)} %slice.7), channel_id=1, source_target_pairs={{4,0},{8,4},{12,8},{16,12},{20,16},{24,20},{28,24},{32,28},{36,32}... | collective-permute-start | bytes 294920 | tf_op jit(solution)/shard_map/ppermute | solution.py:278
  115.8 4.3 %collective-permute-done.6.below_ref = bf16[64,768]{1,0:T(8,128)(2,1)S(1)} collective-permute-done((bf16[64,768]{1,0:T(8,128)(2,1)S(1)}, bf16[64,768]{1,0:T(8,128)(2,1)S(1)}, u32[]{:S(2)}, u32[]{:S(2)}) %collective-permute-start.6) | collective-permute-done | bytes 98336 | tf_op jit(solution)/shard_map/ppermute | solution.py:278
  120.1 6.9 %collective-permute-done.7.side_ref = f32[64,512]{1,0:T(8,128)S(1)} collective-permute-done((f32[64,512]{1,0:T(8,128)}, f32[64,512]{1,0:T(8,128)S(1)}, u32[]{:S(2)}, u32[]{:S(2)}) %collective-permute-start.7) | collective-permute-done | bytes 131104 | tf_op jit(solution)/shard_map/ppermute | solution.py:282
  128.3 3.7 %intra.3.intra_ref = f32[64,3072]{1,0:T(8,128)} custom-call(s32[24,2]{1,0:T(8,128)} %copy.18.pattern_ref, s32[1]{0:T(128)} %bitcast.4.left_ref, bf16[64,3072]{1,0:T(8,128)(2,1)} %get-tuple-element.23.x_ref, bf16[24,128,128]{2,1,0:T(8,128)(2,1)} %onsite_ref.3, bf16[24,128,128]{2,1,0:T(8,128)(2,1)} %down_ref.7, bf16[24,128,128]{2,1,0:T(8,128)(2,1)} %right_ref.3, ...), custom_call_target="tpu_custom_call" | custom-call | tf_op jit(solution)/shard_map/intra/pallas_call | solution.py:176
  132.7 4.4 %second.1 = (f32[64,3072]{1,0:T(8,128)}, f32[12,3072]{1,0:T(8,128)}) custom-call(bf16[64,3072]{1,0:T(8,128)(2,1)} %bitcast.18, f32[64,3072]{1,0:T(8,128)} %get-tuple-element.21.one_ref, bf16[1024,128]{1,0:T(8,128)(2,1)} %bitcast.20, bf16[2048,256]{1,0:T(8,128)(2,1)} %get-tuple-element.17.hot_ref, f32[2048,128]{1,0:T(8,128)} %get-tuple-element.18.high_ref, ...), custom_call_target="tpu_custom_call" | custom-call | tf_op jit(solution)/shard_map/second/pallas_call | solution.py:263
  137.1 1.6 %reshape.54 = f32[3,4,3072]{2,1,0:T(4,128)} reshape(f32[12,3072]{1,0:T(8,128)} %get-tuple-element.28) | data formatting | bytes 294912 | tf_op jit(solution)/shard_map/reshape | solution.py:321
  (33 shorter events, 9.0 us)
Async XLA Ops:
  0.6 1.4 %copy-start.8 = (s32[128,8]{0,1:T(8,128)S(1)}, s32[128,8]{0,1:T(8,128)}, u32[]{:S(2)}) copy-start(s32[128,8]{0,1:T(8,128)} %param.16) | copy-start | bytes 12292
  2.0 0.7 copy-start.9
  3.5 0.7 copy-start.11
  38.6 32.6 %collective-permute-start = (bf16[128,8,128]{2,1,0:T(8,128)(2,1)S(1)}, bf16[128,8,128]{2,1,0:T(8,128)(2,1)S(1)}, u32[]{:S(2)}, u32[]{:S(2)}) collective-permute-start(bf16[128,8,128]{2,1,0:T(8,128)(2,1)S(1)} %all_to_all.10), channel_id=1, source_target_pairs={{0,2},{1,3},{2,0},{3,1},{4,6},{5,7},{6,4},{7,5},{8,10},{9,11},{10,... | collective-permute-start | bytes 786440 | tf_op jit(solution)/shard_map/ppermute | solution.py:282
  48.3 0.7 copy-start.10
  51.7 14.5 %collective-permute-start.1 = (f32[64,768]{1,0:T(8,128)}, f32[64,768]{1,0:T(8,128)S(1)}, u32[]{:S(2)}, u32[]{:S(2)}) collective-permute-start(f32[64,768]{1,0:T(8,128)} %get-tuple-element.19), channel_id=1, source_target_pairs={{0,4},{4,8},{8,12},{12,16},{16,20},{20,24},{24,28},{28,32},{32,36}... | collective-permute-start | bytes 589832 | tf_op jit(solution)/shard_map/ppermute | solution.py:278
  54.4 11.8 %collective-permute-start.3 = (f32[64,512]{1,0:T(8,128)}, f32[64,512]{1,0:T(8,128)S(1)}, u32[]{:S(2)}, u32[]{:S(2)}) collective-permute-start(f32[64,512]{1,0:T(8,128)} %get-tuple-element.20), channel_id=1, source_target_pairs={{0,1},{1,0},{2,3},{3,2},{4,5},{5,4},{6,7},{7,6},{8,9},{9,8},{10,11... | collective-permute-start | bytes 393224 | tf_op jit(solution)/shard_map/ppermute | solution.py:282
  59.3 6.2 %collective-permute-start.2 = (bf16[64,768]{1,0:T(8,128)(2,1)S(1)}, bf16[64,768]{1,0:T(8,128)(2,1)S(1)}, u32[]{:S(2)}, u32[]{:S(2)}) collective-permute-start(bf16[64,768]{1,0:T(8,128)(2,1)S(1)} %slice.8), channel_id=1, source_target_pairs={{4,0},{8,4},{12,8},{16,12},{20,16},{24,20},{28,24},{32,28},{36,32}... | collective-permute-start | bytes 294920 | tf_op jit(solution)/shard_map/ppermute | solution.py:278
  65.5 0.7 copy-start.7
  66.2 0.7 copy-start.5
  66.9 0.7 copy-start.3
  71.2 0.7 copy-start.1
  104.0 28.0 %collective-permute-start.4 = (bf16[128,8,128]{2,1,0:T(8,128)(2,1)S(1)}, bf16[128,8,128]{2,1,0:T(8,128)(2,1)S(1)}, u32[]{:S(2)}, u32[]{:S(2)}) collective-permute-start(bf16[128,8,128]{2,1,0:T(8,128)(2,1)S(1)} %all_to_all.11), channel_id=1, source_target_pairs={{0,2},{1,3},{2,0},{3,1},{4,6},{5,7},{6,4},{7,5},{8,10},{9,11},{10,... | collective-permute-start | bytes 786440 | tf_op jit(solution)/shard_map/ppermute | solution.py:282
  108.0 19.0 %collective-permute-start.5 = (f32[64,768]{1,0:T(8,128)}, f32[64,768]{1,0:T(8,128)S(1)}, u32[]{:S(2)}, u32[]{:S(2)}) collective-permute-start(f32[64,768]{1,0:T(8,128)} %get-tuple-element.24), channel_id=1, source_target_pairs={{0,4},{4,8},{8,12},{12,16},{16,20},{20,24},{24,28},{28,32},{32,36}... | collective-permute-start | bytes 589832 | tf_op jit(solution)/shard_map/ppermute | solution.py:278
  110.3 16.6 %collective-permute-start.7 = (f32[64,512]{1,0:T(8,128)}, f32[64,512]{1,0:T(8,128)S(1)}, u32[]{:S(2)}, u32[]{:S(2)}) collective-permute-start(f32[64,512]{1,0:T(8,128)} %get-tuple-element.25), channel_id=1, source_target_pairs={{0,1},{1,0},{2,3},{3,2},{4,5},{5,4},{6,7},{7,6},{8,9},{9,8},{10,11... | collective-permute-start | bytes 393224 | tf_op jit(solution)/shard_map/ppermute | solution.py:282
  113.9 6.2 %collective-permute-start.6 = (bf16[64,768]{1,0:T(8,128)(2,1)S(1)}, bf16[64,768]{1,0:T(8,128)(2,1)S(1)}, u32[]{:S(2)}, u32[]{:S(2)}) collective-permute-start(bf16[64,768]{1,0:T(8,128)(2,1)S(1)} %slice.7), channel_id=1, source_target_pairs={{4,0},{8,4},{12,8},{16,12},{20,16},{24,20},{28,24},{32,28},{36,32}... | collective-permute-start | bytes 294920 | tf_op jit(solution)/shard_map/ppermute | solution.py:278
  120.1 6.9 %copy-start.6 = (bf16[64,768]{1,0:T(8,128)(2,1)}, bf16[64,768]{1,0:T(8,128)(2,1)S(1)}, u32[]{:S(2)}) copy-start(bf16[64,768]{1,0:T(8,128)(2,1)S(1)} %collective-permute-done.6.below_ref) | copy-start | bytes 294916
  127.0 0.7 copy-start.4
  127.6 0.7 copy-start.2
  132.0 0.7 copy-start

commit v2 on v0

v2 whole, which is shorter than its diff:
```python
import jax
import jax.numpy as jnp
from jax import lax
from jax.experimental import pallas as pl
from jax.experimental.pallas import tpu as pltpu
from jax.sharding import PartitionSpec as P

TILE = 128
TR = 4
TC = 6
ROWS = 64
SITES_DEV = TR * TC * TILE
PEERS = 128
CAP = 8
SLOTS = PEERS * CAP
SPAN = 256
HI = SITES_DEV // SPAN
F32 = jnp.float32
BF16 = jnp.bfloat16
NT = (((1,), (1,)), ((), ()))
NN = (((1,), (0,)), ((), ()))
VMEM_LIMIT = 56 * 1024 * 1024


def dot(a, b, dims=NN):
    return lax.dot_general(a, b, dims, preferred_element_type=F32)


COST = pl.CostEstimate(flops=1000000, bytes_accessed=100000, transcendentals=0)


def params():
    return pltpu.CompilerParams(vmem_limit_bytes=VMEM_LIMIT)


def per_slot(table):
    spread = jnp.broadcast_to(table[None], (PEERS, CAP, PEERS)).reshape(SLOTS, PEERS)
    own = lax.broadcasted_iota(jnp.int32, (SLOTS, PEERS), 0) // CAP == lax.broadcasted_iota(
        jnp.int32, (SLOTS, PEERS), 1
    )
    return dot(jnp.where(own, spread, 0.0).astype(BF16), jnp.ones((PEERS, TILE), BF16))


def build_tables(rows, target, weight, hot_ref, high_ref, weight_ref):
    lane = lax.broadcasted_iota(jnp.int32, (SLOTS, SPAN), 1).astype(F32)
    spread_weight = per_slot(weight)
    weight_ref[...] = spread_weight
    wide_weight = jnp.concatenate([spread_weight, spread_weight], axis=1)
    for end, table in ((0, rows), (1, target)):
        coarse = jnp.floor(table * (1.0 / SPAN))
        low = per_slot(table - coarse * SPAN)
        high_ref[end * SLOTS : (end + 1) * SLOTS, :] = per_slot(coarse)
        same = lane == jnp.concatenate([low, low], axis=1)
        hot_ref[2 * end * SLOTS : (2 * end + 1) * SLOTS, :] = jnp.where(same, 1.0, 0.0).astype(BF16)
        if end == 1:
            hot_ref[SLOTS : 2 * SLOTS, :] = jnp.where(same, wide_weight, 0.0).astype(BF16)


def gather_ends(terms, hot_ref, high_ref, start, chunk):
    lane = lax.broadcasted_iota(jnp.int32, (chunk, TILE), 1)
    half = (lane >= ROWS).astype(F32)
    ends = []
    for end in range(2):
        hot = hot_ref[2 * end * SLOTS + start : 2 * end * SLOTS + start + chunk, :]
        high = high_ref[end * SLOTS + start : end * SLOTS + start + chunk, :] - half
        total = jnp.zeros((chunk, TILE), F32)
        for q in range(HI // 2):
            found = sum(dot(hot, jnp.concatenate([t[2 * q], t[2 * q + 1]], axis=0), NT) for t in terms)
            total = jnp.where(high == 2.0 * q, found, total)
        ends.append(total + pltpu.roll(total, ROWS, 1))
    return jnp.where(lane < ROWS, ends[0], ends[1])


def as_payload(ends, weight):
    field = ends.astype(BF16)
    lane = lax.broadcasted_iota(jnp.int32, ends.shape, 1)
    return jnp.where(lane < ROWS, field.astype(F32), field.astype(F32) * weight).astype(BF16)


def split(value):
    high = value.astype(BF16)
    return high, (value - high.astype(F32)).astype(BF16)


CHUNK = 256


def prepare_kernel(x_ref, table_ref, hot_ref, high_ref, spread_ref, out_ref):
    build_tables(table_ref[0], table_ref[1], table_ref[2], hot_ref, high_ref, spread_ref)
    parts = [x_ref[:, h * SPAN : (h + 1) * SPAN] for h in range(HI)]
    for start in range(0, SLOTS, CHUNK):
        ends = gather_ends([parts], hot_ref, high_ref, start, CHUNK)
        out_ref[start : start + CHUNK, :] = as_payload(ends, spread_ref[start : start + CHUNK, :])


TABLE_SHAPES = (
    jax.ShapeDtypeStruct((3 * SLOTS, SPAN), BF16),
    jax.ShapeDtypeStruct((2 * SLOTS, TILE), F32),
    jax.ShapeDtypeStruct((SLOTS, TILE), F32),
)


def prepare(x, table):
    return pl.pallas_call(
        prepare_kernel,
        out_shape=TABLE_SHAPES + (jax.ShapeDtypeStruct((SLOTS, 2 * ROWS), BF16),),
        compiler_params=params(),
        cost_estimate=COST,
        name="prepare",
    )(x, table)


def tables_kernel(table_ref, hot_ref, high_ref, spread_ref):
    build_tables(table_ref[0], table_ref[1], table_ref[2], hot_ref, high_ref, spread_ref)


def tables_of(table):
    return pl.pallas_call(
        tables_kernel, out_shape=TABLE_SHAPES, compiler_params=params(),
        cost_estimate=COST, name="other_tables"
    )(table)


def write_edges(pattern_ref, left_ref, x_ref, down_ref, right_ref, down_base, top_ref, below_ref, side_ref):
    top_ref[...] = x_ref[:, : TC * TILE]
    for k in range(TC):
        tile = (TR - 1) * TC + k
        keep = pattern_ref[0, tile].astype(F32)
        below_ref[:, k * TILE : (k + 1) * TILE] = keep * dot(
            x_ref[:, tile * TILE : (tile + 1) * TILE], down_ref[down_base + k]
        )
    is_left = left_ref[0] == 1
    for r in range(TR):
        last = r * TC + TC - 1
        keep = pattern_ref[1, last].astype(F32)
        product = keep * dot(x_ref[:, last * TILE : (last + 1) * TILE], right_ref[r, 0])
        first_tile = x_ref[:, r * TC * TILE : (r * TC + 1) * TILE].astype(F32)
        side_ref[:, r * TILE : (r + 1) * TILE] = jnp.where(is_left, product, first_tile)


def edges_kernel(
    pattern_ref, left_ref, x_ref, down_ref, right_ref, rows_ref, target_ref, weight_ref, count_ref,
    top_ref, below_ref, side_ref, table_ref,
):
    live = lax.broadcasted_iota(jnp.int32, (CAP, PEERS), 0) < count_ref[...]
    table_ref[0] = rows_ref[...].astype(F32)
    table_ref[1] = target_ref[...].astype(F32)
    table_ref[2] = jnp.where(live, weight_ref[...].astype(F32), 0.0)
    write_edges(pattern_ref, left_ref, x_ref, down_ref, right_ref, 0, top_ref, below_ref, side_ref)


EDGE_SHAPES = (
    jax.ShapeDtypeStruct((ROWS, TC * TILE), BF16),
    jax.ShapeDtypeStruct((ROWS, TC * TILE), F32),
    jax.ShapeDtypeStruct((ROWS, TR * TILE), F32),
)
SMEM = pl.BlockSpec(memory_space=pltpu.SMEM)
VMEM = pl.BlockSpec(memory_space=pltpu.VMEM)
DOWN_EDGE = pl.BlockSpec((TC, TILE, TILE), lambda i: (TR - 1, 0, 0))
RIGHT_EDGE = pl.BlockSpec((TR, 1, TILE, TILE), lambda i: (0, TC - 1, 0, 0))


def whole(shape):
    return pl.BlockSpec(shape, lambda i: (0,) * len(shape))


def edges(pattern, left_flag, x, down_hop, right_hop, link_rows, link_target, link_weight, link_count):
    links = (link_rows.T, link_target.T, link_weight.T, link_count.reshape(1, PEERS))
    shapes = EDGE_SHAPES + (jax.ShapeDtypeStruct((3, CAP, PEERS), F32),)
    return pl.pallas_call(
        edges_kernel,
        grid=(1,),
        in_specs=[SMEM, SMEM, whole((ROWS, SITES_DEV)), DOWN_EDGE, RIGHT_EDGE] + [whole(a.shape) for a in links],
        out_specs=tuple(whole(s.shape) for s in shapes),
        out_shape=shapes,
        compiler_params=params(),
        cost_estimate=COST,
        name="edges",
    )(pattern, left_flag, x, down_hop, right_hop.reshape(TR, TC, TILE, TILE), *links)


def kept(pattern_ref, which, tile, value):
    return jnp.where(pattern_ref[which, tile] == 1, value, jnp.zeros_like(value))


def local_tile(pattern_ref, x_ref, onsite_ref, down_ref, right_ref, tile):
    def block(other):
        return x_ref[:, other * TILE : (other + 1) * TILE]

    r, k = divmod(tile, TC)
    fields = [block(tile)]
    tiles = [onsite_ref[tile]]
    if r > 0:
        fields.append(kept(pattern_ref, 0, tile - TC, block(tile - TC)))
        tiles.append(down_ref[tile - TC])
    if k > 0:
        fields.append(kept(pattern_ref, 1, tile - 1, block(tile - 1)))
        tiles.append(right_ref[tile - 1])
    total = dot(jnp.concatenate(fields, axis=1), jnp.concatenate(tiles, axis=0))
    fields = []
    tiles = []
    if r < TR - 1:
        fields.append(kept(pattern_ref, 0, tile, block(tile + TC)))
        tiles.append(down_ref[tile])
    if k < TC - 1:
        fields.append(kept(pattern_ref, 1, tile, block(tile + 1)))
        tiles.append(right_ref[tile])
    if fields:
        total = total + dot(jnp.concatenate(fields, axis=1), jnp.concatenate(tiles, axis=1), NT)
    return total


def halo_tile(pattern_ref, is_left, down_edge, right_edge, above_ref, below_ref, side_ref, tile):
    r, k = divmod(tile, TC)
    total = None

    def plus(value):
        return value if total is None else total + value

    if r == 0:
        total = plus(above_ref[:, k * TILE : (k + 1) * TILE])
    if r == TR - 1:
        lower = below_ref[:, k * TILE : (k + 1) * TILE]
        total = plus(dot(kept(pattern_ref, 0, tile, lower), down_edge(k), NT))
    if k == 0:
        total = plus(jnp.where(is_left, 0.0, side_ref[:, r * TILE : (r + 1) * TILE]))
    if k == TC - 1:
        righter = jnp.where(is_left, side_ref[:, r * TILE : (r + 1) * TILE], 0.0).astype(BF16)
        total = plus(dot(kept(pattern_ref, 1, tile, righter), right_edge(r), NT))
    return total


def signed(value):
    return jnp.where(lax.broadcasted_iota(jnp.int32, value.shape, 0) < ROWS // 2, value, -value)


def swapped(value):
    return jnp.concatenate([value[ROWS // 2 :], value[: ROWS // 2]], axis=0)


def vector_mean(value):
    comps = value.reshape(4, 16, value.shape[-1])
    return jnp.sum(comps, axis=1) * (1.0 / 16.0)


def near_kernel(
    pattern_ref, left_ref, v0_ref, onsite_ref, down_ref, right_ref, above_ref, below_ref, side_ref,
    pairing_ref, hot_ref, high_ref, near_ref, out_ref,
):
    is_left = left_ref[0] == 1
    for tile in range(TR * TC):
        cols = slice(tile * TILE, (tile + 1) * TILE)
        hop = local_tile(pattern_ref, v0_ref, onsite_ref, down_ref, right_ref, tile)
        halo = halo_tile(
            pattern_ref, is_left, lambda k: down_ref[(TR - 1) * TC + k], lambda r: right_ref[r * TC + TC - 1],
            above_ref, below_ref, side_ref, tile,
        )
        hop = hop if halo is None else hop + halo
        near_ref[:, cols] = signed(hop) + pairing_ref[:, cols] * swapped(v0_ref[:, cols].astype(F32))
    pairs = [split(near_ref[:, h * SPAN : (h + 1) * SPAN]) for h in range(HI)]
    terms = [[p[0] for p in pairs], [p[1] for p in pairs]]
    for start in range(0, SLOTS, CHUNK):
        out_ref[start : start + CHUNK, :] = gather_ends(terms, hot_ref, high_ref, start, CHUNK)


def near(pattern, left_flag, v0, onsite, down_hop, right_hop, halo, pairing, hot, high):
    return pl.pallas_call(
        near_kernel,
        in_specs=[SMEM, SMEM] + [VMEM] * 10,
        out_shape=(
            jax.ShapeDtypeStruct((ROWS, SITES_DEV), F32),
            jax.ShapeDtypeStruct((SLOTS, 2 * ROWS), F32),
        ),
        compiler_params=params(),
        cost_estimate=COST,
        name="near",
    )(pattern, left_flag, v0, onsite, down_hop, right_hop, *halo, pairing, hot, high)


SCATTER_SCRATCH = [pltpu.VMEM((HI * ROWS, 2 * SLOTS), BF16), pltpu.VMEM((HI * ROWS, SPAN), F32)]


def scatter_into(landed, hot_ref, high_ref, mask_ref, total_ref):
    turned = landed.astype(F32).T.astype(BF16)
    high_send = high_ref[0:SLOTS, :].T.astype(BF16)[:ROWS]
    high_recv = high_ref[SLOTS : 2 * SLOTS, :].T.astype(BF16)[:ROWS]
    zero = jnp.zeros((ROWS, SLOTS), BF16)
    for h in range(HI):
        rows = slice(h * ROWS, (h + 1) * ROWS)
        mask_ref[rows, 0:SLOTS] = jnp.where(high_send == BF16(h), turned[ROWS:], zero)
        mask_ref[rows, SLOTS : 2 * SLOTS] = jnp.where(high_recv == BF16(h), turned[:ROWS], zero)
    group = 4
    for start in range(0, HI, group):
        total_ref[start * ROWS : (start + group) * ROWS, :] = dot(
            mask_ref[start * ROWS : (start + group) * ROWS, :], hot_ref[0 : 2 * SLOTS, :]
        )


def relay_kernel(landed_ref, hot_ref, high_ref, weight_ref, near_ref, out_ref, mask_ref, total_ref):
    scatter_into(landed_ref[...], hot_ref, high_ref, mask_ref, total_ref)
    pairs = [split(signed(total_ref[h * ROWS : (h + 1) * ROWS, :])) for h in range(HI)]
    terms = [[p[0] for p in pairs], [p[1] for p in pairs]]
    for start in range(0, SLOTS, CHUNK):
        rows = slice(start, start + CHUNK)
        ends = gather_ends(terms, hot_ref, high_ref, start, CHUNK) + near_ref[rows, :]
        out_ref[rows, :] = as_payload(ends, weight_ref[rows, :])


def relay(landed, hot, high, weight, near_ends):
    return pl.pallas_call(
        relay_kernel,
        out_shape=jax.ShapeDtypeStruct((SLOTS, 2 * ROWS), BF16),
        scratch_shapes=SCATTER_SCRATCH,
        compiler_params=params(),
        cost_estimate=COST,
        name="relay",
    )(landed, hot, high, weight, near_ends)


def first_kernel(
    pattern_ref, left_ref, v0_ref, landed_ref, hot_ref, high_ref, near_ref, down_ref, right_ref,
    one_ref, x_ref, mom_ref, top_ref, below_ref, side_ref, mask_ref, total_ref,
):
    scatter_into(landed_ref[...], hot_ref, high_ref, mask_ref, total_ref)
    for h in range(HI):
        cols = slice(h * SPAN, (h + 1) * SPAN)
        v0 = v0_ref[:, cols].astype(F32)
        one = near_ref[:, cols] + signed(total_ref[h * ROWS : (h + 1) * ROWS, :])
        one_ref[:, cols] = one
        x_ref[:, cols] = one.astype(BF16)
        mom_ref[0, :, cols] = vector_mean(v0 * v0)
        mom_ref[1, :, cols] = vector_mean(v0 * one)
    write_edges(pattern_ref, left_ref, x_ref, down_ref, right_ref, 0, top_ref, below_ref, side_ref)


def first(pattern, left_flag, v0, landed, hot, high, near_part, down_hop, right_hop):
    shapes = (
        jax.ShapeDtypeStruct((ROWS, SITES_DEV), F32),
        jax.ShapeDtypeStruct((ROWS, SITES_DEV), BF16),
        jax.ShapeDtypeStruct((2, 4, SITES_DEV), F32),
    ) + EDGE_SHAPES
    return pl.pallas_call(
        first_kernel,
        grid=(1,),
        in_specs=[SMEM, SMEM]
        + [whole(a.shape) for a in (v0, landed, hot, high, near_part)]
        + [DOWN_EDGE, RIGHT_EDGE],
        out_specs=tuple(whole(s.shape) for s in shapes),
        out_shape=shapes,
        scratch_shapes=SCATTER_SCRATCH,
        compiler_params=params(),
        cost_estimate=COST,
        name="first",
    )(pattern, left_flag, v0, landed, hot, high, near_part, down_hop, right_hop.reshape(TR, TC, TILE, TILE))


def local_kernel(pattern_ref, x_ref, onsite_ref, down_ref, right_ref, out_ref):
    for tile in range(TR * TC):
        out_ref[:, tile * TILE : (tile + 1) * TILE] = local_tile(
            pattern_ref, x_ref, onsite_ref, down_ref, right_ref, tile
        )


def local(pattern, x, onsite, down_hop, right_hop):
    return pl.pallas_call(
        local_kernel,
        in_specs=[SMEM] + [VMEM] * 4,
        out_shape=jax.ShapeDtypeStruct((ROWS, SITES_DEV), F32),
        compiler_params=params(),
        cost_estimate=COST,
        name="local",
    )(pattern, x, onsite, down_hop, right_hop)


def second_kernel(
    pattern_ref, left_ref, v0_ref, one_ref, landed_ref, hot_ref, high_ref, local_ref, pairing_ref, mom_in_ref,
    above_ref, below_ref, side_ref, down_ref, right_ref, two_ref, mom_ref, mask_ref, total_ref,
):
    scatter_into(landed_ref[...], hot_ref, high_ref, mask_ref, total_ref)
    is_left = left_ref[0] == 1
    mom_ref[0:2] = mom_in_ref[...]
    for tile in range(TR * TC):
        cols = slice(tile * TILE, (tile + 1) * TILE)
        h, part = divmod(tile, SPAN // TILE)
        hop = local_ref[:, cols] + total_ref[h * ROWS : (h + 1) * ROWS, part * TILE : (part + 1) * TILE]
        halo = halo_tile(
            pattern_ref, is_left, lambda k: down_ref[k], lambda r: right_ref[r, 0],
            above_ref, below_ref, side_ref, tile,
        )
        hop = hop if halo is None else hop + halo
        v0 = v0_ref[:, cols].astype(F32)
        two = 2.0 * (signed(hop) + pairing_ref[:, cols] * swapped(one_ref[:, cols])) - v0
        two_ref[:, cols] = two
        mom_ref[2, :, cols] = vector_mean(v0 * two)


def second(pattern, left_flag, v0, one, landed, hot, high, local_part, pairing, mom, halo, down_hop, right_hop):
    shapes = (
        jax.ShapeDtypeStruct((ROWS, SITES_DEV), F32),
        jax.ShapeDtypeStruct((3, 4, SITES_DEV), F32),
    )
    arrays = (v0, one, landed, hot, high, local_part, pairing, mom) + tuple(halo)
    return pl.pallas_call(
        second_kernel,
        grid=(1,),
        in_specs=[SMEM, SMEM] + [whole(a.shape) for a in arrays] + [DOWN_EDGE, RIGHT_EDGE],
        out_specs=tuple(whole(s.shape) for s in shapes),
        out_shape=shapes,
        scratch_shapes=SCATTER_SCRATCH,
        compiler_params=params(),
        cost_estimate=COST,
        name="second",
    )(pattern, left_flag, *arrays, down_hop, right_hop.reshape(TR, TC, TILE, TILE))


def passed_along(value, axis, by):
    length = lax.axis_size(axis)
    pairs = [(i, i + by) for i in range(length) if 0 <= i + by < length]
    return lax.ppermute(value, axis, pairs)


def partner_2(value, axis, bit):
    return lax.ppermute(value, axis, [(i, i ^ 1 << bit) for i in range(lax.axis_size(axis))])


def spread_out(payload):
    return lax.all_to_all(
        payload.reshape(PEERS, CAP, 2 * ROWS), "tile", split_axis=0, concat_axis=0, tiled=True
    ).reshape(SLOTS, 2 * ROWS)


def other_layer(value):
    return partner_2(value, "layer", 1)


def shards(
    rand_vectors,
    onsite,
    down_hop,
    right_hop,
    pattern,
    pairing,
    link_rows,
    link_target,
    link_weight,
    link_count,
):
    v0 = rand_vectors.reshape(ROWS, SITES_DEV)
    pairing = pairing.reshape(1, SITES_DEV)
    pattern = pattern.T
    left_flag = (1 - lax.axis_index("layer") % 2).astype(jnp.int32).reshape(1)

    def halo_of(top, below_part, side_part):
        return (
            passed_along(below_part, "tile", 1),
            passed_along(top, "tile", -1),
            partner_2(side_part, "layer", 0),
        )

    *edge_parts, table = edges(
        pattern, left_flag, v0, down_hop, right_hop, link_rows, link_target, link_weight, link_count
    )
    halo = halo_of(*edge_parts)
    tables_other = tables_of(other_layer(table))
    hot, high, weight, payload = prepare(v0, table)
    landed_other = spread_out(payload)
    hot, tables_other = lax.optimization_barrier((hot, tables_other))
    near_part, near_ends = near(
        pattern, left_flag, v0, onsite, down_hop, right_hop, halo, pairing, hot, high
    )
    near_ends = other_layer(near_ends)
    landed_other, near_part = lax.optimization_barrier((landed_other, near_part))
    landed = other_layer(landed_other)
    payload = relay(landed_other, *tables_other, near_ends)
    landed_two = spread_out(payload)
    one, x, mom, *edge_parts = first(
        pattern, left_flag, v0, landed, hot, high, near_part, down_hop, right_hop
    )
    halo = halo_of(*edge_parts)
    local_part = local(pattern, x, onsite, down_hop, right_hop)
    landed_two, local_part, halo = lax.optimization_barrier((landed_two, local_part, halo))
    two, mom = second(
        pattern, left_flag, v0, one, landed_two, hot, high, local_part, pairing, mom, halo, down_hop, right_hop
    )
    shape = rand_vectors.shape
    return one.reshape(shape), two.reshape(shape), mom


def solution(mesh):
    both = ("tile", "layer")
    in_specs = (
        P(None, None, both),
        P(both, None, None),
        P(both, None, None),
        P(both, None, None),
        P(both, None),
        P(both),
        P(both, None),
        P(both, None),
        P(both, None),
        P(both),
    )
    out_specs = (P(None, None, both), P(None, None, both), P(None, None, both))
    return jax.shard_map(shards, mesh=mesh, in_specs=in_specs, out_specs=out_specs, check_vma=False)
```

time: 252 us -> 141 us (0.56)
  the two profiles are of different devices: /device:TPU:7 before, /device:TPU:31 now
where the time goes in v2:
time: 141 us
  starting transfers between devices  54 us (38%)
  Pallas kernels  37 us (26%)
  blocking collectives  28.1 us (20%)
  waiting for transfers between devices  17.2 us (12%)
  local copies, waits for them, and re-layouts  3.65 us (3%)
    ppermute x5, starting transfers between devices, partner_2(): lax.ppermute(value, axis, [(i, i ^ 1 << bit) for i in range(lax.axis_size...  29.7 us
    all_to_all x1, blocking collectives, spread_out(): lax.all_to_all(payload.reshape(PEERS, CAP, 2 * ROWS), 'tile', split_axis=...  28.1 us
    ppermute x4, starting transfers between devices, passed_along(): return lax.ppermute(value, axis, pairs)  13.5 us
    ppermute x5, waiting for transfers between devices, partner_2(): lax.ppermute(value, axis, [(i, i ^ 1 << bit) for i in range(lax.axis_size...  13.2 us
    all_to_all x1, starting transfers between devices, spread_out(): lax.all_to_all(payload.reshape(PEERS, CAP, 2 * ROWS), 'tile', split_axis=...  10.8 us
    pallas_call x1, Pallas kernels, near(): pl.pallas_call(near_kernel, in_specs=[SMEM, SMEM] + [VMEM] * 10, out_shap...  8 us
    pallas_call x1, Pallas kernels, relay(): pl.pallas_call(relay_kernel, out_shape=jax.ShapeDtypeStruct((SLOTS, 2 * R...  7.3 us
    pallas_call x1, Pallas kernels, second(): pl.pallas_call(second_kernel, grid=(1,), in_specs=[SMEM, SMEM] + [whole(a...  4.81 us
  transfers between devices with their start and end apart: 10, of which 3 were waited for; matrix products, arithmetic and copies ran while one was open for 0% of the time, Pallas kernels for 11%

profile of v2, /device:TPU:31, one launch (start us, length us, event | category | flops | bytes accessed | tf_op | source)
XLA Modules:
  0.0 140.8 jit_solution(16126466826964759545)
XLA Ops:
  0.6 2.0 %edges.1 = (bf16[64,768]{1,0:T(8,128)(2,1)}, f32[64,768]{1,0:T(8,128)}, f32[64,512]{1,0:T(8,128)}, f32[3,8,128]{2,1,0:T(8,128)}) custom-call(s32[2,24]{1,0:T(2,128)} %bitcast.31, s32[1]{0:T(128)} %bitcast.1.left_ref, bf16[64,3072]{1,0:T(8,128)(2,1)} %bitcast.18, bf16[24,128,128]{2,1,0:T(8,128)(2,1)} %down_ref.9, bf16[4,6,128,128]{3,2,1,0:T(8,128)(2,1)} %bitcast.15, ...), custom_call_target="tpu_custom_call" | custom-call | flops 1000000 | bytes 100000 | tf_op jit(solution)/shard_map/edges/pallas_call | solution.py:170
  2.7 4.9 %collective-permute-start = (f32[64,768]{1,0:T(8,128)}, f32[64,768]{1,0:T(8,128)S(1)}, u32[]{:S(2)}, u32[]{:S(2)}) collective-permute-start(f32[64,768]{1,0:T(8,128)} %get-tuple-element.36), channel_id=1, source_target_pairs={{0,4},{4,8},{8,12},{12,16},{16,20},{20,24},{24,28},{28,32},{32,36}... | collective-permute-start | bytes 589832 | tf_op jit(solution)/shard_map/ppermute | solution.py:419
  7.6 5.8 %collective-permute-start.2 = (f32[64,512]{1,0:T(8,128)}, f32[64,512]{1,0:T(8,128)S(1)}, u32[]{:S(2)}, u32[]{:S(2)}) collective-permute-start(f32[64,512]{1,0:T(8,128)} %get-tuple-element.38), channel_id=1, source_target_pairs={{0,1},{1,0},{2,3},{3,2},{4,5},{5,4},{6,7},{7,6},{8,9},{9,8},{10,11... | collective-permute-start | bytes 393224 | tf_op jit(solution)/shard_map/ppermute | solution.py:423
  13.4 1.9 %collective-permute-start.1 = (bf16[64,768]{1,0:T(8,128)(2,1)}, bf16[64,768]{1,0:T(8,128)(2,1)S(1)}, u32[]{:S(2)}, u32[]{:S(2)}) collective-permute-start(bf16[64,768]{1,0:T(8,128)(2,1)} %get-tuple-element.37), channel_id=1, source_target_pairs={{4,0},{8,4},{12,8},{16,12},{20,16},{24,20},{28,24},{32,28},{36,32}... | collective-permute-start | bytes 294920 | tf_op jit(solution)/shard_map/ppermute | solution.py:419
  15.3 8.8 %collective-permute-start.3 = (f32[3,8,128]{2,1,0:T(8,128)}, f32[3,8,128]{2,1,0:T(8,128)S(1)}, u32[]{:S(2)}, u32[]{:S(2)}) collective-permute-start(f32[3,8,128]{2,1,0:T(8,128)} %get-tuple-element.34.table_ref), channel_id=1, source_target_pairs={{0,2},{1,3},{2,0},{3,1},{4,6},{5,7},{6,4},{7,5},{8,10},{9,11},{10,... | collective-permute-start | bytes 36872 | tf_op jit(solution)/shard_map/ppermute | solution.py:423
  24.2 3.9 %prepare.1 = (bf16[3072,256]{1,0:T(8,128)(2,1)}, f32[2048,128]{1,0:T(8,128)}, f32[1024,128]{1,0:T(8,128)}, bf16[1024,128]{1,0:T(8,128)(2,1)}) custom-call(bf16[64,3072]{1,0:T(8,128)(2,1)} %bitcast.19, f32[3,8,128]{2,1,0:T(8,128)} %get-tuple-element.34.table_ref), custom_call_target="tpu_custom_call" | custom-call | flops 1000000 | bytes 100000 | tf_op jit(solution)/shard_map/prepare/pallas_call | solution.py:104
  28.7 2.9 %other_tables.1 = (bf16[3072,256]{1,0:T(8,128)(2,1)}, f32[2048,128]{1,0:T(8,128)}, f32[1024,128]{1,0:T(8,128)}) custom-call(f32[3,8,128]{2,1,0:T(8,128)} %copy-done.11), custom_call_target="tpu_custom_call" | custom-call | flops 1000000 | bytes 100000 | tf_op jit(solution)/shard_map/other_tables/pallas_call | solution.py:118
  31.6 0.6 copy-done.9
  32.3 8.0 %near.1 = (f32[64,3072]{1,0:T(8,128)}, f32[1024,128]{1,0:T(8,128)}) custom-call(s32[2,24]{1,0:T(2,128)} %bitcast.32, s32[1]{0:T(128)} %bitcast.1.left_ref, bf16[64,3072]{1,0:T(8,128)(2,1)} %bitcast.20, bf16[24,128,128]{2,1,0:T(8,128)(2,1)} %onsite_ref.3, bf16[24,128,128]{2,1,0:T(8,128)(2,1)} %down_ref.9, bf16[24,128,128]{2,1,0:T(8,128)(2,1)} %right_ref.3, ...), custom_call_target="tpu_custom_call" | custom-call | flops 1000000 | bytes 100000 | tf_op jit(solution)/shard_map/near/pallas_call | solution.py:267
  40.3 4.8 %collective-permute-start.5 = (f32[1024,128]{1,0:T(8,128)}, f32[1024,128]{1,0:T(8,128)S(1)}, u32[]{:S(2)}, u32[]{:S(2)}) collective-permute-start(f32[1024,128]{1,0:T(8,128)} %get-tuple-element.52), channel_id=1, source_target_pairs={{0,2},{1,3},{2,0},{3,1},{4,6},{5,7},{6,4},{7,5},{8,10},{9,11},{10,... | collective-permute-start | bytes 1572872 | tf_op jit(solution)/shard_map/ppermute | solution.py:423
  45.2 28.1 %all_to_all.10 = bf16[128,8,128]{2,1,0:T(8,128)(2,1)} all-to-all(bf16[128,8,128]{2,1,0:T(8,128)(2,1)S(1)} %bitcast.28), channel_id=1, replica_groups=mesh['tile'=128,'layer'=4] {'tile'}, dimensions={0} | all-to-all | bytes 524288 | tf_op jit(solution)/shard_map/all_to_all | solution.py:427
  73.8 0.8 copy-done.2
  74.6 7.3 %relay.1 = bf16[1024,128]{1,0:T(8,128)(2,1)} custom-call(bf16[1024,128]{1,0:T(8,128)(2,1)} %bitcast.24, bf16[3072,256]{1,0:T(8,128)(2,1)} %get-tuple-element.49.hot_ref, f32[2048,128]{1,0:T(8,128)} %get-tuple-element.50.high_ref, f32[1024,128]{1,0:T(8,128)} %get-tuple-element.51.weight_ref, f32[1024,128]{1,0:T(8,128)} %copy-done.2), custom_call_target="tpu_custom_call" | custom-call | flops 1000000 | bytes 100000 | tf_op jit(solution)/shard_map/relay/pallas_call | solution.py:310
  81.9 10.8 %all-to-all-start.1 = ((bf16[128,8,128]{2,1,0:T(8,128)(2,1)}), bf16[128,8,128]{2,1,0:T(8,128)(2,1)S(1)}, u32[]{:S(2)}, u32[]{:S(2)}) async-start(bf16[128,8,128]{2,1,0:T(8,128)(2,1)} %bitcast.23), calls=%async_computation.1 | async-start | bytes 524288 | tf_op jit(solution)/shard_map/all_to_all | solution.py:427
  92.7 4.7 %collective-permute-start.4 = (bf16[1024,128]{1,0:T(8,128)(2,1)S(1)}, bf16[1024,128]{1,0:T(8,128)(2,1)S(1)}, u32[]{:S(2)}, u32[]{:S(2)}) collective-permute-start(bf16[1024,128]{1,0:T(8,128)(2,1)S(1)} %bitcast.25), channel_id=1, source_target_pairs={{0,2},{1,3},{2,0},{3,1},{4,6},{5,7},{6,4},{7,5},{8,10},{9,11},{10,... | collective-permute-start | bytes 786440 | tf_op jit(solution)/shard_map/ppermute | solution.py:423
  97.5 12.7 %collective-permute-done.4.landed_ref = bf16[1024,128]{1,0:T(8,128)(2,1)S(1)} collective-permute-done((bf16[1024,128]{1,0:T(8,128)(2,1)S(1)}, bf16[1024,128]{1,0:T(8,128)(2,1)S(1)}, u32[]{:S(2)}, u32[]{:S(2)}) %collective-permute-start.4) | collective-permute-done | bytes 262176 | tf_op jit(solution)/shard_map/ppermute | solution.py:423
  110.1 0.7 copy-done.3
  110.8 4.5 %first.1 = (f32[64,3072]{1,0:T(8,128)}, bf16[64,3072]{1,0:T(8,128)(2,1)}, f32[2,4,3072]{2,1,0:T(4,128)}, bf16[64,768]{1,0:T(8,128)(2,1)}, f32[64,768]{1,0:T(8,128)}, /*index=5*/f32[64,512]{1,0:T(8,128)}) custom-call(s32[2,24]{1,0:T(2,128)} %bitcast.33, s32[1]{0:T(128)} %bitcast.1.left_ref, bf16[64,3072]{1,0:T(8,128)(2,1)} %bitcast.21, ...), custom_call_target="tpu_custom_call" | custom-call | flops 1000000 | bytes 100000 | tf_op jit(solution)/shard_map/first/pallas_call | solution.py:342
  115.4 4.8 %collective-permute-start.6 = (f32[64,768]{1,0:T(8,128)}, f32[64,768]{1,0:T(8,128)S(1)}, u32[]{:S(2)}, u32[]{:S(2)}) collective-permute-start(f32[64,768]{1,0:T(8,128)} %get-tuple-element.54), channel_id=1, source_target_pairs={{0,4},{4,8},{8,12},{12,16},{16,20},{20,24},{24,28},{28,32},{32,36}... | collective-permute-start | bytes 589832 | tf_op jit(solution)/shard_map/ppermute | solution.py:419
  120.1 5.5 %collective-permute-start.8 = (f32[64,512]{1,0:T(8,128)}, f32[64,512]{1,0:T(8,128)S(1)}, u32[]{:S(2)}, u32[]{:S(2)}) collective-permute-start(f32[64,512]{1,0:T(8,128)} %get-tuple-element.56), channel_id=1, source_target_pairs={{0,1},{1,0},{2,3},{3,2},{4,5},{5,4},{6,7},{7,6},{8,9},{9,8},{10,11... | collective-permute-start | bytes 393224 | tf_op jit(solution)/shard_map/ppermute | solution.py:423
  125.6 1.9 %collective-permute-start.7 = (bf16[64,768]{1,0:T(8,128)(2,1)}, bf16[64,768]{1,0:T(8,128)(2,1)S(1)}, u32[]{:S(2)}, u32[]{:S(2)}) collective-permute-start(bf16[64,768]{1,0:T(8,128)(2,1)} %get-tuple-element.55), channel_id=1, source_target_pairs={{4,0},{8,4},{12,8},{16,12},{20,16},{24,20},{28,24},{32,28},{36,32}... | collective-permute-start | bytes 294920 | tf_op jit(solution)/shard_map/ppermute | solution.py:419
  127.6 3.6 %local.1.local_ref = f32[64,3072]{1,0:T(8,128)} custom-call(s32[2,24]{1,0:T(2,128)} %bitcast.34, bf16[64,3072]{1,0:T(8,128)(2,1)} %get-tuple-element.53.x_ref, bf16[24,128,128]{2,1,0:T(8,128)(2,1)} %onsite_ref.3, bf16[24,128,128]{2,1,0:T(8,128)(2,1)} %down_ref.9, bf16[24,128,128]{2,1,0:T(8,128)(2,1)} %right_ref.3), custom_call_target="tpu_custom_call" | custom-call | flops 1000000 | bytes 100000 | tf_op jit(solution)/shard_map/local/pallas_call | solution.py:365
  131.1 4.0 %collective-permute-done.7.below_ref = bf16[64,768]{1,0:T(8,128)(2,1)S(1)} collective-permute-done((bf16[64,768]{1,0:T(8,128)(2,1)}, bf16[64,768]{1,0:T(8,128)(2,1)S(1)}, u32[]{:S(2)}, u32[]{:S(2)}) %collective-permute-start.7) | collective-permute-done | bytes 98336 | tf_op jit(solution)/shard_map/ppermute | solution.py:419
  136.0 4.8 %second.1 = (f32[64,3072]{1,0:T(8,128)}, f32[3,4,3072]{2,1,0:T(4,128)}) custom-call(s32[2,24]{1,0:T(2,128)} %bitcast.35, s32[1]{0:T(128)} %bitcast.1.left_ref, bf16[64,3072]{1,0:T(8,128)(2,1)} %bitcast.22, f32[64,3072]{1,0:T(8,128)} %get-tuple-element.48.one_ref, bf16[1024,128]{1,0:T(8,128)(2,1)} %bitcast.26, bf16[3072,256]{1,0:T(8,128)(2,1)} %get-tuple-element.43.hot_ref, ...), custom_call_target="tpu_custom_call" | custom-call | flops 1000000 | bytes 100000 | tf_op jit(solution)/shard_map/second/pallas_call | solution.py:403
  (29 shorter events, 2.1 us)
Async XLA Ops:
  2.7 28.9 %collective-permute-start = (f32[64,768]{1,0:T(8,128)}, f32[64,768]{1,0:T(8,128)S(1)}, u32[]{:S(2)}, u32[]{:S(2)}) collective-permute-start(f32[64,768]{1,0:T(8,128)} %get-tuple-element.36), channel_id=1, source_target_pairs={{0,4},{4,8},{8,12},{12,16},{16,20},{20,24},{24,28},{28,32},{32,36}... | collective-permute-start | bytes 589832 | tf_op jit(solution)/shard_map/ppermute | solution.py:419
  7.6 24.0 %collective-permute-start.2 = (f32[64,512]{1,0:T(8,128)}, f32[64,512]{1,0:T(8,128)S(1)}, u32[]{:S(2)}, u32[]{:S(2)}) collective-permute-start(f32[64,512]{1,0:T(8,128)} %get-tuple-element.38), channel_id=1, source_target_pairs={{0,1},{1,0},{2,3},{3,2},{4,5},{5,4},{6,7},{7,6},{8,9},{9,8},{10,11... | collective-permute-start | bytes 393224 | tf_op jit(solution)/shard_map/ppermute | solution.py:423
  13.4 18.2 %collective-permute-start.1 = (bf16[64,768]{1,0:T(8,128)(2,1)}, bf16[64,768]{1,0:T(8,128)(2,1)S(1)}, u32[]{:S(2)}, u32[]{:S(2)}) collective-permute-start(bf16[64,768]{1,0:T(8,128)(2,1)} %get-tuple-element.37), channel_id=1, source_target_pairs={{4,0},{8,4},{12,8},{16,12},{20,16},{24,20},{28,24},{32,28},{36,32}... | collective-permute-start | bytes 294920 | tf_op jit(solution)/shard_map/ppermute | solution.py:419
  15.3 12.8 %collective-permute-start.3 = (f32[3,8,128]{2,1,0:T(8,128)}, f32[3,8,128]{2,1,0:T(8,128)S(1)}, u32[]{:S(2)}, u32[]{:S(2)}) collective-permute-start(f32[3,8,128]{2,1,0:T(8,128)} %get-tuple-element.34.table_ref), channel_id=1, source_target_pairs={{0,2},{1,3},{2,0},{3,1},{4,6},{5,7},{6,4},{7,5},{8,10},{9,11},{10,... | collective-permute-start | bytes 36872 | tf_op jit(solution)/shard_map/ppermute | solution.py:423
  28.1 0.6 copy-start.11
  31.6 0.6 copy-start.9
  31.6 0.7 copy-start.7
  31.6 0.7 copy-start.5
  32.3 12.8 %copy-start.4 = (bf16[1024,128]{1,0:T(8,128)(2,1)S(1)}, bf16[1024,128]{1,0:T(8,128)(2,1)}, u32[]{:S(2)}) copy-start(bf16[1024,128]{1,0:T(8,128)(2,1)} %get-tuple-element.35) | copy-start | bytes 786436
  40.3 33.5 %collective-permute-start.5 = (f32[1024,128]{1,0:T(8,128)}, f32[1024,128]{1,0:T(8,128)S(1)}, u32[]{:S(2)}, u32[]{:S(2)}) collective-permute-start(f32[1024,128]{1,0:T(8,128)} %get-tuple-element.52), channel_id=1, source_target_pairs={{0,2},{1,3},{2,0},{3,1},{4,6},{5,7},{6,4},{7,5},{8,10},{9,11},{10,... | collective-permute-start | bytes 1572872 | tf_op jit(solution)/shard_map/ppermute | solution.py:423
  73.2 19.5 %copy-start = (bf16[128,8,128]{2,1,0:T(8,128)(2,1)S(1)}, bf16[128,8,128]{2,1,0:T(8,128)(2,1)}, u32[]{:S(2)}) copy-start(bf16[128,8,128]{2,1,0:T(8,128)(2,1)} %all_to_all.10) | copy-start | bytes 786436
  73.8 0.8 copy-start.2
  81.9 53.2 %all-to-all-start.1 = ((bf16[128,8,128]{2,1,0:T(8,128)(2,1)}), bf16[128,8,128]{2,1,0:T(8,128)(2,1)S(1)}, u32[]{:S(2)}, u32[]{:S(2)}) async-start(bf16[128,8,128]{2,1,0:T(8,128)(2,1)} %bitcast.23), calls=%async_computation.1 | async-start | bytes 524288 | tf_op jit(solution)/shard_map/all_to_all | solution.py:427
  92.7 17.4 %collective-permute-start.4 = (bf16[1024,128]{1,0:T(8,128)(2,1)S(1)}, bf16[1024,128]{1,0:T(8,128)(2,1)S(1)}, u32[]{:S(2)}, u32[]{:S(2)}) collective-permute-start(bf16[1024,128]{1,0:T(8,128)(2,1)S(1)} %bitcast.25), channel_id=1, source_target_pairs={{0,2},{1,3},{2,0},{3,1},{4,6},{5,7},{6,4},{7,5},{8,10},{9,11},{10,... | collective-permute-start | bytes 786440 | tf_op jit(solution)/shard_map/ppermute | solution.py:423
  110.1 0.7 copy-start.3
  115.4 19.8 %collective-permute-start.6 = (f32[64,768]{1,0:T(8,128)}, f32[64,768]{1,0:T(8,128)S(1)}, u32[]{:S(2)}, u32[]{:S(2)}) collective-permute-start(f32[64,768]{1,0:T(8,128)} %get-tuple-element.54), channel_id=1, source_target_pairs={{0,4},{4,8},{8,12},{12,16},{16,20},{20,24},{24,28},{28,32},{32,36}... | collective-permute-start | bytes 589832 | tf_op jit(solution)/shard_map/ppermute | solution.py:419
  120.1 15.0 %collective-permute-start.8 = (f32[64,512]{1,0:T(8,128)}, f32[64,512]{1,0:T(8,128)S(1)}, u32[]{:S(2)}, u32[]{:S(2)}) collective-permute-start(f32[64,512]{1,0:T(8,128)} %get-tuple-element.56), channel_id=1, source_target_pairs={{0,1},{1,0},{2,3},{3,2},{4,5},{5,4},{6,7},{7,6},{8,9},{9,8},{10,11... | collective-permute-start | bytes 393224 | tf_op jit(solution)/shard_map/ppermute | solution.py:423
  125.6 9.5 %collective-permute-start.7 = (bf16[64,768]{1,0:T(8,128)(2,1)}, bf16[64,768]{1,0:T(8,128)(2,1)S(1)}, u32[]{:S(2)}, u32[]{:S(2)}) collective-permute-start(bf16[64,768]{1,0:T(8,128)(2,1)} %get-tuple-element.55), channel_id=1, source_target_pairs={{4,0},{8,4},{12,8},{16,12},{20,16},{24,20},{28,24},{32,28},{36,32}... | collective-permute-start | bytes 294920 | tf_op jit(solution)/shard_map/ppermute | solution.py:419
  135.1 0.6 copy-start.10
  135.1 0.7 copy-start.8
  135.1 0.8 copy-start.6
  135.1 0.8 copy-start.1

commit v3 on v2

--- a/solution.py
+++ b/solution.py
@@ -56,7 +56,7 @@
             hot_ref[SLOTS : 2 * SLOTS, :] = jnp.where(same, wide_weight, 0.0).astype(BF16)
 
 
-def gather_ends(terms, hot_ref, high_ref, start, chunk):
+def gather_ends(parts, hot_ref, high_ref, start, chunk):
     lane = lax.broadcasted_iota(jnp.int32, (chunk, TILE), 1)
     half = (lane >= ROWS).astype(F32)
     ends = []
@@ -65,7 +65,7 @@
         high = high_ref[end * SLOTS + start : end * SLOTS + start + chunk, :] - half
         total = jnp.zeros((chunk, TILE), F32)
         for q in range(HI // 2):
-            found = sum(dot(hot, jnp.concatenate([t[2 * q], t[2 * q + 1]], axis=0), NT) for t in terms)
+            found = dot(hot, jnp.concatenate([parts[2 * q], parts[2 * q + 1]], axis=0), NT)
             total = jnp.where(high == 2.0 * q, found, total)
         ends.append(total + pltpu.roll(total, ROWS, 1))
     return jnp.where(lane < ROWS, ends[0], ends[1])
@@ -77,20 +77,25 @@
     return jnp.where(lane < ROWS, field.astype(F32), field.astype(F32) * weight).astype(BF16)
 
 
-def split(value):
-    high = value.astype(BF16)
-    return high, (value - high.astype(F32)).astype(BF16)
-
-
 CHUNK = 256
 
 
-def prepare_kernel(x_ref, table_ref, hot_ref, high_ref, spread_ref, out_ref):
-    build_tables(table_ref[0], table_ref[1], table_ref[2], hot_ref, high_ref, spread_ref)
+def gather_payload(x_ref, hot_ref, high_ref, weight_ref, out_ref):
     parts = [x_ref[:, h * SPAN : (h + 1) * SPAN] for h in range(HI)]
     for start in range(0, SLOTS, CHUNK):
-        ends = gather_ends([parts], hot_ref, high_ref, start, CHUNK)
-        out_ref[start : start + CHUNK, :] = as_payload(ends, spread_ref[start : start + CHUNK, :])
+        ends = gather_ends(parts, hot_ref, high_ref, start, CHUNK)
+        out_ref[start : start + CHUNK, :] = as_payload(ends, weight_ref[start : start + CHUNK, :])
+
+
+def prepare_kernel(
+    x_ref, rows_ref, target_ref, weight_ref, count_ref, hot_ref, high_ref, spread_ref, out_ref
+):
+    live = lax.broadcasted_iota(jnp.int32, (CAP, PEERS), 0) < count_ref[...]
+    weight = jnp.where(live, weight_ref[...].astype(F32), 0.0)
+    build_tables(
+        rows_ref[...].astype(F32), target_ref[...].astype(F32), weight, hot_ref, high_ref, spread_ref
+    )
+    gather_payload(x_ref, hot_ref, high_ref, spread_ref, out_ref)
 
 
 TABLE_SHAPES = (
@@ -100,25 +105,14 @@
 )
 
 
-def prepare(x, table):
+def prepare(x, link_rows, link_target, link_weight, link_count):
     return pl.pallas_call(
         prepare_kernel,
         out_shape=TABLE_SHAPES + (jax.ShapeDtypeStruct((SLOTS, 2 * ROWS), BF16),),
         compiler_params=params(),
         cost_estimate=COST,
         name="prepare",
-    )(x, table)
-
-
-def tables_kernel(table_ref, hot_ref, high_ref, spread_ref):
-    build_tables(table_ref[0], table_ref[1], table_ref[2], hot_ref, high_ref, spread_ref)
-
-
-def tables_of(table):
-    return pl.pallas_call(
-        tables_kernel, out_shape=TABLE_SHAPES, compiler_params=params(),
-        cost_estimate=COST, name="other_tables"
-    )(table)
+    )(x, link_rows.T, link_target.T, link_weight.T, link_count.reshape(1, PEERS))
 
 
 def write_edges(pattern_ref, left_ref, x_ref, down_ref, right_ref, down_base, top_ref, below_ref, side_ref):
@@ -138,14 +132,7 @@
         side_ref[:, r * TILE : (r + 1) * TILE] = jnp.where(is_left, product, first_tile)
 
 
-def edges_kernel(
-    pattern_ref, left_ref, x_ref, down_ref, right_ref, rows_ref, target_ref, weight_ref, count_ref,
-    top_ref, below_ref, side_ref, table_ref,
-):
-    live = lax.broadcasted_iota(jnp.int32, (CAP, PEERS), 0) < count_ref[...]
-    table_ref[0] = rows_ref[...].astype(F32)
-    table_ref[1] = target_ref[...].astype(F32)
-    table_ref[2] = jnp.where(live, weight_ref[...].astype(F32), 0.0)
+def edges_kernel(pattern_ref, left_ref, x_ref, down_ref, right_ref, top_ref, below_ref, side_ref):
     write_edges(pattern_ref, left_ref, x_ref, down_ref, right_ref, 0, top_ref, below_ref, side_ref)
 
 
@@ -164,19 +151,17 @@
     return pl.BlockSpec(shape, lambda i: (0,) * len(shape))
 
 
-def edges(pattern, left_flag, x, down_hop, right_hop, link_rows, link_target, link_weight, link_count):
-    links = (link_rows.T, link_target.T, link_weight.T, link_count.reshape(1, PEERS))
-    shapes = EDGE_SHAPES + (jax.ShapeDtypeStruct((3, CAP, PEERS), F32),)
+def edges(pattern, left_flag, x, down_hop, right_hop):
     return pl.pallas_call(
         edges_kernel,
         grid=(1,),
-        in_specs=[SMEM, SMEM, whole((ROWS, SITES_DEV)), DOWN_EDGE, RIGHT_EDGE] + [whole(a.shape) for a in links],
-        out_specs=tuple(whole(s.shape) for s in shapes),
-        out_shape=shapes,
+        in_specs=[SMEM, SMEM, whole((ROWS, SITES_DEV)), DOWN_EDGE, RIGHT_EDGE],
+        out_specs=tuple(whole(s.shape) for s in EDGE_SHAPES),
+        out_shape=EDGE_SHAPES,
         compiler_params=params(),
         cost_estimate=COST,
         name="edges",
-    )(pattern, left_flag, x, down_hop, right_hop.reshape(TR, TC, TILE, TILE), *links)
+    )(pattern, left_flag, x, down_hop, right_hop.reshape(TR, TC, TILE, TILE))
 
 
 def kept(pattern_ref, which, tile, value):
@@ -245,7 +230,7 @@
 
 def near_kernel(
     pattern_ref, left_ref, v0_ref, onsite_ref, down_ref, right_ref, above_ref, below_ref, side_ref,
-    pairing_ref, hot_ref, high_ref, near_ref, out_ref,
+    pairing_ref, near_ref,
 ):
     is_left = left_ref[0] == 1
     for tile in range(TR * TC):
@@ -257,24 +242,17 @@
         )
         hop = hop if halo is None else hop + halo
         near_ref[:, cols] = signed(hop) + pairing_ref[:, cols] * swapped(v0_ref[:, cols].astype(F32))
-    pairs = [split(near_ref[:, h * SPAN : (h + 1) * SPAN]) for h in range(HI)]
-    terms = [[p[0] for p in pairs], [p[1] for p in pairs]]
-    for start in range(0, SLOTS, CHUNK):
-        out_ref[start : start + CHUNK, :] = gather_ends(terms, hot_ref, high_ref, start, CHUNK)
-
-
-def near(pattern, left_flag, v0, onsite, down_hop, right_hop, halo, pairing, hot, high):
+
+
+def near(pattern, left_flag, v0, onsite, down_hop, right_hop, halo, pairing):
     return pl.pallas_call(
         near_kernel,
-        in_specs=[SMEM, SMEM] + [VMEM] * 10,
-        out_shape=(
-            jax.ShapeDtypeStruct((ROWS, SITES_DEV), F32),
-            jax.ShapeDtypeStruct((SLOTS, 2 * ROWS), F32),
-        ),
+        in_specs=[SMEM, SMEM] + [VMEM] * 8,
+        out_shape=jax.ShapeDtypeStruct((ROWS, SITES_DEV), F32),
         compiler_params=params(),
         cost_estimate=COST,
         name="near",
-    )(pattern, left_flag, v0, onsite, down_hop, right_hop, *halo, pairing, hot, high)
+    )(pattern, left_flag, v0, onsite, down_hop, right_hop, *halo, pairing)
 
 
 SCATTER_SCRATCH = [pltpu.VMEM((HI * ROWS, 2 * SLOTS), BF16), pltpu.VMEM((HI * ROWS, SPAN), F32)]
@@ -296,30 +274,9 @@
         )
 
 
-def relay_kernel(landed_ref, hot_ref, high_ref, weight_ref, near_ref, out_ref, mask_ref, total_ref):
-    scatter_into(landed_ref[...], hot_ref, high_ref, mask_ref, total_ref)
-    pairs = [split(signed(total_ref[h * ROWS : (h + 1) * ROWS, :])) for h in range(HI)]
-    terms = [[p[0] for p in pairs], [p[1] for p in pairs]]
-    for start in range(0, SLOTS, CHUNK):
-        rows = slice(start, start + CHUNK)
-        ends = gather_ends(terms, hot_ref, high_ref, start, CHUNK) + near_ref[rows, :]
-        out_ref[rows, :] = as_payload(ends, weight_ref[rows, :])
-
-
-def relay(landed, hot, high, weight, near_ends):
-    return pl.pallas_call(
-        relay_kernel,
-        out_shape=jax.ShapeDtypeStruct((SLOTS, 2 * ROWS), BF16),
-        scratch_shapes=SCATTER_SCRATCH,
-        compiler_params=params(),
-        cost_estimate=COST,
-        name="relay",
-    )(landed, hot, high, weight, near_ends)
-
-
 def first_kernel(
-    pattern_ref, left_ref, v0_ref, landed_ref, hot_ref, high_ref, near_ref, down_ref, right_ref,
-    one_ref, x_ref, mom_ref, top_ref, below_ref, side_ref, mask_ref, total_ref,
+    pattern_ref, left_ref, v0_ref, landed_ref, hot_ref, high_ref, weight_ref, near_ref, down_ref, right_ref,
+    one_ref, x_ref, mom_ref, top_ref, below_ref, side_ref, out_ref, mask_ref, total_ref,
 ):
     scatter_into(landed_ref[...], hot_ref, high_ref, mask_ref, total_ref)
     for h in range(HI):
@@ -330,20 +287,21 @@
         x_ref[:, cols] = one.astype(BF16)
         mom_ref[0, :, cols] = vector_mean(v0 * v0)
         mom_ref[1, :, cols] = vector_mean(v0 * one)
+    gather_payload(x_ref, hot_ref, high_ref, weight_ref, out_ref)
     write_edges(pattern_ref, left_ref, x_ref, down_ref, right_ref, 0, top_ref, below_ref, side_ref)
 
 
-def first(pattern, left_flag, v0, landed, hot, high, near_part, down_hop, right_hop):
+def first(pattern, left_flag, v0, landed, hot, high, weight, near_part, down_hop, right_hop):
     shapes = (
         jax.ShapeDtypeStruct((ROWS, SITES_DEV), F32),
         jax.ShapeDtypeStruct((ROWS, SITES_DEV), BF16),
         jax.ShapeDtypeStruct((2, 4, SITES_DEV), F32),
-    ) + EDGE_SHAPES
+    ) + EDGE_SHAPES + (jax.ShapeDtypeStruct((SLOTS, 2 * ROWS), BF16),)
     return pl.pallas_call(
         first_kernel,
         grid=(1,),
         in_specs=[SMEM, SMEM]
-        + [whole(a.shape) for a in (v0, landed, hot, high, near_part)]
+        + [whole(a.shape) for a in (v0, landed, hot, high, weight, near_part)]
         + [DOWN_EDGE, RIGHT_EDGE],
         out_specs=tuple(whole(s.shape) for s in shapes),
         out_shape=shapes,
@@ -351,7 +309,7 @@
         compiler_params=params(),
         cost_estimate=COST,
         name="first",
-    )(pattern, left_flag, v0, landed, hot, high, near_part, down_hop, right_hop.reshape(TR, TC, TILE, TILE))
+    )(pattern, left_flag, v0, landed, hot, high, weight, near_part, down_hop, right_hop.reshape(TR, TC, TILE, TILE))
 
 
 def local_kernel(pattern_ref, x_ref, onsite_ref, down_ref, right_ref, out_ref):
@@ -457,30 +415,22 @@
             partner_2(side_part, "layer", 0),
         )
 
-    *edge_parts, table = edges(
-        pattern, left_flag, v0, down_hop, right_hop, link_rows, link_target, link_weight, link_count
-    )
-    halo = halo_of(*edge_parts)
-    tables_other = tables_of(other_layer(table))
-    hot, high, weight, payload = prepare(v0, table)
-    landed_other = spread_out(payload)
-    hot, tables_other = lax.optimization_barrier((hot, tables_other))
-    near_part, near_ends = near(
-        pattern, left_flag, v0, onsite, down_hop, right_hop, halo, pairing, hot, high
-    )
-    near_ends = other_layer(near_ends)
-    landed_other, near_part = lax.optimization_barrier((landed_other, near_part))
-    landed = other_layer(landed_other)
-    payload = relay(landed_other, *tables_other, near_ends)
-    landed_two = spread_out(payload)
-    one, x, mom, *edge_parts = first(
-        pattern, left_flag, v0, landed, hot, high, near_part, down_hop, right_hop
-    )
+    hot, high, weight, payload = prepare(v0, link_rows, link_target, link_weight, link_count)
+    spread = spread_out(payload)
+    halo = halo_of(*edges(pattern, left_flag, v0, down_hop, right_hop))
+    near_part = near(pattern, left_flag, v0, onsite, down_hop, right_hop, halo, pairing)
+    spread, near_part = lax.optimization_barrier((spread, near_part))
+    landed = other_layer(spread)
+    one, x, mom, *edge_parts, payload = first(
+        pattern, left_flag, v0, landed, hot, high, weight, near_part, down_hop, right_hop
+    )
+    spread = spread_out(payload)
     halo = halo_of(*edge_parts)
     local_part = local(pattern, x, onsite, down_hop, right_hop)
-    landed_two, local_part, halo = lax.optimization_barrier((landed_two, local_part, halo))
+    spread, local_part, halo = lax.optimization_barrier((spread, local_part, halo))
+    landed = other_layer(spread)
     two, mom = second(
-        pattern, left_flag, v0, one, landed_two, hot, high, local_part, pairing, mom, halo, down_hop, right_hop
+        pattern, left_flag, v0, one, landed, hot, high, local_part, pairing, mom, halo, down_hop, right_hop
     )
     shape = rand_vectors.shape
     return one.reshape(shape), two.reshape(shape), mom

time: 141 us -> 120 us (0.85)
  the two profiles are of different devices: /device:TPU:31 before, /device:TPU:63 now
where the time goes in v3:
time: 120 us; the launch traced here: 119 us
  starting transfers between devices  58.2 us (48%)
  waiting for transfers between devices  33.6 us (28%)
  Pallas kernels  24.5 us (20%)
  local copies, waits for them, and re-layouts  2.1 us (2%)
    all_to_all x2, starting transfers between devices, spread_out(): lax.all_to_all(payload.reshape(PEERS, CAP, 2 * ROWS), 'tile', split_axis=...  24.7 us
    ppermute x4, starting transfers between devices, partner_2(): lax.ppermute(value, axis, [(i, i ^ 1 << bit) for i in range(lax.axis_size...  23 us
    ppermute x4, waiting for transfers between devices, partner_2(): lax.ppermute(value, axis, [(i, i ^ 1 << bit) for i in range(lax.axis_size...  20.3 us
    ppermute x4, waiting for transfers between devices, passed_along(): return lax.ppermute(value, axis, pairs)  13.3 us
    ppermute x4, starting transfers between devices, passed_along(): return lax.ppermute(value, axis, pairs)  10.5 us
    pallas_call x1, Pallas kernels, first(): pl.pallas_call(first_kernel, grid=(1,), in_specs=[SMEM, SMEM] + [whole(a....  6.35 us
    pallas_call x1, Pallas kernels, second(): pl.pallas_call(second_kernel, grid=(1,), in_specs=[SMEM, SMEM] + [whole(a...  4.81 us
    pallas_call x1, Pallas kernels, prepare(): pl.pallas_call(prepare_kernel, out_shape=TABLE_SHAPES + (jax.ShapeDtypeSt...  3.95 us
  transfers between devices with their start and end apart: 10, of which 4 were waited for; matrix products, arithmetic and copies ran while one was open for 0% of the time, Pallas kernels for 8%

profile of v3, /device:TPU:63, one launch (start us, length us, event | category | flops | bytes accessed | tf_op | source)
XLA Modules:
  0.0 119.2 jit_solution(4678884497786047521)
XLA Ops:
  0.6 3.9 %prepare.1 = (bf16[3072,256]{1,0:T(8,128)(2,1)}, f32[2048,128]{1,0:T(8,128)}, f32[1024,128]{1,0:T(8,128)}, bf16[1024,128]{1,0:T(8,128)(2,1)}) custom-call(bf16[64,3072]{1,0:T(8,128)(2,1)} %bitcast.18, s32[8,128]{1,0:T(8,128)} %bitcast.35, s32[8,128]{1,0:T(8,128)} %bitcast.36, bf16[8,128]{1,0:T(8,128)(2,1)} %bitcast.37, s32[1,128]{1,0:T(1,128)} %bitcast.38), custom_call_target="tpu_custom_call" | custom-call | flops 1000000 | bytes 100000 | tf_op jit(solution)/shard_map/prepare/pallas_call | solution.py:109
  4.6 13.0 %all-to-all-start = ((bf16[128,8,128]{2,1,0:T(8,128)(2,1)}), bf16[128,8,128]{2,1,0:T(8,128)(2,1)S(1)}, u32[]{:S(2)}, u32[]{:S(2)}) async-start(bf16[128,8,128]{2,1,0:T(8,128)(2,1)} %bitcast.25), calls=%async_computation | async-start | bytes 524288 | tf_op jit(solution)/shard_map/all_to_all | solution.py:385
  17.6 2.0 %edges.1 = (bf16[64,768]{1,0:T(8,128)(2,1)}, f32[64,768]{1,0:T(8,128)}, f32[64,512]{1,0:T(8,128)}) custom-call(s32[2,24]{1,0:T(2,128)} %bitcast.30, s32[1]{0:T(128)} %bitcast.1.left_ref, bf16[64,3072]{1,0:T(8,128)(2,1)} %bitcast.19, bf16[24,128,128]{2,1,0:T(8,128)(2,1)} %down_ref.9, bf16[4,6,128,128]{3,2,1,0:T(8,128)(2,1)} %bitcast.15), custom_call_target="tpu_custom_call" | custom-call | flops 1000000 | bytes 100000 | tf_op jit(solution)/shard_map/edges/pallas_call | solution.py:155
  19.7 3.3 %collective-permute-start = (f32[64,768]{1,0:T(8,128)}, f32[64,768]{1,0:T(8,128)S(1)}, u32[]{:S(2)}, u32[]{:S(2)}) collective-permute-start(f32[64,768]{1,0:T(8,128)} %get-tuple-element.27), channel_id=1, source_target_pairs={{0,4},{4,8},{8,12},{12,16},{16,20},{20,24},{24,28},{28,32},{32,36}... | collective-permute-start | bytes 589832 | tf_op jit(solution)/shard_map/ppermute | solution.py:377
  23.0 5.8 %collective-permute-start.2 = (f32[64,512]{1,0:T(8,128)}, f32[64,512]{1,0:T(8,128)S(1)}, u32[]{:S(2)}, u32[]{:S(2)}) collective-permute-start(f32[64,512]{1,0:T(8,128)} %get-tuple-element.29), channel_id=1, source_target_pairs={{0,1},{1,0},{2,3},{3,2},{4,5},{5,4},{6,7},{7,6},{8,9},{9,8},{10,11... | collective-permute-start | bytes 393224 | tf_op jit(solution)/shard_map/ppermute | solution.py:381
  28.8 1.9 %collective-permute-start.1 = (bf16[64,768]{1,0:T(8,128)(2,1)}, bf16[64,768]{1,0:T(8,128)(2,1)S(1)}, u32[]{:S(2)}, u32[]{:S(2)}) collective-permute-start(bf16[64,768]{1,0:T(8,128)(2,1)} %get-tuple-element.28), channel_id=1, source_target_pairs={{4,0},{8,4},{12,8},{16,12},{20,16},{24,20},{28,24},{32,28},{36,32}... | collective-permute-start | bytes 294920 | tf_op jit(solution)/shard_map/ppermute | solution.py:377
  30.7 8.4 %collective-permute-done.1.below_ref = bf16[64,768]{1,0:T(8,128)(2,1)S(1)} collective-permute-done((bf16[64,768]{1,0:T(8,128)(2,1)}, bf16[64,768]{1,0:T(8,128)(2,1)S(1)}, u32[]{:S(2)}, u32[]{:S(2)}) %collective-permute-start.1) | collective-permute-done | bytes 98336 | tf_op jit(solution)/shard_map/ppermute | solution.py:377
  39.2 0.6 copy-done.7
  39.8 0.1 copy-done.5
  39.9 3.8 %near.1.near_ref = f32[64,3072]{1,0:T(8,128)} custom-call(s32[2,24]{1,0:T(2,128)} %bitcast.31, s32[1]{0:T(128)} %bitcast.1.left_ref, bf16[64,3072]{1,0:T(8,128)(2,1)} %bitcast.20, bf16[24,128,128]{2,1,0:T(8,128)(2,1)} %onsite_ref.3, bf16[24,128,128]{2,1,0:T(8,128)(2,1)} %down_ref.9, bf16[24,128,128]{2,1,0:T(8,128)(2,1)} %right_ref.3, f32[64,768]{1,0:T(8,128)} %copy-done.3, ...), custom_call_target="tpu_custom_call" | custom-call | flops 1000000 | bytes 100000 | tf_op jit(solution)/shard_map/near/pallas_call | solution.py:248
  43.8 7.9 %collective-permute-start.3 = (bf16[1024,128]{1,0:T(8,128)(2,1)S(1)}, bf16[1024,128]{1,0:T(8,128)(2,1)S(1)}, u32[]{:S(2)}, u32[]{:S(2)}) collective-permute-start(bf16[1024,128]{1,0:T(8,128)(2,1)S(1)} %bitcast.24), channel_id=1, source_target_pairs={{0,2},{1,3},{2,0},{3,1},{4,6},{5,7},{6,4},{7,5},{8,10},{9,11},{10,... | collective-permute-start | bytes 786440 | tf_op jit(solution)/shard_map/ppermute | solution.py:381
  51.7 9.0 %collective-permute-done.3.landed_ref = bf16[1024,128]{1,0:T(8,128)(2,1)S(1)} collective-permute-done((bf16[1024,128]{1,0:T(8,128)(2,1)S(1)}, bf16[1024,128]{1,0:T(8,128)(2,1)S(1)}, u32[]{:S(2)}, u32[]{:S(2)}) %collective-permute-start.3) | collective-permute-done | bytes 262176 | tf_op jit(solution)/shard_map/ppermute | solution.py:381
  60.7 0.7 copy-done.1
  61.3 6.3 %first.1 = (f32[64,3072]{1,0:T(8,128)}, bf16[64,3072]{1,0:T(8,128)(2,1)}, f32[2,4,3072]{2,1,0:T(4,128)}, bf16[64,768]{1,0:T(8,128)(2,1)}, f32[64,768]{1,0:T(8,12...) custom-call(s32[2,24]{1,0:T(2,128)} %bitcast.32, s32[1]{0:T(128)} %bitcast.1.left_ref, bf16[64,3072]{1,0:T(8,128)(2,1)} %bitcast.21, ...), custom_call_target="tpu_custom_call" | custom-call | flops 1000000 | bytes 100000 | tf_op jit(solution)/shard_map/first/pallas_call | solution.py:300
  67.7 11.6 %all-to-all-start.1 = ((bf16[128,8,128]{2,1,0:T(8,128)(2,1)}), bf16[128,8,128]{2,1,0:T(8,128)(2,1)S(1)}, u32[]{:S(2)}, u32[]{:S(2)}) async-start(bf16[128,8,128]{2,1,0:T(8,128)(2,1)} %bitcast.27), calls=%async_computation.1 | async-start | bytes 524288 | tf_op jit(solution)/shard_map/all_to_all | solution.py:385
  79.3 3.4 %collective-permute-start.4 = (f32[64,768]{1,0:T(8,128)}, f32[64,768]{1,0:T(8,128)S(1)}, u32[]{:S(2)}, u32[]{:S(2)}) collective-permute-start(f32[64,768]{1,0:T(8,128)} %get-tuple-element.38), channel_id=1, source_target_pairs={{0,4},{4,8},{8,12},{12,16},{16,20},{20,24},{24,28},{28,32},{32,36}... | collective-permute-start | bytes 589832 | tf_op jit(solution)/shard_map/ppermute | solution.py:377
  82.7 1.9 %collective-permute-start.6 = (f32[64,512]{1,0:T(8,128)}, f32[64,512]{1,0:T(8,128)S(1)}, u32[]{:S(2)}, u32[]{:S(2)}) collective-permute-start(f32[64,512]{1,0:T(8,128)} %get-tuple-element.40), channel_id=1, source_target_pairs={{0,1},{1,0},{2,3},{3,2},{4,5},{5,4},{6,7},{7,6},{8,9},{9,8},{10,11... | collective-permute-start | bytes 393224 | tf_op jit(solution)/shard_map/ppermute | solution.py:381
  84.6 1.9 %collective-permute-start.5 = (bf16[64,768]{1,0:T(8,128)(2,1)}, bf16[64,768]{1,0:T(8,128)(2,1)S(1)}, u32[]{:S(2)}, u32[]{:S(2)}) collective-permute-start(bf16[64,768]{1,0:T(8,128)(2,1)} %get-tuple-element.39), channel_id=1, source_target_pairs={{4,0},{8,4},{12,8},{16,12},{20,16},{24,20},{28,24},{32,28},{36,32}... | collective-permute-start | bytes 294920 | tf_op jit(solution)/shard_map/ppermute | solution.py:377
  86.5 3.5 %local.1.local_ref = f32[64,3072]{1,0:T(8,128)} custom-call(s32[2,24]{1,0:T(2,128)} %bitcast.33, bf16[64,3072]{1,0:T(8,128)(2,1)} %get-tuple-element.37.x_ref, bf16[24,128,128]{2,1,0:T(8,128)(2,1)} %onsite_ref.3, bf16[24,128,128]{2,1,0:T(8,128)(2,1)} %down_ref.9, bf16[24,128,128]{2,1,0:T(8,128)(2,1)} %right_ref.3), custom_call_target="tpu_custom_call" | custom-call | flops 1000000 | bytes 100000 | tf_op jit(solution)/shard_map/local/pallas_call | solution.py:323
  90.1 4.9 %collective-permute-done.5.below_ref = bf16[64,768]{1,0:T(8,128)(2,1)S(1)} collective-permute-done((bf16[64,768]{1,0:T(8,128)(2,1)}, bf16[64,768]{1,0:T(8,128)(2,1)S(1)}, u32[]{:S(2)}, u32[]{:S(2)}) %collective-permute-start.5) | collective-permute-done | bytes 98336 | tf_op jit(solution)/shard_map/ppermute | solution.py:377
  95.0 7.4 %collective-permute-start.7 = (bf16[1024,128]{1,0:T(8,128)(2,1)S(1)}, bf16[1024,128]{1,0:T(8,128)(2,1)S(1)}, u32[]{:S(2)}, u32[]{:S(2)}) collective-permute-start(bf16[1024,128]{1,0:T(8,128)(2,1)S(1)} %bitcast.26), channel_id=1, source_target_pairs={{0,2},{1,3},{2,0},{3,1},{4,6},{5,7},{6,4},{7,5},{8,10},{9,11},{10,... | collective-permute-start | bytes 786440 | tf_op jit(solution)/shard_map/ppermute | solution.py:381
  102.4 11.3 %collective-permute-done.7.landed_ref = bf16[1024,128]{1,0:T(8,128)(2,1)S(1)} collective-permute-done((bf16[1024,128]{1,0:T(8,128)(2,1)S(1)}, bf16[1024,128]{1,0:T(8,128)(2,1)S(1)}, u32[]{:S(2)}, u32[]{:S(2)}) %collective-permute-start.7) | collective-permute-done | bytes 262176 | tf_op jit(solution)/shard_map/ppermute | solution.py:381
  113.7 0.7 copy-done
  114.4 4.8 %second.1 = (f32[64,3072]{1,0:T(8,128)}, f32[3,4,3072]{2,1,0:T(4,128)}) custom-call(s32[2,24]{1,0:T(2,128)} %bitcast.34, s32[1]{0:T(128)} %bitcast.1.left_ref, bf16[64,3072]{1,0:T(8,128)(2,1)} %bitcast.22, f32[64,3072]{1,0:T(8,128)} %get-tuple-element.35.one_ref, bf16[1024,128]{1,0:T(8,128)(2,1)} %copy-done, bf16[3072,256]{1,0:T(8,128)(2,1)} %get-tuple-element.31.hot_ref, ...), custom_call_target="tpu_custom_call" | custom-call | flops 1000000 | bytes 100000 | tf_op jit(solution)/shard_map/second/pallas_call | solution.py:361
  (18 shorter events, 0.1 us)
Async XLA Ops:
  4.6 39.2 %all-to-all-start = ((bf16[128,8,128]{2,1,0:T(8,128)(2,1)}), bf16[128,8,128]{2,1,0:T(8,128)(2,1)S(1)}, u32[]{:S(2)}, u32[]{:S(2)}) async-start(bf16[128,8,128]{2,1,0:T(8,128)(2,1)} %bitcast.25), calls=%async_computation | async-start | bytes 524288 | tf_op jit(solution)/shard_map/all_to_all | solution.py:385
  19.7 19.5 %collective-permute-start = (f32[64,768]{1,0:T(8,128)}, f32[64,768]{1,0:T(8,128)S(1)}, u32[]{:S(2)}, u32[]{:S(2)}) collective-permute-start(f32[64,768]{1,0:T(8,128)} %get-tuple-element.27), channel_id=1, source_target_pairs={{0,4},{4,8},{8,12},{12,16},{16,20},{20,24},{24,28},{28,32},{32,36}... | collective-permute-start | bytes 589832 | tf_op jit(solution)/shard_map/ppermute | solution.py:377
  23.0 16.2 %collective-permute-start.2 = (f32[64,512]{1,0:T(8,128)}, f32[64,512]{1,0:T(8,128)S(1)}, u32[]{:S(2)}, u32[]{:S(2)}) collective-permute-start(f32[64,512]{1,0:T(8,128)} %get-tuple-element.29), channel_id=1, source_target_pairs={{0,1},{1,0},{2,3},{3,2},{4,5},{5,4},{6,7},{7,6},{8,9},{9,8},{10,11... | collective-permute-start | bytes 393224 | tf_op jit(solution)/shard_map/ppermute | solution.py:381
  28.8 10.4 %collective-permute-start.1 = (bf16[64,768]{1,0:T(8,128)(2,1)}, bf16[64,768]{1,0:T(8,128)(2,1)S(1)}, u32[]{:S(2)}, u32[]{:S(2)}) collective-permute-start(bf16[64,768]{1,0:T(8,128)(2,1)} %get-tuple-element.28), channel_id=1, source_target_pairs={{4,0},{8,4},{12,8},{16,12},{20,16},{24,20},{28,24},{32,28},{36,32}... | collective-permute-start | bytes 294920 | tf_op jit(solution)/shard_map/ppermute | solution.py:377
  39.2 0.6 copy-start.7
  39.2 0.7 copy-start.5
  39.2 0.7 copy-start.3
  43.8 16.9 %collective-permute-start.3 = (bf16[1024,128]{1,0:T(8,128)(2,1)S(1)}, bf16[1024,128]{1,0:T(8,128)(2,1)S(1)}, u32[]{:S(2)}, u32[]{:S(2)}) collective-permute-start(bf16[1024,128]{1,0:T(8,128)(2,1)S(1)} %bitcast.24), channel_id=1, source_target_pairs={{0,2},{1,3},{2,0},{3,1},{4,6},{5,7},{6,4},{7,5},{8,10},{9,11},{10,... | collective-permute-start | bytes 786440 | tf_op jit(solution)/shard_map/ppermute | solution.py:381
  60.6 0.7 copy-start.1
  67.7 27.3 %all-to-all-start.1 = ((bf16[128,8,128]{2,1,0:T(8,128)(2,1)}), bf16[128,8,128]{2,1,0:T(8,128)(2,1)S(1)}, u32[]{:S(2)}, u32[]{:S(2)}) async-start(bf16[128,8,128]{2,1,0:T(8,128)(2,1)} %bitcast.27), calls=%async_computation.1 | async-start | bytes 524288 | tf_op jit(solution)/shard_map/all_to_all | solution.py:385
  79.3 15.7 %collective-permute-start.4 = (f32[64,768]{1,0:T(8,128)}, f32[64,768]{1,0:T(8,128)S(1)}, u32[]{:S(2)}, u32[]{:S(2)}) collective-permute-start(f32[64,768]{1,0:T(8,128)} %get-tuple-element.38), channel_id=1, source_target_pairs={{0,4},{4,8},{8,12},{12,16},{16,20},{20,24},{24,28},{28,32},{32,36}... | collective-permute-start | bytes 589832 | tf_op jit(solution)/shard_map/ppermute | solution.py:377
  82.7 12.3 %collective-permute-start.6 = (f32[64,512]{1,0:T(8,128)}, f32[64,512]{1,0:T(8,128)S(1)}, u32[]{:S(2)}, u32[]{:S(2)}) collective-permute-start(f32[64,512]{1,0:T(8,128)} %get-tuple-element.40), channel_id=1, source_target_pairs={{0,1},{1,0},{2,3},{3,2},{4,5},{5,4},{6,7},{7,6},{8,9},{9,8},{10,11... | collective-permute-start | bytes 393224 | tf_op jit(solution)/shard_map/ppermute | solution.py:381
  84.6 10.4 %collective-permute-start.5 = (bf16[64,768]{1,0:T(8,128)(2,1)}, bf16[64,768]{1,0:T(8,128)(2,1)S(1)}, u32[]{:S(2)}, u32[]{:S(2)}) collective-permute-start(bf16[64,768]{1,0:T(8,128)(2,1)} %get-tuple-element.39), channel_id=1, source_target_pairs={{4,0},{8,4},{12,8},{16,12},{20,16},{24,20},{28,24},{32,28},{36,32}... | collective-permute-start | bytes 294920 | tf_op jit(solution)/shard_map/ppermute | solution.py:377
  95.0 18.7 %copy-start.6 = (bf16[64,768]{1,0:T(8,128)(2,1)}, bf16[64,768]{1,0:T(8,128)(2,1)S(1)}, u32[]{:S(2)}) copy-start(bf16[64,768]{1,0:T(8,128)(2,1)S(1)} %collective-permute-done.5.below_ref) | copy-start | bytes 294916
  95.0 18.7 %copy-start.4 = (f32[64,512]{1,0:T(8,128)}, f32[64,512]{1,0:T(8,128)S(1)}, u32[]{:S(2)}) copy-start(f32[64,512]{1,0:T(8,128)S(1)} %collective-permute-done.6.side_ref) | copy-start | bytes 393220
  95.0 18.7 %copy-start.2 = (f32[64,768]{1,0:T(8,128)}, f32[64,768]{1,0:T(8,128)S(1)}, u32[]{:S(2)}) copy-start(f32[64,768]{1,0:T(8,128)S(1)} %collective-permute-done.4.above_ref) | copy-start | bytes 589828
  95.0 18.7 %collective-permute-start.7 = (bf16[1024,128]{1,0:T(8,128)(2,1)S(1)}, bf16[1024,128]{1,0:T(8,128)(2,1)S(1)}, u32[]{:S(2)}, u32[]{:S(2)}) collective-permute-start(bf16[1024,128]{1,0:T(8,128)(2,1)S(1)} %bitcast.26), channel_id=1, source_target_pairs={{0,2},{1,3},{2,0},{3,1},{4,6},{5,7},{6,4},{7,5},{8,10},{9,11},{10,... | collective-permute-start | bytes 786440 | tf_op jit(solution)/shard_map/ppermute | solution.py:381
  113.7 0.7 copy-start

commit v4 on v3

--- a/solution.py
+++ b/solution.py
@@ -3,6 +3,7 @@
 from jax import lax
 from jax.experimental import pallas as pl
 from jax.experimental.pallas import tpu as pltpu
+from jax.sharding import Mesh
 from jax.sharding import PartitionSpec as P
 
 TILE = 128
@@ -84,7 +85,9 @@
     parts = [x_ref[:, h * SPAN : (h + 1) * SPAN] for h in range(HI)]
     for start in range(0, SLOTS, CHUNK):
         ends = gather_ends(parts, hot_ref, high_ref, start, CHUNK)
-        out_ref[start : start + CHUNK, :] = as_payload(ends, weight_ref[start : start + CHUNK, :])
+        payload = as_payload(ends, weight_ref[start : start + CHUNK, :])
+        out_ref[0, start : start + CHUNK, :] = payload
+        out_ref[1, start : start + CHUNK, :] = payload
 
 
 def prepare_kernel(
@@ -108,7 +111,7 @@
 def prepare(x, link_rows, link_target, link_weight, link_count):
     return pl.pallas_call(
         prepare_kernel,
-        out_shape=TABLE_SHAPES + (jax.ShapeDtypeStruct((SLOTS, 2 * ROWS), BF16),),
+        out_shape=TABLE_SHAPES + (jax.ShapeDtypeStruct((2, SLOTS, 2 * ROWS), BF16),),
         compiler_params=params(),
         cost_estimate=COST,
         name="prepare",
@@ -278,7 +281,7 @@
     pattern_ref, left_ref, v0_ref, landed_ref, hot_ref, high_ref, weight_ref, near_ref, down_ref, right_ref,
     one_ref, x_ref, mom_ref, top_ref, below_ref, side_ref, out_ref, mask_ref, total_ref,
 ):
-    scatter_into(landed_ref[...], hot_ref, high_ref, mask_ref, total_ref)
+    scatter_into(landed_ref[left_ref[1]], hot_ref, high_ref, mask_ref, total_ref)
     for h in range(HI):
         cols = slice(h * SPAN, (h + 1) * SPAN)
         v0 = v0_ref[:, cols].astype(F32)
@@ -296,7 +299,7 @@
         jax.ShapeDtypeStruct((ROWS, SITES_DEV), F32),
         jax.ShapeDtypeStruct((ROWS, SITES_DEV), BF16),
         jax.ShapeDtypeStruct((2, 4, SITES_DEV), F32),
-    ) + EDGE_SHAPES + (jax.ShapeDtypeStruct((SLOTS, 2 * ROWS), BF16),)
+    ) + EDGE_SHAPES + (jax.ShapeDtypeStruct((2, SLOTS, 2 * ROWS), BF16),)
     return pl.pallas_call(
         first_kernel,
         grid=(1,),
@@ -334,7 +337,7 @@
     pattern_ref, left_ref, v0_ref, one_ref, landed_ref, hot_ref, high_ref, local_ref, pairing_ref, mom_in_ref,
     above_ref, below_ref, side_ref, down_ref, right_ref, two_ref, mom_ref, mask_ref, total_ref,
 ):
-    scatter_into(landed_ref[...], hot_ref, high_ref, mask_ref, total_ref)
+    scatter_into(landed_ref[left_ref[1]], hot_ref, high_ref, mask_ref, total_ref)
     is_left = left_ref[0] == 1
     mom_ref[0:2] = mom_in_ref[...]
     for tile in range(TR * TC):
@@ -371,24 +374,20 @@
     )(pattern, left_flag, *arrays, down_hop, right_hop.reshape(TR, TC, TILE, TILE))
 
 
-def passed_along(value, axis, by):
-    length = lax.axis_size(axis)
+TILE_AXES = ("z_low", "y", "x", "core")
+
+
+def passed_along(value, by):
+    length = PEERS
     pairs = [(i, i + by) for i in range(length) if 0 <= i + by < length]
-    return lax.ppermute(value, axis, pairs)
-
-
-def partner_2(value, axis, bit):
-    return lax.ppermute(value, axis, [(i, i ^ 1 << bit) for i in range(lax.axis_size(axis))])
+    return lax.ppermute(value, TILE_AXES, pairs)
 
 
 def spread_out(payload):
-    return lax.all_to_all(
-        payload.reshape(PEERS, CAP, 2 * ROWS), "tile", split_axis=0, concat_axis=0, tiled=True
-    ).reshape(SLOTS, 2 * ROWS)
-
-
-def other_layer(value):
-    return partner_2(value, "layer", 1)
+    spread = lax.all_to_all(
+        payload.reshape(2 * PEERS, CAP, 2 * ROWS), ("sheet",) + TILE_AXES, split_axis=0, concat_axis=0, tiled=True
+    )
+    return spread.reshape(2, SLOTS, 2 * ROWS)
 
 
 def shards(
@@ -406,29 +405,27 @@
     v0 = rand_vectors.reshape(ROWS, SITES_DEV)
     pairing = pairing.reshape(1, SITES_DEV)
     pattern = pattern.T
-    left_flag = (1 - lax.axis_index("layer") % 2).astype(jnp.int32).reshape(1)
+    left_flag = jnp.stack([1 - lax.axis_index("side"), 1 - lax.axis_index("sheet")]).astype(jnp.int32)
 
     def halo_of(top, below_part, side_part):
         return (
-            passed_along(below_part, "tile", 1),
-            passed_along(top, "tile", -1),
-            partner_2(side_part, "layer", 0),
+            passed_along(below_part, 1),
+            passed_along(top, -1),
+            lax.ppermute(side_part, "side", [(0, 1), (1, 0)]),
         )
 
     hot, high, weight, payload = prepare(v0, link_rows, link_target, link_weight, link_count)
     spread = spread_out(payload)
     halo = halo_of(*edges(pattern, left_flag, v0, down_hop, right_hop))
     near_part = near(pattern, left_flag, v0, onsite, down_hop, right_hop, halo, pairing)
-    spread, near_part = lax.optimization_barrier((spread, near_part))
-    landed = other_layer(spread)
+    landed, near_part = lax.optimization_barrier((spread, near_part))
     one, x, mom, *edge_parts, payload = first(
         pattern, left_flag, v0, landed, hot, high, weight, near_part, down_hop, right_hop
     )
     spread = spread_out(payload)
     halo = halo_of(*edge_parts)
     local_part = local(pattern, x, onsite, down_hop, right_hop)
-    spread, local_part, halo = lax.optimization_barrier((spread, local_part, halo))
-    landed = other_layer(spread)
+    landed, local_part, halo = lax.optimization_barrier((spread, local_part, halo))
     two, mom = second(
         pattern, left_flag, v0, one, landed, hot, high, local_part, pairing, mom, halo, down_hop, right_hop
     )
@@ -437,7 +434,8 @@
 
 
 def solution(mesh):
-    both = ("tile", "layer")
+    both = TILE_AXES + ("sheet", "side")
+    mesh = Mesh(mesh.devices.reshape(2, 8, 4, 2, 2, 2), both)
     in_specs = (
         P(None, None, both),
         P(both, None, None),

time: 120 us -> 105 us (0.88)
  the two profiles are of different devices: /device:TPU:63 before, /device:TPU:1 now
where the time goes in v4:
time: 105 us; the launch traced here: 104 us
  starting transfers between devices  53.7 us (51%)
  Pallas kernels  24.9 us (24%)
  waiting for transfers between devices  22 us (21%)
  local copies, waits for them, and re-layouts  2.31 us (2%)
    all_to_all x2, starting transfers between devices, spread_out(): lax.all_to_all(payload.reshape(2 * PEERS, CAP, 2 * ROWS), ('sheet',) + TI...  36.4 us
    ppermute x2, waiting for transfers between devices, halo_of(): lax.ppermute(side_part, 'side', [(0, 1), (1, 0)])  13.8 us
    ppermute x4, starting transfers between devices, passed_along(): return lax.ppermute(value, TILE_AXES, pairs)  10.9 us
    pallas_call x1, Pallas kernels, first(): pl.pallas_call(first_kernel, grid=(1,), in_specs=[SMEM, SMEM] + [whole(a....  6.54 us
    ppermute x4, waiting for transfers between devices, passed_along(): return lax.ppermute(value, TILE_AXES, pairs)  6.38 us
    ppermute x2, starting transfers between devices, halo_of(): lax.ppermute(side_part, 'side', [(0, 1), (1, 0)])  6.33 us
    pallas_call x1, Pallas kernels, second(): pl.pallas_call(second_kernel, grid=(1,), in_specs=[SMEM, SMEM] + [whole(a...  4.9 us
    pallas_call x1, Pallas kernels, prepare(): pl.pallas_call(prepare_kernel, out_shape=TABLE_SHAPES + (jax.ShapeDtypeSt...  4.04 us
  transfers between devices with their start and end apart: 8, of which 5 were waited for; matrix products, arithmetic and copies ran while one was open for 1% of the time, Pallas kernels for 9%

profile of v4, /device:TPU:1, one launch (start us, length us, event | category | flops | bytes accessed | tf_op | source)
XLA Modules:
  0.0 104.2 jit_solution(578231361935065858)
XLA Ops:
  0.6 4.0 %prepare.1 = (bf16[3072,256]{1,0:T(8,128)(2,1)}, f32[2048,128]{1,0:T(8,128)}, f32[1024,128]{1,0:T(8,128)}, bf16[2,1024,128]{2,1,0:T(8,128)(2,1)}) custom-call(bf16[64,3072]{1,0:T(8,128)(2,1)} %bitcast.19, s32[8,128]{1,0:T(8,128)} %bitcast.36, s32[8,128]{1,0:T(8,128)} %bitcast.37, bf16[8,128]{1,0:T(8,128)(2,1)} %bitcast.38, s32[1,128]{1,0:T(1,128)} %bitcast.39), custom_call_target="tpu_custom_call" | custom-call | flops 1000000 | bytes 100000 | tf_op jit(solution)/shard_map/prepare/pallas_call | solution.py:112
  4.7 22.4 %all-to-all-start = ((bf16[256,8,128]{2,1,0:T(8,128)(2,1)}), bf16[256,8,128]{2,1,0:T(8,128)(2,1)S(1)}, u32[]{:S(2)}, u32[]{:S(2)}) async-start(bf16[256,8,128]{2,1,0:T(8,128)(2,1)} %bitcast.27), calls=%async_computation | async-start | bytes 1048576 | tf_op jit(solution)/shard_map/all_to_all | solution.py:387
  27.1 0.6 pad_add_fusion.left_ref
  27.7 2.0 %edges.1 = (bf16[64,768]{1,0:T(8,128)(2,1)}, f32[64,768]{1,0:T(8,128)}, f32[64,512]{1,0:T(8,128)}) custom-call(s32[2,24]{1,0:T(2,128)} %bitcast.31, s32[2]{0:T(128)} %pad_add_fusion.left_ref, bf16[64,3072]{1,0:T(8,128)(2,1)} %bitcast.20, bf16[24,128,128]{2,1,0:T(8,128)(2,1)} %down_ref.9, bf16[4,6,128,128]{3,2,1,0:T(8,128)(2,1)} %bitcast.16), custom_call_target="tpu_custom_call" | custom-call | flops 1000000 | bytes 100000 | tf_op jit(solution)/shard_map/edges/pallas_call | solution.py:158
  29.7 3.5 %collective-permute-start = (f32[64,768]{1,0:T(8,128)}, f32[64,768]{1,0:T(8,128)S(1)}, u32[]{:S(2)}, u32[]{:S(2)}) collective-permute-start(f32[64,768]{1,0:T(8,128)} %get-tuple-element.27), channel_id=1, source_target_pairs={{0,4},{4,8},{8,12},{12,16},{16,20},{20,24},{24,28},{28,32},{32,36}... | collective-permute-start | bytes 589832 | tf_op jit(solution)/shard_map/ppermute | solution.py:383
  33.3 4.0 %collective-permute-start.2 = (f32[64,512]{1,0:T(8,128)}, f32[64,512]{1,0:T(8,128)S(1)}, u32[]{:S(2)}, u32[]{:S(2)}) collective-permute-start(f32[64,512]{1,0:T(8,128)} %get-tuple-element.29), channel_id=1, source_target_pairs={{0,1},{1,0},{2,3},{3,2},{4,5},{5,4},{6,7},{7,6},{8,9},{9,8},{10,11... | collective-permute-start | bytes 393224 | tf_op jit(solution)/shard_map/ppermute | solution.py:414
  37.3 1.9 %collective-permute-start.1 = (bf16[64,768]{1,0:T(8,128)(2,1)}, bf16[64,768]{1,0:T(8,128)(2,1)S(1)}, u32[]{:S(2)}, u32[]{:S(2)}) collective-permute-start(bf16[64,768]{1,0:T(8,128)(2,1)} %get-tuple-element.28), channel_id=1, source_target_pairs={{4,0},{8,4},{12,8},{16,12},{20,16},{24,20},{28,24},{32,28},{36,32}... | collective-permute-start | bytes 294920 | tf_op jit(solution)/shard_map/ppermute | solution.py:383
  39.2 4.7 %collective-permute-done.1.below_ref = bf16[64,768]{1,0:T(8,128)(2,1)S(1)} collective-permute-done((bf16[64,768]{1,0:T(8,128)(2,1)}, bf16[64,768]{1,0:T(8,128)(2,1)S(1)}, u32[]{:S(2)}, u32[]{:S(2)}) %collective-permute-start.1) | collective-permute-done | bytes 98336 | tf_op jit(solution)/shard_map/ppermute | solution.py:383
  44.0 5.6 %collective-permute-done.2.side_ref = f32[64,512]{1,0:T(8,128)S(1)} collective-permute-done((f32[64,512]{1,0:T(8,128)}, f32[64,512]{1,0:T(8,128)S(1)}, u32[]{:S(2)}, u32[]{:S(2)}) %collective-permute-start.2) | collective-permute-done | bytes 131104 | tf_op jit(solution)/shard_map/ppermute | solution.py:414
  49.5 0.6 copy-done.5
  50.2 0.1 copy-done.2
  50.2 3.8 %near.1.near_ref = f32[64,3072]{1,0:T(8,128)} custom-call(s32[2,24]{1,0:T(2,128)} %bitcast.32, s32[2]{0:T(128)} %pad_add_fusion.left_ref, bf16[64,3072]{1,0:T(8,128)(2,1)} %bitcast.21, bf16[24,128,128]{2,1,0:T(8,128)(2,1)} %onsite_ref.3, bf16[24,128,128]{2,1,0:T(8,128)(2,1)} %down_ref.9, bf16[24,128,128]{2,1,0:T(8,128)(2,1)} %right_ref.3, ...), custom_call_target="tpu_custom_call" | custom-call | flops 1000000 | bytes 100000 | tf_op jit(solution)/shard_map/near/pallas_call | solution.py:251
  54.1 0.8 copy-done
  54.9 6.5 %first.1 = (f32[64,3072]{1,0:T(8,128)}, bf16[64,3072]{1,0:T(8,128)(2,1)}, f32[2,4,3072]{2,1,0:T(4,128)}, bf16[64,768]{1,0:T(8,128)(2,1)}, f32[64,768]{1,0:T(8,12...) custom-call(s32[2,24]{1,0:T(2,128)} %bitcast.33, s32[2]{0:T(128)} %pad_add_fusion.left_ref, ...), custom_call_target="tpu_custom_call" | custom-call | flops 1000000 | bytes 100000 | tf_op jit(solution)/shard_map/first/pallas_call | solution.py:303
  61.4 14.0 %all-to-all-start.1 = ((bf16[256,8,128]{2,1,0:T(8,128)(2,1)}), bf16[256,8,128]{2,1,0:T(8,128)(2,1)S(1)}, u32[]{:S(2)}, u32[]{:S(2)}) async-start(bf16[256,8,128]{2,1,0:T(8,128)(2,1)} %bitcast.28), calls=%async_computation.1 | async-start | bytes 1048576 | tf_op jit(solution)/shard_map/all_to_all | solution.py:387
  75.5 3.5 %collective-permute-start.3 = (f32[64,768]{1,0:T(8,128)}, f32[64,768]{1,0:T(8,128)S(1)}, u32[]{:S(2)}, u32[]{:S(2)}) collective-permute-start(f32[64,768]{1,0:T(8,128)} %get-tuple-element.38), channel_id=1, source_target_pairs={{0,4},{4,8},{8,12},{12,16},{16,20},{20,24},{24,28},{28,32},{32,36}... | collective-permute-start | bytes 589832 | tf_op jit(solution)/shard_map/ppermute | solution.py:383
  79.0 2.3 %collective-permute-start.5 = (f32[64,512]{1,0:T(8,128)}, f32[64,512]{1,0:T(8,128)S(1)}, u32[]{:S(2)}, u32[]{:S(2)}) collective-permute-start(f32[64,512]{1,0:T(8,128)} %get-tuple-element.40), channel_id=1, source_target_pairs={{0,1},{1,0},{2,3},{3,2},{4,5},{5,4},{6,7},{7,6},{8,9},{9,8},{10,11... | collective-permute-start | bytes 393224 | tf_op jit(solution)/shard_map/ppermute | solution.py:414
  81.3 1.9 %collective-permute-start.4 = (bf16[64,768]{1,0:T(8,128)(2,1)}, bf16[64,768]{1,0:T(8,128)(2,1)S(1)}, u32[]{:S(2)}, u32[]{:S(2)}) collective-permute-start(bf16[64,768]{1,0:T(8,128)(2,1)} %get-tuple-element.39), channel_id=1, source_target_pairs={{4,0},{8,4},{12,8},{16,12},{20,16},{24,20},{28,24},{32,28},{36,32}... | collective-permute-start | bytes 294920 | tf_op jit(solution)/shard_map/ppermute | solution.py:383
  83.3 3.5 %local.1.local_ref = f32[64,3072]{1,0:T(8,128)} custom-call(s32[2,24]{1,0:T(2,128)} %bitcast.34, bf16[64,3072]{1,0:T(8,128)(2,1)} %get-tuple-element.37.x_ref, bf16[24,128,128]{2,1,0:T(8,128)(2,1)} %onsite_ref.3, bf16[24,128,128]{2,1,0:T(8,128)(2,1)} %down_ref.9, bf16[24,128,128]{2,1,0:T(8,128)(2,1)} %right_ref.3), custom_call_target="tpu_custom_call" | custom-call | flops 1000000 | bytes 100000 | tf_op jit(solution)/shard_map/local/pallas_call | solution.py:326
  86.8 1.6 %collective-permute-done.4.below_ref = bf16[64,768]{1,0:T(8,128)(2,1)S(1)} collective-permute-done((bf16[64,768]{1,0:T(8,128)(2,1)}, bf16[64,768]{1,0:T(8,128)(2,1)S(1)}, u32[]{:S(2)}, u32[]{:S(2)}) %collective-permute-start.4) | collective-permute-done | bytes 98336 | tf_op jit(solution)/shard_map/ppermute | solution.py:383
  88.4 8.2 %collective-permute-done.5.side_ref = f32[64,512]{1,0:T(8,128)S(1)} collective-permute-done((f32[64,512]{1,0:T(8,128)}, f32[64,512]{1,0:T(8,128)S(1)}, u32[]{:S(2)}, u32[]{:S(2)}) %collective-permute-start.5) | collective-permute-done | bytes 131104 | tf_op jit(solution)/shard_map/ppermute | solution.py:414
  96.7 1.8 %all-to-all-done.1 = bf16[256,8,128]{2,1,0:T(8,128)(2,1)S(1)} async-done(((bf16[256,8,128]{2,1,0:T(8,128)(2,1)}), bf16[256,8,128]{2,1,0:T(8,128)(2,1)S(1)}, u32[]{:S(2)}, u32[]{:S(2)}) %all-to-all-start.1) | async-done | bytes 524320 | tf_op jit(solution)/shard_map/all_to_all | solution.py:387
  98.5 0.8 copy-done.1
  99.3 4.9 %second.1 = (f32[64,3072]{1,0:T(8,128)}, f32[3,4,3072]{2,1,0:T(4,128)}) custom-call(s32[2,24]{1,0:T(2,128)} %bitcast.35, s32[2]{0:T(128)} %pad_add_fusion.left_ref, bf16[64,3072]{1,0:T(8,128)(2,1)} %bitcast.23, f32[64,3072]{1,0:T(8,128)} %get-tuple-element.35.one_ref, bf16[2,1024,128]{2,1,0:T(8,128)(2,1)} %bitcast.25, ...), custom_call_target="tpu_custom_call" | custom-call | flops 1000000 | bytes 100000 | tf_op jit(solution)/shard_map/second/pallas_call | solution.py:364
  (15 shorter events, 0.0 us)
Async XLA Ops:
  4.7 49.4 %all-to-all-start = ((bf16[256,8,128]{2,1,0:T(8,128)(2,1)}), bf16[256,8,128]{2,1,0:T(8,128)(2,1)S(1)}, u32[]{:S(2)}, u32[]{:S(2)}) async-start(bf16[256,8,128]{2,1,0:T(8,128)(2,1)} %bitcast.27), calls=%async_computation | async-start | bytes 1048576 | tf_op jit(solution)/shard_map/all_to_all | solution.py:387
  29.7 19.8 %collective-permute-start = (f32[64,768]{1,0:T(8,128)}, f32[64,768]{1,0:T(8,128)S(1)}, u32[]{:S(2)}, u32[]{:S(2)}) collective-permute-start(f32[64,768]{1,0:T(8,128)} %get-tuple-element.27), channel_id=1, source_target_pairs={{0,4},{4,8},{8,12},{12,16},{16,20},{20,24},{24,28},{28,32},{32,36}... | collective-permute-start | bytes 589832 | tf_op jit(solution)/shard_map/ppermute | solution.py:383
  33.3 16.3 %collective-permute-start.2 = (f32[64,512]{1,0:T(8,128)}, f32[64,512]{1,0:T(8,128)S(1)}, u32[]{:S(2)}, u32[]{:S(2)}) collective-permute-start(f32[64,512]{1,0:T(8,128)} %get-tuple-element.29), channel_id=1, source_target_pairs={{0,1},{1,0},{2,3},{3,2},{4,5},{5,4},{6,7},{7,6},{8,9},{9,8},{10,11... | collective-permute-start | bytes 393224 | tf_op jit(solution)/shard_map/ppermute | solution.py:414
  37.3 6.7 %collective-permute-start.1 = (bf16[64,768]{1,0:T(8,128)(2,1)}, bf16[64,768]{1,0:T(8,128)(2,1)S(1)}, u32[]{:S(2)}, u32[]{:S(2)}) collective-permute-start(bf16[64,768]{1,0:T(8,128)(2,1)} %get-tuple-element.28), channel_id=1, source_target_pairs={{4,0},{8,4},{12,8},{16,12},{20,16},{24,20},{28,24},{32,28},{36,32}... | collective-permute-start | bytes 294920 | tf_op jit(solution)/shard_map/ppermute | solution.py:383
  44.0 5.6 %copy-start.7 = (bf16[64,768]{1,0:T(8,128)(2,1)}, bf16[64,768]{1,0:T(8,128)(2,1)S(1)}, u32[]{:S(2)}) copy-start(bf16[64,768]{1,0:T(8,128)(2,1)S(1)} %collective-permute-done.1.below_ref) | copy-start | bytes 294916
  49.5 0.7 copy-start.5
  49.5 0.7 copy-start.2
  54.1 0.8 copy-start
  61.4 37.1 %all-to-all-start.1 = ((bf16[256,8,128]{2,1,0:T(8,128)(2,1)}), bf16[256,8,128]{2,1,0:T(8,128)(2,1)S(1)}, u32[]{:S(2)}, u32[]{:S(2)}) async-start(bf16[256,8,128]{2,1,0:T(8,128)(2,1)} %bitcast.28), calls=%async_computation.1 | async-start | bytes 1048576 | tf_op jit(solution)/shard_map/all_to_all | solution.py:387
  75.5 21.2 %collective-permute-start.3 = (f32[64,768]{1,0:T(8,128)}, f32[64,768]{1,0:T(8,128)S(1)}, u32[]{:S(2)}, u32[]{:S(2)}) collective-permute-start(f32[64,768]{1,0:T(8,128)} %get-tuple-element.38), channel_id=1, source_target_pairs={{0,4},{4,8},{8,12},{12,16},{16,20},{20,24},{24,28},{28,32},{32,36}... | collective-permute-start | bytes 589832 | tf_op jit(solution)/shard_map/ppermute | solution.py:383
  79.0 17.7 %collective-permute-start.5 = (f32[64,512]{1,0:T(8,128)}, f32[64,512]{1,0:T(8,128)S(1)}, u32[]{:S(2)}, u32[]{:S(2)}) collective-permute-start(f32[64,512]{1,0:T(8,128)} %get-tuple-element.40), channel_id=1, source_target_pairs={{0,1},{1,0},{2,3},{3,2},{4,5},{5,4},{6,7},{7,6},{8,9},{9,8},{10,11... | collective-permute-start | bytes 393224 | tf_op jit(solution)/shard_map/ppermute | solution.py:414
  81.3 7.1 %collective-permute-start.4 = (bf16[64,768]{1,0:T(8,128)(2,1)}, bf16[64,768]{1,0:T(8,128)(2,1)S(1)}, u32[]{:S(2)}, u32[]{:S(2)}) collective-permute-start(bf16[64,768]{1,0:T(8,128)(2,1)} %get-tuple-element.39), channel_id=1, source_target_pairs={{4,0},{8,4},{12,8},{16,12},{20,16},{24,20},{28,24},{32,28},{36,32}... | collective-permute-start | bytes 294920 | tf_op jit(solution)/shard_map/ppermute | solution.py:383
  88.4 10.1 %copy-start.6 = (bf16[64,768]{1,0:T(8,128)(2,1)}, bf16[64,768]{1,0:T(8,128)(2,1)S(1)}, u32[]{:S(2)}) copy-start(bf16[64,768]{1,0:T(8,128)(2,1)S(1)} %collective-permute-done.4.below_ref) | copy-start | bytes 294916
  96.7 1.8 %copy-start.4 = (f32[64,512]{1,0:T(8,128)}, f32[64,512]{1,0:T(8,128)S(1)}, u32[]{:S(2)}) copy-start(f32[64,512]{1,0:T(8,128)S(1)} %collective-permute-done.5.side_ref) | copy-start | bytes 393220
  96.7 1.8 %copy-start.3 = (f32[64,768]{1,0:T(8,128)}, f32[64,768]{1,0:T(8,128)S(1)}, u32[]{:S(2)}) copy-start(f32[64,768]{1,0:T(8,128)S(1)} %collective-permute-done.3.above_ref) | copy-start | bytes 589828
  98.5 0.8 copy-start.1

commit v5 on v4

--- a/solution.py
+++ b/solution.py
@@ -152,6 +152,10 @@
 
 def whole(shape):
     return pl.BlockSpec(shape, lambda i: (0,) * len(shape))
+
+
+def on_core(value):
+    return pltpu.with_memory_space_constraint(value, pltpu.VMEM)
 
 
 def edges(pattern, left_flag, x, down_hop, right_hop):
@@ -231,33 +235,6 @@
     return jnp.sum(comps, axis=1) * (1.0 / 16.0)
 
 
-def near_kernel(
-    pattern_ref, left_ref, v0_ref, onsite_ref, down_ref, right_ref, above_ref, below_ref, side_ref,
-    pairing_ref, near_ref,
-):
-    is_left = left_ref[0] == 1
-    for tile in range(TR * TC):
-        cols = slice(tile * TILE, (tile + 1) * TILE)
-        hop = local_tile(pattern_ref, v0_ref, onsite_ref, down_ref, right_ref, tile)
-        halo = halo_tile(
-            pattern_ref, is_left, lambda k: down_ref[(TR - 1) * TC + k], lambda r: right_ref[r * TC + TC - 1],
-            above_ref, below_ref, side_ref, tile,
-        )
-        hop = hop if halo is None else hop + halo
-        near_ref[:, cols] = signed(hop) + pairing_ref[:, cols] * swapped(v0_ref[:, cols].astype(F32))
-
-
-def near(pattern, left_flag, v0, onsite, down_hop, right_hop, halo, pairing):
-    return pl.pallas_call(
-        near_kernel,
-        in_specs=[SMEM, SMEM] + [VMEM] * 8,
-        out_shape=jax.ShapeDtypeStruct((ROWS, SITES_DEV), F32),
-        compiler_params=params(),
-        cost_estimate=COST,
-        name="near",
-    )(pattern, left_flag, v0, onsite, down_hop, right_hop, *halo, pairing)
-
-
 SCATTER_SCRATCH = [pltpu.VMEM((HI * ROWS, 2 * SLOTS), BF16), pltpu.VMEM((HI * ROWS, SPAN), F32)]
 
 
@@ -277,42 +254,57 @@
         )
 
 
+def whole_hop(pattern_ref, left_ref, local_ref, total_ref, above_ref, below_ref, side_ref, down_ref, right_ref, tile):
+    h, part = divmod(tile, SPAN // TILE)
+    hop = local_ref[:, tile * TILE : (tile + 1) * TILE]
+    hop = hop + total_ref[h * ROWS : (h + 1) * ROWS, part * TILE : (part + 1) * TILE]
+    halo = halo_tile(
+        pattern_ref, left_ref[0] == 1, lambda k: down_ref[k], lambda r: right_ref[r, 0],
+        above_ref, below_ref, side_ref, tile,
+    )
+    return hop if halo is None else hop + halo
+
+
 def first_kernel(
-    pattern_ref, left_ref, v0_ref, landed_ref, hot_ref, high_ref, weight_ref, near_ref, down_ref, right_ref,
-    one_ref, x_ref, mom_ref, top_ref, below_ref, side_ref, out_ref, mask_ref, total_ref,
+    pattern_ref, left_ref, landed_ref, above_ref, below_ref, side_ref,
+    v0_ref, hot_ref, high_ref, weight_ref, local_ref, pairing_ref, down_ref, right_ref,
+    one_ref, x_ref, mom_ref, top_ref, lower_ref, beside_ref, out_ref, mask_ref, total_ref,
 ):
     scatter_into(landed_ref[left_ref[1]], hot_ref, high_ref, mask_ref, total_ref)
-    for h in range(HI):
-        cols = slice(h * SPAN, (h + 1) * SPAN)
+    for tile in range(TR * TC):
+        cols = slice(tile * TILE, (tile + 1) * TILE)
+        hop = whole_hop(
+            pattern_ref, left_ref, local_ref, total_ref, above_ref, below_ref, side_ref, down_ref, right_ref, tile
+        )
         v0 = v0_ref[:, cols].astype(F32)
-        one = near_ref[:, cols] + signed(total_ref[h * ROWS : (h + 1) * ROWS, :])
+        one = signed(hop) + pairing_ref[:, cols] * swapped(v0)
         one_ref[:, cols] = one
         x_ref[:, cols] = one.astype(BF16)
         mom_ref[0, :, cols] = vector_mean(v0 * v0)
         mom_ref[1, :, cols] = vector_mean(v0 * one)
     gather_payload(x_ref, hot_ref, high_ref, weight_ref, out_ref)
-    write_edges(pattern_ref, left_ref, x_ref, down_ref, right_ref, 0, top_ref, below_ref, side_ref)
-
-
-def first(pattern, left_flag, v0, landed, hot, high, weight, near_part, down_hop, right_hop):
+    write_edges(pattern_ref, left_ref, x_ref, down_ref, right_ref, 0, top_ref, lower_ref, beside_ref)
+
+
+def first(pattern, left_flag, v0, landed, tables, local_part, pairing, halo, down_hop, right_hop):
     shapes = (
         jax.ShapeDtypeStruct((ROWS, SITES_DEV), F32),
         jax.ShapeDtypeStruct((ROWS, SITES_DEV), BF16),
         jax.ShapeDtypeStruct((2, 4, SITES_DEV), F32),
     ) + EDGE_SHAPES + (jax.ShapeDtypeStruct((2, SLOTS, 2 * ROWS), BF16),)
+    resident = [on_core(a) for a in (landed, *halo)]
+    arrays = (v0, *tables, local_part, pairing)
     return pl.pallas_call(
         first_kernel,
         grid=(1,),
-        in_specs=[SMEM, SMEM]
-        + [whole(a.shape) for a in (v0, landed, hot, high, weight, near_part)]
-        + [DOWN_EDGE, RIGHT_EDGE],
+        in_specs=[SMEM, SMEM] + [VMEM] * 4 + [whole(a.shape) for a in arrays] + [DOWN_EDGE, RIGHT_EDGE],
         out_specs=tuple(whole(s.shape) for s in shapes),
         out_shape=shapes,
         scratch_shapes=SCATTER_SCRATCH,
         compiler_params=params(),
         cost_estimate=COST,
         name="first",
-    )(pattern, left_flag, v0, landed, hot, high, weight, near_part, down_hop, right_hop.reshape(TR, TC, TILE, TILE))
+    )(pattern, left_flag, *resident, *arrays, down_hop, right_hop.reshape(TR, TC, TILE, TILE))
 
 
 def local_kernel(pattern_ref, x_ref, onsite_ref, down_ref, right_ref, out_ref):
@@ -334,21 +326,17 @@
 
 
 def second_kernel(
-    pattern_ref, left_ref, v0_ref, one_ref, landed_ref, hot_ref, high_ref, local_ref, pairing_ref, mom_in_ref,
-    above_ref, below_ref, side_ref, down_ref, right_ref, two_ref, mom_ref, mask_ref, total_ref,
+    pattern_ref, left_ref, landed_ref, above_ref, below_ref, side_ref,
+    v0_ref, one_ref, hot_ref, high_ref, local_ref, pairing_ref, mom_in_ref, down_ref, right_ref,
+    two_ref, mom_ref, mask_ref, total_ref,
 ):
     scatter_into(landed_ref[left_ref[1]], hot_ref, high_ref, mask_ref, total_ref)
-    is_left = left_ref[0] == 1
     mom_ref[0:2] = mom_in_ref[...]
     for tile in range(TR * TC):
         cols = slice(tile * TILE, (tile + 1) * TILE)
-        h, part = divmod(tile, SPAN // TILE)
-        hop = local_ref[:, cols] + total_ref[h * ROWS : (h + 1) * ROWS, part * TILE : (part + 1) * TILE]
-        halo = halo_tile(
-            pattern_ref, is_left, lambda k: down_ref[k], lambda r: right_ref[r, 0],
-            above_ref, below_ref, side_ref, tile,
-        )
-        hop = hop if halo is None else hop + halo
+        hop = whole_hop(
+            pattern_ref, left_ref, local_ref, total_ref, above_ref, below_ref, side_ref, down_ref, right_ref, tile
+        )
         v0 = v0_ref[:, cols].astype(F32)
         two = 2.0 * (signed(hop) + pairing_ref[:, cols] * swapped(one_ref[:, cols])) - v0
         two_ref[:, cols] = two
@@ -360,18 +348,19 @@
         jax.ShapeDtypeStruct((ROWS, SITES_DEV), F32),
         jax.ShapeDtypeStruct((3, 4, SITES_DEV), F32),
     )
-    arrays = (v0, one, landed, hot, high, local_part, pairing, mom) + tuple(halo)
+    resident = [on_core(a) for a in (landed, *halo)]
+    arrays = (v0, one, hot, high, local_part, pairing, mom)
     return pl.pallas_call(
         second_kernel,
         grid=(1,),
-        in_specs=[SMEM, SMEM] + [whole(a.shape) for a in arrays] + [DOWN_EDGE, RIGHT_EDGE],
+        in_specs=[SMEM, SMEM] + [VMEM] * 4 + [whole(a.shape) for a in arrays] + [DOWN_EDGE, RIGHT_EDGE],
         out_specs=tuple(whole(s.shape) for s in shapes),
         out_shape=shapes,
         scratch_shapes=SCATTER_SCRATCH,
         compiler_params=params(),
         cost_estimate=COST,
         name="second",
-    )(pattern, left_flag, *arrays, down_hop, right_hop.reshape(TR, TC, TILE, TILE))
+    )(pattern, left_flag, *resident, *arrays, down_hop, right_hop.reshape(TR, TC, TILE, TILE))
 
 
 TILE_AXES = ("z_low", "y", "x", "core")
@@ -414,13 +403,14 @@
             lax.ppermute(side_part, "side", [(0, 1), (1, 0)]),
         )
 
-    hot, high, weight, payload = prepare(v0, link_rows, link_target, link_weight, link_count)
+    *tables, payload = prepare(v0, link_rows, link_target, link_weight, link_count)
+    hot, high, weight = tables
     spread = spread_out(payload)
     halo = halo_of(*edges(pattern, left_flag, v0, down_hop, right_hop))
-    near_part = near(pattern, left_flag, v0, onsite, down_hop, right_hop, halo, pairing)
-    landed, near_part = lax.optimization_barrier((spread, near_part))
+    local_part = local(pattern, v0, onsite, down_hop, right_hop)
+    landed, local_part, halo = lax.optimization_barrier((spread, local_part, halo))
     one, x, mom, *edge_parts, payload = first(
-        pattern, left_flag, v0, landed, hot, high, weight, near_part, down_hop, right_hop
+        pattern, left_flag, v0, landed, tables, local_part, pairing, halo, down_hop, right_hop
     )
     spread = spread_out(payload)
     halo = halo_of(*edge_parts)

time: 105 us -> 98.2 us (0.935)
  waiting for transfers between devices: 22 us -> 19.2 us
  local copies, waits for them, and re-layouts: 2.31 us -> 0 us
    pallas_call x3 -> x2, Pallas kernels: 15.3 us -> 11.3 us  [the longest x1 6.64 us: first(): pl.pallas_call(first_kernel, grid=(1,), in_specs=[SMEM, SMEM] + [VMEM] *...]
    pallas_call x1 -> x2, Pallas kernels: 3.55 us -> 7.09 us  [local(): pl.pallas_call(local_kernel, in_specs=[SMEM] + [VMEM] * 4, out_shape=jax....]
    ppermute x4, waiting for transfers between devices: 6.38 us -> 2.85 us  [passed_along(): return lax.ppermute(value, TILE_AXES, pairs)]
    unnamed x16 -> x0, local copies, waits for them, and re-layouts: 2.31 us -> none
  transfers between devices with their start and end apart: 8 -> 8, of which waited for: 5 -> 6; matrix products, arithmetic and copies ran while one was open for 1% -> 1% of each run, Pallas kernels for 9% -> 9%
where the time goes in v5:
time: 98.2 us; the launch traced here: 97.7 us
  starting transfers between devices  52.7 us (54%)
  Pallas kernels  24.4 us (25%)
  waiting for transfers between devices  19.2 us (20%)
    all_to_all x2, starting transfers between devices, spread_out(): lax.all_to_all(payload.reshape(2 * PEERS, CAP, 2 * ROWS), ('sheet',) + TI...  35.5 us
    ppermute x2, waiting for transfers between devices, halo_of(): lax.ppermute(side_part, 'side', [(0, 1), (1, 0)])  13.8 us
    ppermute x4, starting transfers between devices, passed_along(): return lax.ppermute(value, TILE_AXES, pairs)  10.9 us
    pallas_call x2, Pallas kernels, local(): pl.pallas_call(local_kernel, in_specs=[SMEM] + [VMEM] * 4, out_shape=jax....  7.09 us
    pallas_call x1, Pallas kernels, first(): pl.pallas_call(first_kernel, grid=(1,), in_specs=[SMEM, SMEM] + [VMEM] *...  6.64 us
    ppermute x2, starting transfers between devices, halo_of(): lax.ppermute(side_part, 'side', [(0, 1), (1, 0)])  6.34 us
    pallas_call x1, Pallas kernels, second(): pl.pallas_call(second_kernel, grid=(1,), in_specs=[SMEM, SMEM] + [VMEM] *...  4.64 us
    pallas_call x1, Pallas kernels, prepare(): pl.pallas_call(prepare_kernel, out_shape=TABLE_SHAPES + (jax.ShapeDtypeSt...  4.04 us
  transfers between devices with their start and end apart: 8, of which 6 were waited for; matrix products, arithmetic and copies ran while one was open for 1% of the time, Pallas kernels for 9%

profile of v5, /device:TPU:1, one launch (start us, length us, event | category | flops | bytes accessed | tf_op | source)
XLA Modules:
  0.0 97.7 jit_solution(926716608694765708)
XLA Ops:
  0.6 4.0 %prepare.1 = (bf16[3072,256]{1,0:T(8,128)(2,1)}, f32[2048,128]{1,0:T(8,128)}, f32[1024,128]{1,0:T(8,128)}, bf16[2,1024,128]{2,1,0:T(8,128)(2,1)}) custom-call(bf16[64,3072]{1,0:T(8,128)(2,1)} %bitcast.21, s32[8,128]{1,0:T(8,128)} %bitcast.36, s32[8,128]{1,0:T(8,128)} %bitcast.37, bf16[8,128]{1,0:T(8,128)(2,1)} %bitcast.38, s32[1,128]{1,0:T(1,128)} %bitcast.39), custom_call_target="tpu_custom_call" | custom-call | flops 1000000 | bytes 100000 | tf_op jit(solution)/shard_map/prepare/pallas_call | solution.py:112
  4.7 22.4 %all-to-all-start = ((bf16[256,8,128]{2,1,0:T(8,128)(2,1)}), bf16[256,8,128]{2,1,0:T(8,128)(2,1)S(1)}, u32[]{:S(2)}, u32[]{:S(2)}) async-start(bf16[256,8,128]{2,1,0:T(8,128)(2,1)} %bitcast.27), calls=%async_computation | async-start | bytes 1048576 | tf_op jit(solution)/shard_map/all_to_all | solution.py:376
  27.1 0.6 pad_add_fusion.left_ref
  27.7 2.0 %edges.1 = (bf16[64,768]{1,0:T(8,128)(2,1)}, f32[64,768]{1,0:T(8,128)}, f32[64,512]{1,0:T(8,128)}) custom-call(s32[2,24]{1,0:T(2,128)} %bitcast.31, s32[2]{0:T(128)} %pad_add_fusion.left_ref, bf16[64,3072]{1,0:T(8,128)(2,1)} %bitcast.22, bf16[24,128,128]{2,1,0:T(8,128)(2,1)} %down_ref.9, bf16[4,6,128,128]{3,2,1,0:T(8,128)(2,1)} %bitcast.18), custom_call_target="tpu_custom_call" | custom-call | flops 1000000 | bytes 100000 | tf_op jit(solution)/shard_map/edges/pallas_call | solution.py:162
  29.7 3.5 %collective-permute-start = (f32[64,768]{1,0:T(8,128)}, f32[64,768]{1,0:T(8,128)S(1)}, u32[]{:S(2)}, u32[]{:S(2)}) collective-permute-start(f32[64,768]{1,0:T(8,128)} %get-tuple-element.30), channel_id=1, source_target_pairs={{0,4},{4,8},{8,12},{12,16},{16,20},{20,24},{24,28},{28,32},{32,36}... | collective-permute-start | bytes 589832 | tf_op jit(solution)/shard_map/ppermute | solution.py:372
  33.2 4.0 %collective-permute-start.2 = (f32[64,512]{1,0:T(8,128)}, f32[64,512]{1,0:T(8,128)S(1)}, u32[]{:S(2)}, u32[]{:S(2)}) collective-permute-start(f32[64,512]{1,0:T(8,128)} %get-tuple-element.32), channel_id=1, source_target_pairs={{0,1},{1,0},{2,3},{3,2},{4,5},{5,4},{6,7},{7,6},{8,9},{9,8},{10,11... | collective-permute-start | bytes 393224 | tf_op jit(solution)/shard_map/ppermute | solution.py:403
  37.3 1.9 %collective-permute-start.1 = (bf16[64,768]{1,0:T(8,128)(2,1)}, bf16[64,768]{1,0:T(8,128)(2,1)S(1)}, u32[]{:S(2)}, u32[]{:S(2)}) collective-permute-start(bf16[64,768]{1,0:T(8,128)(2,1)} %get-tuple-element.31), channel_id=1, source_target_pairs={{4,0},{8,4},{12,8},{16,12},{20,16},{24,20},{28,24},{32,28},{36,32}... | collective-permute-start | bytes 294920 | tf_op jit(solution)/shard_map/ppermute | solution.py:372
  39.2 3.5 %local.2.local_ref = f32[64,3072]{1,0:T(8,128)} custom-call(s32[2,24]{1,0:T(2,128)} %bitcast.32, bf16[64,3072]{1,0:T(8,128)(2,1)} %bitcast.23, bf16[24,128,128]{2,1,0:T(8,128)(2,1)} %onsite_ref.3, bf16[24,128,128]{2,1,0:T(8,128)(2,1)} %down_ref.9, bf16[24,128,128]{2,1,0:T(8,128)(2,1)} %right_ref.3), custom_call_target="tpu_custom_call" | custom-call | flops 1000000 | bytes 100000 | tf_op jit(solution)/shard_map/local/pallas_call | solution.py:318
  42.7 1.2 %collective-permute-done.1.below_ref = bf16[64,768]{1,0:T(8,128)(2,1)S(1)} collective-permute-done((bf16[64,768]{1,0:T(8,128)(2,1)}, bf16[64,768]{1,0:T(8,128)(2,1)S(1)}, u32[]{:S(2)}, u32[]{:S(2)}) %collective-permute-start.1) | collective-permute-done | bytes 98336 | tf_op jit(solution)/shard_map/ppermute | solution.py:372
  43.9 5.6 %collective-permute-done.2.side_ref = f32[64,512]{1,0:T(8,128)S(1)} collective-permute-done((f32[64,512]{1,0:T(8,128)}, f32[64,512]{1,0:T(8,128)S(1)}, u32[]{:S(2)}, u32[]{:S(2)}) %collective-permute-start.2) | collective-permute-done | bytes 131104 | tf_op jit(solution)/shard_map/ppermute | solution.py:403
  49.5 0.0 collective-permute-done.above_ref
  49.5 0.7 all-to-all-done
  50.2 6.6 %first.1 = (f32[64,3072]{1,0:T(8,128)}, bf16[64,3072]{1,0:T(8,128)(2,1)}, f32[2,4,3072]{2,1,0:T(4,128)}, bf16[64,768]{1,0:T(8,128)(2,1)}, f32[64,768]{1,0:T(8,12...) custom-call(s32[2,24]{1,0:T(2,128)} %bitcast.33, s32[2]{0:T(128)} %pad_add_fusion.left_ref, ...), custom_call_target="tpu_custom_call" | custom-call | flops 1000000 | bytes 100000 | tf_op jit(solution)/shard_map/first/pallas_call | solution.py:297
  56.9 13.1 %all-to-all-start.1 = ((bf16[256,8,128]{2,1,0:T(8,128)(2,1)}), bf16[256,8,128]{2,1,0:T(8,128)(2,1)S(1)}, u32[]{:S(2)}, u32[]{:S(2)}) async-start(bf16[256,8,128]{2,1,0:T(8,128)(2,1)} %bitcast.28), calls=%async_computation.1 | async-start | bytes 1048576 | tf_op jit(solution)/shard_map/all_to_all | solution.py:376
  70.0 3.5 %collective-permute-start.3 = (f32[64,768]{1,0:T(8,128)}, f32[64,768]{1,0:T(8,128)S(1)}, u32[]{:S(2)}, u32[]{:S(2)}) collective-permute-start(f32[64,768]{1,0:T(8,128)} %get-tuple-element.44), channel_id=1, source_target_pairs={{0,4},{4,8},{8,12},{12,16},{16,20},{20,24},{24,28},{28,32},{32,36}... | collective-permute-start | bytes 589832 | tf_op jit(solution)/shard_map/ppermute | solution.py:372
  73.5 2.3 %collective-permute-start.5 = (f32[64,512]{1,0:T(8,128)}, f32[64,512]{1,0:T(8,128)S(1)}, u32[]{:S(2)}, u32[]{:S(2)}) collective-permute-start(f32[64,512]{1,0:T(8,128)} %get-tuple-element.46), channel_id=1, source_target_pairs={{0,1},{1,0},{2,3},{3,2},{4,5},{5,4},{6,7},{7,6},{8,9},{9,8},{10,11... | collective-permute-start | bytes 393224 | tf_op jit(solution)/shard_map/ppermute | solution.py:403
  75.9 1.9 %collective-permute-start.4 = (bf16[64,768]{1,0:T(8,128)(2,1)}, bf16[64,768]{1,0:T(8,128)(2,1)S(1)}, u32[]{:S(2)}, u32[]{:S(2)}) collective-permute-start(bf16[64,768]{1,0:T(8,128)(2,1)} %get-tuple-element.45), channel_id=1, source_target_pairs={{4,0},{8,4},{12,8},{16,12},{20,16},{24,20},{28,24},{32,28},{36,32}... | collective-permute-start | bytes 294920 | tf_op jit(solution)/shard_map/ppermute | solution.py:372
  77.8 3.5 %local.3.local_ref = f32[64,3072]{1,0:T(8,128)} custom-call(s32[2,24]{1,0:T(2,128)} %bitcast.34, bf16[64,3072]{1,0:T(8,128)(2,1)} %get-tuple-element.43.x_ref, bf16[24,128,128]{2,1,0:T(8,128)(2,1)} %onsite_ref.3, bf16[24,128,128]{2,1,0:T(8,128)(2,1)} %down_ref.9, bf16[24,128,128]{2,1,0:T(8,128)(2,1)} %right_ref.3), custom_call_target="tpu_custom_call" | custom-call | flops 1000000 | bytes 100000 | tf_op jit(solution)/shard_map/local/pallas_call | solution.py:318
  81.3 1.6 %collective-permute-done.4.below_ref = bf16[64,768]{1,0:T(8,128)(2,1)S(1)} collective-permute-done((bf16[64,768]{1,0:T(8,128)(2,1)}, bf16[64,768]{1,0:T(8,128)(2,1)S(1)}, u32[]{:S(2)}, u32[]{:S(2)}) %collective-permute-start.4) | collective-permute-done | bytes 98336 | tf_op jit(solution)/shard_map/ppermute | solution.py:372
  83.0 8.2 %collective-permute-done.5.side_ref = f32[64,512]{1,0:T(8,128)S(1)} collective-permute-done((f32[64,512]{1,0:T(8,128)}, f32[64,512]{1,0:T(8,128)S(1)}, u32[]{:S(2)}, u32[]{:S(2)}) %collective-permute-start.5) | collective-permute-done | bytes 131104 | tf_op jit(solution)/shard_map/ppermute | solution.py:403
  91.2 0.0 collective-permute-done.3.above_ref
  91.2 1.8 %all-to-all-done.1 = bf16[256,8,128]{2,1,0:T(8,128)(2,1)S(1)} async-done(((bf16[256,8,128]{2,1,0:T(8,128)(2,1)}), bf16[256,8,128]{2,1,0:T(8,128)(2,1)S(1)}, u32[]{:S(2)}, u32[]{:S(2)}) %all-to-all-start.1) | async-done | bytes 524320 | tf_op jit(solution)/shard_map/all_to_all | solution.py:376
  93.1 4.6 %second.1 = (f32[64,3072]{1,0:T(8,128)}, f32[3,4,3072]{2,1,0:T(4,128)}) custom-call(s32[2,24]{1,0:T(2,128)} %bitcast.35, s32[2]{0:T(128)} %pad_add_fusion.left_ref, bf16[2,1024,128]{2,1,0:T(8,128)(2,1)S(1)} %bitcast.17, f32[64,768]{1,0:T(8,128)S(1)} %collective-permute-done.3.above_ref, bf16[64,768]{1,0:T(8,128)(2,1)S(1)} %collective-permute-done.4.below_ref, ...), custom_call_target="tpu_custom_call" | custom-call | flops 1000000 | bytes 100000 | tf_op jit(solution)/shard_map/second/pallas_call | solution.py:353
Async XLA Ops:
  4.7 45.6 %all-to-all-start = ((bf16[256,8,128]{2,1,0:T(8,128)(2,1)}), bf16[256,8,128]{2,1,0:T(8,128)(2,1)S(1)}, u32[]{:S(2)}, u32[]{:S(2)}) async-start(bf16[256,8,128]{2,1,0:T(8,128)(2,1)} %bitcast.27), calls=%async_computation | async-start | bytes 1048576 | tf_op jit(solution)/shard_map/all_to_all | solution.py:376
  29.7 19.8 %collective-permute-start = (f32[64,768]{1,0:T(8,128)}, f32[64,768]{1,0:T(8,128)S(1)}, u32[]{:S(2)}, u32[]{:S(2)}) collective-permute-start(f32[64,768]{1,0:T(8,128)} %get-tuple-element.30), channel_id=1, source_target_pairs={{0,4},{4,8},{8,12},{12,16},{16,20},{20,24},{24,28},{28,32},{32,36}... | collective-permute-start | bytes 589832 | tf_op jit(solution)/shard_map/ppermute | solution.py:372
  33.2 16.3 %collective-permute-start.2 = (f32[64,512]{1,0:T(8,128)}, f32[64,512]{1,0:T(8,128)S(1)}, u32[]{:S(2)}, u32[]{:S(2)}) collective-permute-start(f32[64,512]{1,0:T(8,128)} %get-tuple-element.32), channel_id=1, source_target_pairs={{0,1},{1,0},{2,3},{3,2},{4,5},{5,4},{6,7},{7,6},{8,9},{9,8},{10,11... | collective-permute-start | bytes 393224 | tf_op jit(solution)/shard_map/ppermute | solution.py:403
  37.3 6.7 %collective-permute-start.1 = (bf16[64,768]{1,0:T(8,128)(2,1)}, bf16[64,768]{1,0:T(8,128)(2,1)S(1)}, u32[]{:S(2)}, u32[]{:S(2)}) collective-permute-start(bf16[64,768]{1,0:T(8,128)(2,1)} %get-tuple-element.31), channel_id=1, source_target_pairs={{4,0},{8,4},{12,8},{16,12},{20,16},{24,20},{28,24},{32,28},{36,32}... | collective-permute-start | bytes 294920 | tf_op jit(solution)/shard_map/ppermute | solution.py:372
  56.9 36.2 %all-to-all-start.1 = ((bf16[256,8,128]{2,1,0:T(8,128)(2,1)}), bf16[256,8,128]{2,1,0:T(8,128)(2,1)S(1)}, u32[]{:S(2)}, u32[]{:S(2)}) async-start(bf16[256,8,128]{2,1,0:T(8,128)(2,1)} %bitcast.28), calls=%async_computation.1 | async-start | bytes 1048576 | tf_op jit(solution)/shard_map/all_to_all | solution.py:376
  70.0 21.2 %collective-permute-start.3 = (f32[64,768]{1,0:T(8,128)}, f32[64,768]{1,0:T(8,128)S(1)}, u32[]{:S(2)}, u32[]{:S(2)}) collective-permute-start(f32[64,768]{1,0:T(8,128)} %get-tuple-element.44), channel_id=1, source_target_pairs={{0,4},{4,8},{8,12},{12,16},{16,20},{20,24},{24,28},{28,32},{32,36}... | collective-permute-start | bytes 589832 | tf_op jit(solution)/shard_map/ppermute | solution.py:372
  73.5 17.7 %collective-permute-start.5 = (f32[64,512]{1,0:T(8,128)}, f32[64,512]{1,0:T(8,128)S(1)}, u32[]{:S(2)}, u32[]{:S(2)}) collective-permute-start(f32[64,512]{1,0:T(8,128)} %get-tuple-element.46), channel_id=1, source_target_pairs={{0,1},{1,0},{2,3},{3,2},{4,5},{5,4},{6,7},{7,6},{8,9},{9,8},{10,11... | collective-permute-start | bytes 393224 | tf_op jit(solution)/shard_map/ppermute | solution.py:403
  75.9 7.1 %collective-permute-start.4 = (bf16[64,768]{1,0:T(8,128)(2,1)}, bf16[64,768]{1,0:T(8,128)(2,1)S(1)}, u32[]{:S(2)}, u32[]{:S(2)}) collective-permute-start(bf16[64,768]{1,0:T(8,128)(2,1)} %get-tuple-element.45), channel_id=1, source_target_pairs={{4,0},{8,4},{12,8},{16,12},{20,16},{24,20},{28,24},{32,28},{36,32}... | collective-permute-start | bytes 294920 | tf_op jit(solution)/shard_map/ppermute | solution.py:372

commit v6 on v5

--- a/solution.py
+++ b/solution.py
@@ -102,8 +102,8 @@
 
 
 TABLE_SHAPES = (
-    jax.ShapeDtypeStruct((3 * SLOTS, SPAN), BF16),
-    jax.ShapeDtypeStruct((2 * SLOTS, TILE), F32),
+    pltpu.VMEM((3 * SLOTS, SPAN), BF16),
+    pltpu.VMEM((2 * SLOTS, TILE), F32),
     jax.ShapeDtypeStruct((SLOTS, TILE), F32),
 )
 
@@ -123,16 +123,15 @@
     for k in range(TC):
         tile = (TR - 1) * TC + k
         keep = pattern_ref[0, tile].astype(F32)
-        below_ref[:, k * TILE : (k + 1) * TILE] = keep * dot(
-            x_ref[:, tile * TILE : (tile + 1) * TILE], down_ref[down_base + k]
-        )
+        product = keep * dot(x_ref[:, tile * TILE : (tile + 1) * TILE], down_ref[down_base + k])
+        below_ref[:, k * TILE : (k + 1) * TILE] = product.astype(BF16)
     is_left = left_ref[0] == 1
     for r in range(TR):
         last = r * TC + TC - 1
         keep = pattern_ref[1, last].astype(F32)
         product = keep * dot(x_ref[:, last * TILE : (last + 1) * TILE], right_ref[r, 0])
-        first_tile = x_ref[:, r * TC * TILE : (r * TC + 1) * TILE].astype(F32)
-        side_ref[:, r * TILE : (r + 1) * TILE] = jnp.where(is_left, product, first_tile)
+        first_tile = x_ref[:, r * TC * TILE : (r * TC + 1) * TILE]
+        side_ref[:, r * TILE : (r + 1) * TILE] = jnp.where(is_left, product.astype(BF16), first_tile)
 
 
 def edges_kernel(pattern_ref, left_ref, x_ref, down_ref, right_ref, top_ref, below_ref, side_ref):
@@ -141,8 +140,8 @@
 
 EDGE_SHAPES = (
     jax.ShapeDtypeStruct((ROWS, TC * TILE), BF16),
-    jax.ShapeDtypeStruct((ROWS, TC * TILE), F32),
-    jax.ShapeDtypeStruct((ROWS, TR * TILE), F32),
+    jax.ShapeDtypeStruct((ROWS, TC * TILE), BF16),
+    jax.ShapeDtypeStruct((ROWS, TR * TILE), BF16),
 )
 SMEM = pl.BlockSpec(memory_space=pltpu.SMEM)
 VMEM = pl.BlockSpec(memory_space=pltpu.VMEM)
@@ -210,14 +209,15 @@
         return value if total is None else total + value
 
     if r == 0:
-        total = plus(above_ref[:, k * TILE : (k + 1) * TILE])
+        total = plus(above_ref[:, k * TILE : (k + 1) * TILE].astype(F32))
     if r == TR - 1:
         lower = below_ref[:, k * TILE : (k + 1) * TILE]
         total = plus(dot(kept(pattern_ref, 0, tile, lower), down_edge(k), NT))
     if k == 0:
-        total = plus(jnp.where(is_left, 0.0, side_ref[:, r * TILE : (r + 1) * TILE]))
+        total = plus(jnp.where(is_left, 0.0, side_ref[:, r * TILE : (r + 1) * TILE].astype(F32)))
     if k == TC - 1:
-        righter = jnp.where(is_left, side_ref[:, r * TILE : (r + 1) * TILE], 0.0).astype(BF16)
+        righter = side_ref[:, r * TILE : (r + 1) * TILE]
+        righter = jnp.where(is_left, righter, jnp.zeros_like(righter))
         total = plus(dot(kept(pattern_ref, 1, tile, righter), right_edge(r), NT))
     return total
 
@@ -266,8 +266,8 @@
 
 
 def first_kernel(
-    pattern_ref, left_ref, landed_ref, above_ref, below_ref, side_ref,
-    v0_ref, hot_ref, high_ref, weight_ref, local_ref, pairing_ref, down_ref, right_ref,
+    pattern_ref, left_ref, landed_ref, above_ref, below_ref, side_ref, hot_ref, high_ref,
+    v0_ref, weight_ref, local_ref, pairing_ref, down_ref, right_ref,
     one_ref, x_ref, mom_ref, top_ref, lower_ref, beside_ref, out_ref, mask_ref, total_ref,
 ):
     scatter_into(landed_ref[left_ref[1]], hot_ref, high_ref, mask_ref, total_ref)
@@ -292,12 +292,13 @@
         jax.ShapeDtypeStruct((ROWS, SITES_DEV), BF16),
         jax.ShapeDtypeStruct((2, 4, SITES_DEV), F32),
     ) + EDGE_SHAPES + (jax.ShapeDtypeStruct((2, SLOTS, 2 * ROWS), BF16),)
-    resident = [on_core(a) for a in (landed, *halo)]
-    arrays = (v0, *tables, local_part, pairing)
+    hot, high, weight = tables
+    resident = [on_core(a) for a in (landed, *halo, hot, high)]
+    arrays = (v0, weight, local_part, pairing)
     return pl.pallas_call(
         first_kernel,
         grid=(1,),
-        in_specs=[SMEM, SMEM] + [VMEM] * 4 + [whole(a.shape) for a in arrays] + [DOWN_EDGE, RIGHT_EDGE],
+        in_specs=[SMEM, SMEM] + [VMEM] * len(resident) + [whole(a.shape) for a in arrays] + [DOWN_EDGE, RIGHT_EDGE],
         out_specs=tuple(whole(s.shape) for s in shapes),
         out_shape=shapes,
         scratch_shapes=SCATTER_SCRATCH,
@@ -326,8 +327,8 @@
 
 
 def second_kernel(
-    pattern_ref, left_ref, landed_ref, above_ref, below_ref, side_ref,
-    v0_ref, one_ref, hot_ref, high_ref, local_ref, pairing_ref, mom_in_ref, down_ref, right_ref,
+    pattern_ref, left_ref, landed_ref, above_ref, below_ref, side_ref, hot_ref, high_ref,
+    v0_ref, one_ref, local_ref, pairing_ref, mom_in_ref, down_ref, right_ref,
     two_ref, mom_ref, mask_ref, total_ref,
 ):
     scatter_into(landed_ref[left_ref[1]], hot_ref, high_ref, mask_ref, total_ref)
@@ -348,12 +349,12 @@
         jax.ShapeDtypeStruct((ROWS, SITES_DEV), F32),
         jax.ShapeDtypeStruct((3, 4, SITES_DEV), F32),
     )
-    resident = [on_core(a) for a in (landed, *halo)]
-    arrays = (v0, one, hot, high, local_part, pairing, mom)
+    resident = [on_core(a) for a in (landed, *halo, hot, high)]
+    arrays = (v0, one, local_part, pairing, mom)
     return pl.pallas_call(
         second_kernel,
         grid=(1,),
-        in_specs=[SMEM, SMEM] + [VMEM] * 4 + [whole(a.shape) for a in arrays] + [DOWN_EDGE, RIGHT_EDGE],
+        in_specs=[SMEM, SMEM] + [VMEM] * len(resident) + [whole(a.shape) for a in arrays] + [DOWN_EDGE, RIGHT_EDGE],
         out_specs=tuple(whole(s.shape) for s in shapes),
         out_shape=shapes,
         scratch_shapes=SCATTER_SCRATCH,

time: 98.2 us -> 95 us (0.967)
  waiting for transfers between devices: 19.2 us -> 16.9 us
  Pallas kernels: 24.4 us -> 22.7 us
    all_to_all x2, waiting for transfers between devices: 2.56 us -> 8.09 us  [spread_out(): lax.all_to_all(payload.reshape(2 * PEERS, CAP, 2 * ROWS), ('sheet',) + TI...]
    ppermute x2, waiting for transfers between devices: 13.8 us -> 8.81 us  [halo_of(): lax.ppermute(side_part, 'side', [(0, 1), (1, 0)])]
    ppermute x4, waiting for transfers between devices: 2.85 us -> 0.01 us  [passed_along(): return lax.ppermute(value, TILE_AXES, pairs)]
    ppermute x2, starting transfers between devices: 6.34 us -> 7.55 us  [halo_of(): lax.ppermute(side_part, 'side', [(0, 1), (1, 0)])]
  transfers between devices with their start and end apart: 8 -> 8, of which waited for: 6 -> 4; matrix products, arithmetic and copies ran while one was open for 1% -> 1% of each run, Pallas kernels for 9% -> 10%
where the time goes in v6:
time: 95 us; the launch traced here: 94.4 us
  starting transfers between devices  53.5 us (56%)
  Pallas kernels  22.7 us (24%)
  waiting for transfers between devices  16.9 us (18%)
    all_to_all x2, starting transfers between devices, spread_out(): lax.all_to_all(payload.reshape(2 * PEERS, CAP, 2 * ROWS), ('sheet',) + TI...  35 us
    ppermute x4, starting transfers between devices, passed_along(): return lax.ppermute(value, TILE_AXES, pairs)  10.9 us
    ppermute x2, waiting for transfers between devices, halo_of(): lax.ppermute(side_part, 'side', [(0, 1), (1, 0)])  8.81 us
    all_to_all x2, waiting for transfers between devices, spread_out(): lax.all_to_all(payload.reshape(2 * PEERS, CAP, 2 * ROWS), ('sheet',) + TI...  8.09 us
    ppermute x2, starting transfers between devices, halo_of(): lax.ppermute(side_part, 'side', [(0, 1), (1, 0)])  7.55 us
    pallas_call x2, Pallas kernels, local(): pl.pallas_call(local_kernel, in_specs=[SMEM] + [VMEM] * 4, out_shape=jax....  7.11 us
    pallas_call x1, Pallas kernels, first(): pl.pallas_call(first_kernel, grid=(1,), in_specs=[SMEM, SMEM] + [VMEM] *...  5.77 us
    pallas_call x1, Pallas kernels, prepare(): pl.pallas_call(prepare_kernel, out_shape=TABLE_SHAPES + (jax.ShapeDtypeSt...  4.04 us
  transfers between devices with their start and end apart: 8, of which 4 were waited for; matrix products, arithmetic and copies ran while one was open for 1% of the time, Pallas kernels for 10%

profile of v6, /device:TPU:1, one launch (start us, length us, event | category | flops | bytes accessed | tf_op | source)
XLA Modules:
  0.0 94.4 jit_solution(5174083388708894935)
XLA Ops:
  0.6 4.0 %prepare.1 = (bf16[3072,256]{1,0:T(8,128)(2,1)S(1)}, f32[2048,128]{1,0:T(8,128)S(1)}, f32[1024,128]{1,0:T(8,128)}, bf16[2,1024,128]{2,1,0:T(8,128)(2,1)}) custom-call(bf16[64,3072]{1,0:T(8,128)(2,1)} %bitcast.21, s32[8,128]{1,0:T(8,128)} %bitcast.36, s32[8,128]{1,0:T(8,128)} %bitcast.37, bf16[8,128]{1,0:T(8,128)(2,1)} %bitcast.38, s32[1,128]{1,0:T(1,128)} %bitcast.39), custom_call_target="tpu_custom_call" | custom-call | flops 1000000 | bytes 100000 | tf_op jit(solution)/shard_map/prepare/pallas_call | solution.py:112
  4.7 22.4 %all-to-all-start = ((bf16[256,8,128]{2,1,0:T(8,128)(2,1)}), bf16[256,8,128]{2,1,0:T(8,128)(2,1)S(1)}, u32[]{:S(2)}, u32[]{:S(2)}) async-start(bf16[256,8,128]{2,1,0:T(8,128)(2,1)} %bitcast.27), calls=%async_computation | async-start | bytes 1048576 | tf_op jit(solution)/shard_map/all_to_all | solution.py:377
  27.1 0.6 pad_add_fusion.left_ref
  27.6 2.0 %edges.1 = (bf16[64,768]{1,0:T(8,128)(2,1)}, bf16[64,768]{1,0:T(8,128)(2,1)}, bf16[64,512]{1,0:T(8,128)(2,1)}) custom-call(s32[2,24]{1,0:T(2,128)} %bitcast.31, s32[2]{0:T(128)} %pad_add_fusion.left_ref, bf16[64,3072]{1,0:T(8,128)(2,1)} %bitcast.22, bf16[24,128,128]{2,1,0:T(8,128)(2,1)} %down_ref.9, bf16[4,6,128,128]{3,2,1,0:T(8,128)(2,1)} %bitcast.18), custom_call_target="tpu_custom_call" | custom-call | flops 1000000 | bytes 100000 | tf_op jit(solution)/shard_map/edges/pallas_call | solution.py:161
  29.6 3.5 %collective-permute-start = (bf16[64,768]{1,0:T(8,128)(2,1)}, bf16[64,768]{1,0:T(8,128)(2,1)S(1)}, u32[]{:S(2)}, u32[]{:S(2)}) collective-permute-start(bf16[64,768]{1,0:T(8,128)(2,1)} %get-tuple-element.30), channel_id=1, source_target_pairs={{0,4},{4,8},{8,12},{12,16},{16,20},{20,24},{24,28},{28,32},{32,36}... | collective-permute-start | bytes 294920 | tf_op jit(solution)/shard_map/ppermute | solution.py:373
  33.1 1.9 %collective-permute-start.1 = (bf16[64,768]{1,0:T(8,128)(2,1)}, bf16[64,768]{1,0:T(8,128)(2,1)S(1)}, u32[]{:S(2)}, u32[]{:S(2)}) collective-permute-start(bf16[64,768]{1,0:T(8,128)(2,1)} %get-tuple-element.31), channel_id=1, source_target_pairs={{4,0},{8,4},{12,8},{16,12},{20,16},{24,20},{28,24},{32,28},{36,32}... | collective-permute-start | bytes 294920 | tf_op jit(solution)/shard_map/ppermute | solution.py:373
  35.1 4.0 %collective-permute-start.2 = (bf16[64,512]{1,0:T(8,128)(2,1)}, bf16[64,512]{1,0:T(8,128)(2,1)S(1)}, u32[]{:S(2)}, u32[]{:S(2)}) collective-permute-start(bf16[64,512]{1,0:T(8,128)(2,1)} %get-tuple-element.32), channel_id=1, source_target_pairs={{0,1},{1,0},{2,3},{3,2},{4,5},{5,4},{6,7},{7,6},{8,9},{9,8},{10,11... | collective-permute-start | bytes 196616 | tf_op jit(solution)/shard_map/ppermute | solution.py:404
  39.1 3.5 %local.2.local_ref = f32[64,3072]{1,0:T(8,128)} custom-call(s32[2,24]{1,0:T(2,128)} %bitcast.32, bf16[64,3072]{1,0:T(8,128)(2,1)} %bitcast.23, bf16[24,128,128]{2,1,0:T(8,128)(2,1)} %onsite_ref.3, bf16[24,128,128]{2,1,0:T(8,128)(2,1)} %down_ref.9, bf16[24,128,128]{2,1,0:T(8,128)(2,1)} %right_ref.3), custom_call_target="tpu_custom_call" | custom-call | flops 1000000 | bytes 100000 | tf_op jit(solution)/shard_map/local/pallas_call | solution.py:319
  42.6 3.2 %collective-permute-done.2.side_ref = bf16[64,512]{1,0:T(8,128)(2,1)S(1)} collective-permute-done((bf16[64,512]{1,0:T(8,128)(2,1)}, bf16[64,512]{1,0:T(8,128)(2,1)S(1)}, u32[]{:S(2)}, u32[]{:S(2)}) %collective-permute-start.2) | collective-permute-done | bytes 65568 | tf_op jit(solution)/shard_map/ppermute | solution.py:404
  45.8 0.0 collective-permute-done.above_ref
  45.8 0.0 collective-permute-done.1.below_ref
  45.8 3.9 %all-to-all-done = bf16[256,8,128]{2,1,0:T(8,128)(2,1)S(1)} async-done(((bf16[256,8,128]{2,1,0:T(8,128)(2,1)}), bf16[256,8,128]{2,1,0:T(8,128)(2,1)S(1)}, u32[]{:S(2)}, u32[]{:S(2)}) %all-to-all-start) | async-done | bytes 524320 | tf_op jit(solution)/shard_map/all_to_all | solution.py:377
  49.7 5.8 %first.1 = (f32[64,3072]{1,0:T(8,128)}, bf16[64,3072]{1,0:T(8,128)(2,1)}, f32[2,4,3072]{2,1,0:T(4,128)}, bf16[64,768]{1,0:T(8,128)(2,1)}, bf16[64,768]{1,0:T(8,1...) custom-call(s32[2,24]{1,0:T(2,128)} %bitcast.33, s32[2]{0:T(128)} %pad_add_fusion.left_ref, ...), custom_call_target="tpu_custom_call" | custom-call | flops 1000000 | bytes 100000 | tf_op jit(solution)/shard_map/first/pallas_call | solution.py:298
  55.5 12.6 %all-to-all-start.1 = ((bf16[256,8,128]{2,1,0:T(8,128)(2,1)}), bf16[256,8,128]{2,1,0:T(8,128)(2,1)S(1)}, u32[]{:S(2)}, u32[]{:S(2)}) async-start(bf16[256,8,128]{2,1,0:T(8,128)(2,1)} %bitcast.28), calls=%async_computation.1 | async-start | bytes 1048576 | tf_op jit(solution)/shard_map/all_to_all | solution.py:377
  68.1 3.5 %collective-permute-start.3 = (bf16[64,768]{1,0:T(8,128)(2,1)}, bf16[64,768]{1,0:T(8,128)(2,1)S(1)}, u32[]{:S(2)}, u32[]{:S(2)}) collective-permute-start(bf16[64,768]{1,0:T(8,128)(2,1)} %get-tuple-element.44), channel_id=1, source_target_pairs={{0,4},{4,8},{8,12},{12,16},{16,20},{20,24},{24,28},{28,32},{32,36}... | collective-permute-start | bytes 294920 | tf_op jit(solution)/shard_map/ppermute | solution.py:373
  71.7 1.9 %collective-permute-start.4 = (bf16[64,768]{1,0:T(8,128)(2,1)}, bf16[64,768]{1,0:T(8,128)(2,1)S(1)}, u32[]{:S(2)}, u32[]{:S(2)}) collective-permute-start(bf16[64,768]{1,0:T(8,128)(2,1)} %get-tuple-element.45), channel_id=1, source_target_pairs={{4,0},{8,4},{12,8},{16,12},{20,16},{24,20},{28,24},{32,28},{36,32}... | collective-permute-start | bytes 294920 | tf_op jit(solution)/shard_map/ppermute | solution.py:373
  73.6 3.5 %collective-permute-start.5 = (bf16[64,512]{1,0:T(8,128)(2,1)}, bf16[64,512]{1,0:T(8,128)(2,1)S(1)}, u32[]{:S(2)}, u32[]{:S(2)}) collective-permute-start(bf16[64,512]{1,0:T(8,128)(2,1)} %get-tuple-element.46), channel_id=1, source_target_pairs={{0,1},{1,0},{2,3},{3,2},{4,5},{5,4},{6,7},{7,6},{8,9},{9,8},{10,11... | collective-permute-start | bytes 196616 | tf_op jit(solution)/shard_map/ppermute | solution.py:404
  77.1 3.6 %local.3.local_ref = f32[64,3072]{1,0:T(8,128)} custom-call(s32[2,24]{1,0:T(2,128)} %bitcast.34, bf16[64,3072]{1,0:T(8,128)(2,1)} %get-tuple-element.43.x_ref, bf16[24,128,128]{2,1,0:T(8,128)(2,1)} %onsite_ref.3, bf16[24,128,128]{2,1,0:T(8,128)(2,1)} %down_ref.9, bf16[24,128,128]{2,1,0:T(8,128)(2,1)} %right_ref.3), custom_call_target="tpu_custom_call" | custom-call | flops 1000000 | bytes 100000 | tf_op jit(solution)/shard_map/local/pallas_call | solution.py:319
  80.7 5.6 %collective-permute-done.5.side_ref = bf16[64,512]{1,0:T(8,128)(2,1)S(1)} collective-permute-done((bf16[64,512]{1,0:T(8,128)(2,1)}, bf16[64,512]{1,0:T(8,128)(2,1)S(1)}, u32[]{:S(2)}, u32[]{:S(2)}) %collective-permute-start.5) | collective-permute-done | bytes 65568 | tf_op jit(solution)/shard_map/ppermute | solution.py:404
  86.3 0.0 collective-permute-done.3.above_ref
  86.3 0.0 collective-permute-done.4.below_ref
  86.3 4.2 %all-to-all-done.1 = bf16[256,8,128]{2,1,0:T(8,128)(2,1)S(1)} async-done(((bf16[256,8,128]{2,1,0:T(8,128)(2,1)}), bf16[256,8,128]{2,1,0:T(8,128)(2,1)S(1)}, u32[]{:S(2)}, u32[]{:S(2)}) %all-to-all-start.1) | async-done | bytes 524320 | tf_op jit(solution)/shard_map/all_to_all | solution.py:377
  90.5 3.9 %second.1 = (f32[64,3072]{1,0:T(8,128)}, f32[3,4,3072]{2,1,0:T(4,128)}) custom-call(s32[2,24]{1,0:T(2,128)} %bitcast.35, s32[2]{0:T(128)} %pad_add_fusion.left_ref, bf16[2,1024,128]{2,1,0:T(8,128)(2,1)S(1)} %bitcast.17, bf16[64,768]{1,0:T(8,128)(2,1)S(1)} %collective-permute-done.3.above_ref, bf16[64,768]{1,0:T(8,128)(2,1)S(1)} %collective-permute-done.4.below_ref, ...), custom_call_target="tpu_custom_call" | custom-call | flops 1000000 | bytes 100000 | tf_op jit(solution)/shard_map/second/pallas_call | solution.py:354
Async XLA Ops:
  4.7 45.0 %all-to-all-start = ((bf16[256,8,128]{2,1,0:T(8,128)(2,1)}), bf16[256,8,128]{2,1,0:T(8,128)(2,1)S(1)}, u32[]{:S(2)}, u32[]{:S(2)}) async-start(bf16[256,8,128]{2,1,0:T(8,128)(2,1)} %bitcast.27), calls=%async_computation | async-start | bytes 1048576 | tf_op jit(solution)/shard_map/all_to_all | solution.py:377
  29.6 16.2 %collective-permute-start = (bf16[64,768]{1,0:T(8,128)(2,1)}, bf16[64,768]{1,0:T(8,128)(2,1)S(1)}, u32[]{:S(2)}, u32[]{:S(2)}) collective-permute-start(bf16[64,768]{1,0:T(8,128)(2,1)} %get-tuple-element.30), channel_id=1, source_target_pairs={{0,4},{4,8},{8,12},{12,16},{16,20},{20,24},{24,28},{28,32},{32,36}... | collective-permute-start | bytes 294920 | tf_op jit(solution)/shard_map/ppermute | solution.py:373
  33.1 12.7 %collective-permute-start.1 = (bf16[64,768]{1,0:T(8,128)(2,1)}, bf16[64,768]{1,0:T(8,128)(2,1)S(1)}, u32[]{:S(2)}, u32[]{:S(2)}) collective-permute-start(bf16[64,768]{1,0:T(8,128)(2,1)} %get-tuple-element.31), channel_id=1, source_target_pairs={{4,0},{8,4},{12,8},{16,12},{20,16},{24,20},{28,24},{32,28},{36,32}... | collective-permute-start | bytes 294920 | tf_op jit(solution)/shard_map/ppermute | solution.py:373
  35.1 10.8 %collective-permute-start.2 = (bf16[64,512]{1,0:T(8,128)(2,1)}, bf16[64,512]{1,0:T(8,128)(2,1)S(1)}, u32[]{:S(2)}, u32[]{:S(2)}) collective-permute-start(bf16[64,512]{1,0:T(8,128)(2,1)} %get-tuple-element.32), channel_id=1, source_target_pairs={{0,1},{1,0},{2,3},{3,2},{4,5},{5,4},{6,7},{7,6},{8,9},{9,8},{10,11... | collective-permute-start | bytes 196616 | tf_op jit(solution)/shard_map/ppermute | solution.py:404
  55.5 35.1 %all-to-all-start.1 = ((bf16[256,8,128]{2,1,0:T(8,128)(2,1)}), bf16[256,8,128]{2,1,0:T(8,128)(2,1)S(1)}, u32[]{:S(2)}, u32[]{:S(2)}) async-start(bf16[256,8,128]{2,1,0:T(8,128)(2,1)} %bitcast.28), calls=%async_computation.1 | async-start | bytes 1048576 | tf_op jit(solution)/shard_map/all_to_all | solution.py:377
  68.1 18.2 %collective-permute-start.3 = (bf16[64,768]{1,0:T(8,128)(2,1)}, bf16[64,768]{1,0:T(8,128)(2,1)S(1)}, u32[]{:S(2)}, u32[]{:S(2)}) collective-permute-start(bf16[64,768]{1,0:T(8,128)(2,1)} %get-tuple-element.44), channel_id=1, source_target_pairs={{0,4},{4,8},{8,12},{12,16},{16,20},{20,24},{24,28},{28,32},{32,36}... | collective-permute-start | bytes 294920 | tf_op jit(solution)/shard_map/ppermute | solution.py:373
  71.7 14.7 %collective-permute-start.4 = (bf16[64,768]{1,0:T(8,128)(2,1)}, bf16[64,768]{1,0:T(8,128)(2,1)S(1)}, u32[]{:S(2)}, u32[]{:S(2)}) collective-permute-start(bf16[64,768]{1,0:T(8,128)(2,1)} %get-tuple-element.45), channel_id=1, source_target_pairs={{4,0},{8,4},{12,8},{16,12},{20,16},{24,20},{28,24},{32,28},{36,32}... | collective-permute-start | bytes 294920 | tf_op jit(solution)/shard_map/ppermute | solution.py:373
  73.6 12.7 %collective-permute-start.5 = (bf16[64,512]{1,0:T(8,128)(2,1)}, bf16[64,512]{1,0:T(8,128)(2,1)S(1)}, u32[]{:S(2)}, u32[]{:S(2)}) collective-permute-start(bf16[64,512]{1,0:T(8,128)(2,1)} %get-tuple-element.46), channel_id=1, source_target_pairs={{0,1},{1,0},{2,3},{3,2},{4,5},{5,4},{6,7},{7,6},{8,9},{9,8},{10,11... | collective-permute-start | bytes 196616 | tf_op jit(solution)/shard_map/ppermute | solution.py:404

commit v7 on v6

--- a/solution.py
+++ b/solution.py
@@ -34,15 +34,19 @@
     return pltpu.CompilerParams(vmem_limit_bytes=VMEM_LIMIT)
 
 
-def per_slot(table):
+def picked(table):
     spread = jnp.broadcast_to(table[None], (PEERS, CAP, PEERS)).reshape(SLOTS, PEERS)
     own = lax.broadcasted_iota(jnp.int32, (SLOTS, PEERS), 0) // CAP == lax.broadcasted_iota(
         jnp.int32, (SLOTS, PEERS), 1
     )
-    return dot(jnp.where(own, spread, 0.0).astype(BF16), jnp.ones((PEERS, TILE), BF16))
-
-
-def build_tables(rows, target, weight, hot_ref, high_ref, weight_ref):
+    return jnp.where(own, spread, 0.0).astype(BF16)
+
+
+def per_slot(table):
+    return dot(picked(table), jnp.ones((PEERS, TILE), BF16))
+
+
+def build_tables(rows, target, weight, hot_ref, high_ref, across_ref, weight_ref):
     lane = lax.broadcasted_iota(jnp.int32, (SLOTS, SPAN), 1).astype(F32)
     spread_weight = per_slot(weight)
     weight_ref[...] = spread_weight
@@ -50,7 +54,9 @@
     for end, table in ((0, rows), (1, target)):
         coarse = jnp.floor(table * (1.0 / SPAN))
         low = per_slot(table - coarse * SPAN)
-        high_ref[end * SLOTS : (end + 1) * SLOTS, :] = per_slot(coarse)
+        coarse = picked(coarse)
+        high_ref[end * SLOTS : (end + 1) * SLOTS, :] = dot(coarse, jnp.ones((PEERS, TILE), BF16)).astype(BF16)
+        across_ref[:, end * SLOTS : (end + 1) * SLOTS] = dot(jnp.ones((ROWS, PEERS), BF16), coarse, NT).astype(BF16)
         same = lane == jnp.concatenate([low, low], axis=1)
         hot_ref[2 * end * SLOTS : (2 * end + 1) * SLOTS, :] = jnp.where(same, 1.0, 0.0).astype(BF16)
         if end == 1:
@@ -63,7 +69,7 @@
     ends = []
     for end in range(2):
         hot = hot_ref[2 * end * SLOTS + start : 2 * end * SLOTS + start + chunk, :]
-        high = high_ref[end * SLOTS + start : end * SLOTS + start + chunk, :] - half
+        high = high_ref[end * SLOTS + start : end * SLOTS + start + chunk, :].astype(F32) - half
         total = jnp.zeros((chunk, TILE), F32)
         for q in range(HI // 2):
             found = dot(hot, jnp.concatenate([parts[2 * q], parts[2 * q + 1]], axis=0), NT)
@@ -81,29 +87,56 @@
 CHUNK = 256
 
 
-def gather_payload(x_ref, hot_ref, high_ref, weight_ref, out_ref):
+CHUNKS = SLOTS // CHUNK
+
+
+def started(source, target, semaphore):
+    copy = pltpu.make_async_copy(source, target, semaphore)
+    copy.start()
+    return copy
+
+
+def gather_payload(x_ref, hot_ref, high_ref, weight_ref, out_ref, stage_ref, sems):
     parts = [x_ref[:, h * SPAN : (h + 1) * SPAN] for h in range(HI)]
-    for start in range(0, SLOTS, CHUNK):
-        ends = gather_ends(parts, hot_ref, high_ref, start, CHUNK)
-        payload = as_payload(ends, weight_ref[start : start + CHUNK, :])
-        out_ref[0, start : start + CHUNK, :] = payload
-        out_ref[1, start : start + CHUNK, :] = payload
+    copies = []
+    for i in range(CHUNKS):
+        rows = pl.ds(i * CHUNK, CHUNK)
+        ends = gather_ends(parts, hot_ref, high_ref, i * CHUNK, CHUNK)
+        stage_ref[i * CHUNK : (i + 1) * CHUNK, :] = as_payload(ends, weight_ref[i * CHUNK : (i + 1) * CHUNK, :])
+        for sheet in range(2):
+            copies.append(started(stage_ref.at[rows, :], out_ref.at[sheet, rows, :], sems.at[sheet, i]))
+    return copies
+
+
+STAGE_SCRATCH = [pltpu.VMEM((SLOTS, 2 * ROWS), BF16), pltpu.SemaphoreType.DMA((2, CHUNKS))]
+ANY = pl.BlockSpec(memory_space=pl.ANY)
+SMEM = pl.BlockSpec(memory_space=pltpu.SMEM)
+VMEM = pl.BlockSpec(memory_space=pltpu.VMEM)
+
+
+def span(ref, h):
+    return ref.at[:, pl.ds(h * SPAN, SPAN)]
 
 
 def prepare_kernel(
-    x_ref, rows_ref, target_ref, weight_ref, count_ref, hot_ref, high_ref, spread_ref, out_ref
+    x_ref, rows_ref, target_ref, weight_ref, count_ref, hot_ref, high_ref, across_ref, spread_ref, out_ref,
+    x_buf, x_sem, stage_ref, stage_sems,
 ):
+    x_copy = started(x_ref, x_buf, x_sem)
     live = lax.broadcasted_iota(jnp.int32, (CAP, PEERS), 0) < count_ref[...]
     weight = jnp.where(live, weight_ref[...].astype(F32), 0.0)
     build_tables(
-        rows_ref[...].astype(F32), target_ref[...].astype(F32), weight, hot_ref, high_ref, spread_ref
-    )
-    gather_payload(x_ref, hot_ref, high_ref, spread_ref, out_ref)
+        rows_ref[...].astype(F32), target_ref[...].astype(F32), weight, hot_ref, high_ref, across_ref, spread_ref
+    )
+    x_copy.wait()
+    for copy in gather_payload(x_buf, hot_ref, high_ref, spread_ref, out_ref, stage_ref, stage_sems):
+        copy.wait()
 
 
 TABLE_SHAPES = (
     pltpu.VMEM((3 * SLOTS, SPAN), BF16),
-    pltpu.VMEM((2 * SLOTS, TILE), F32),
+    pltpu.VMEM((2 * SLOTS, TILE), BF16),
+    pltpu.VMEM((ROWS, 2 * SLOTS), BF16),
     jax.ShapeDtypeStruct((SLOTS, TILE), F32),
 )
 
@@ -111,7 +144,10 @@
 def prepare(x, link_rows, link_target, link_weight, link_count):
     return pl.pallas_call(
         prepare_kernel,
+        in_specs=[ANY] + [VMEM] * 4,
+        out_specs=(VMEM,) * len(TABLE_SHAPES) + (ANY,),
         out_shape=TABLE_SHAPES + (jax.ShapeDtypeStruct((2, SLOTS, 2 * ROWS), BF16),),
+        scratch_shapes=[pltpu.VMEM((ROWS, SITES_DEV), BF16), pltpu.SemaphoreType.DMA(())] + STAGE_SCRATCH,
         compiler_params=params(),
         cost_estimate=COST,
         name="prepare",
@@ -143,8 +179,6 @@
     jax.ShapeDtypeStruct((ROWS, TC * TILE), BF16),
     jax.ShapeDtypeStruct((ROWS, TR * TILE), BF16),
 )
-SMEM = pl.BlockSpec(memory_space=pltpu.SMEM)
-VMEM = pl.BlockSpec(memory_space=pltpu.VMEM)
 DOWN_EDGE = pl.BlockSpec((TC, TILE, TILE), lambda i: (TR - 1, 0, 0))
 RIGHT_EDGE = pl.BlockSpec((TR, 1, TILE, TILE), lambda i: (0, TC - 1, 0, 0))
 
@@ -238,15 +272,12 @@
 SCATTER_SCRATCH = [pltpu.VMEM((HI * ROWS, 2 * SLOTS), BF16), pltpu.VMEM((HI * ROWS, SPAN), F32)]
 
 
-def scatter_into(landed, hot_ref, high_ref, mask_ref, total_ref):
-    turned = landed.astype(F32).T.astype(BF16)
-    high_send = high_ref[0:SLOTS, :].T.astype(BF16)[:ROWS]
-    high_recv = high_ref[SLOTS : 2 * SLOTS, :].T.astype(BF16)[:ROWS]
-    zero = jnp.zeros((ROWS, SLOTS), BF16)
+def scatter_into(landed, hot_ref, across_ref, mask_ref, total_ref):
+    turned = landed.T
+    ends = jnp.concatenate([turned[ROWS:], turned[:ROWS]], axis=1)
+    zero = jnp.zeros_like(ends)
     for h in range(HI):
-        rows = slice(h * ROWS, (h + 1) * ROWS)
-        mask_ref[rows, 0:SLOTS] = jnp.where(high_send == BF16(h), turned[ROWS:], zero)
-        mask_ref[rows, SLOTS : 2 * SLOTS] = jnp.where(high_recv == BF16(h), turned[:ROWS], zero)
+        mask_ref[h * ROWS : (h + 1) * ROWS, :] = jnp.where(across_ref[...] == BF16(h), ends, zero)
     group = 4
     for start in range(0, HI, group):
         total_ref[start * ROWS : (start + group) * ROWS, :] = dot(
@@ -266,11 +297,19 @@
 
 
 def first_kernel(
-    pattern_ref, left_ref, landed_ref, above_ref, below_ref, side_ref, hot_ref, high_ref,
-    v0_ref, weight_ref, local_ref, pairing_ref, down_ref, right_ref,
-    one_ref, x_ref, mom_ref, top_ref, lower_ref, beside_ref, out_ref, mask_ref, total_ref,
+    pattern_ref, left_ref, landed_ref, above_ref, below_ref, side_ref, hot_ref, high_ref, across_ref,
+    v0_hbm, local_hbm, weight_hbm, pairing_ref, down_ref, right_ref,
+    one_hbm, x_hbm, mom_ref, top_ref, lower_ref, beside_ref, out_ref, mask_ref, total_ref,
+    v0_ref, local_ref, weight_ref, one_ref, x_ref, in_sems, one_sems, x_sems, stage_ref, stage_sems,
 ):
-    scatter_into(landed_ref[left_ref[1]], hot_ref, high_ref, mask_ref, total_ref)
+    arriving = [
+        started(source, target, in_sems.at[i])
+        for i, (source, target) in enumerate(((v0_hbm, v0_ref), (local_hbm, local_ref), (weight_hbm, weight_ref)))
+    ]
+    scatter_into(landed_ref[left_ref[1]], hot_ref, across_ref, mask_ref, total_ref)
+    for copy in arriving:
+        copy.wait()
+    leaving = []
     for tile in range(TR * TC):
         cols = slice(tile * TILE, (tile + 1) * TILE)
         hop = whole_hop(
@@ -282,8 +321,14 @@
         x_ref[:, cols] = one.astype(BF16)
         mom_ref[0, :, cols] = vector_mean(v0 * v0)
         mom_ref[1, :, cols] = vector_mean(v0 * one)
-    gather_payload(x_ref, hot_ref, high_ref, weight_ref, out_ref)
+        h, part = divmod(tile, SPAN // TILE)
+        if part == SPAN // TILE - 1:
+            leaving.append(started(span(one_ref, h), span(one_hbm, h), one_sems.at[h]))
+            leaving.append(started(span(x_ref, h), span(x_hbm, h), x_sems.at[h]))
+    leaving += gather_payload(x_ref, hot_ref, high_ref, weight_ref, out_ref, stage_ref, stage_sems)
     write_edges(pattern_ref, left_ref, x_ref, down_ref, right_ref, 0, top_ref, lower_ref, beside_ref)
+    for copy in leaving:
+        copy.wait()
 
 
 def first(pattern, left_flag, v0, landed, tables, local_part, pairing, halo, down_hop, right_hop):
@@ -292,16 +337,27 @@
         jax.ShapeDtypeStruct((ROWS, SITES_DEV), BF16),
         jax.ShapeDtypeStruct((2, 4, SITES_DEV), F32),
     ) + EDGE_SHAPES + (jax.ShapeDtypeStruct((2, SLOTS, 2 * ROWS), BF16),)
-    hot, high, weight = tables
-    resident = [on_core(a) for a in (landed, *halo, hot, high)]
-    arrays = (v0, weight, local_part, pairing)
+    hot, high, across, weight = tables
+    resident = [on_core(a) for a in (landed, *halo, hot, high, across)]
+    arrays = (v0, local_part, weight, pairing)
     return pl.pallas_call(
         first_kernel,
         grid=(1,),
-        in_specs=[SMEM, SMEM] + [VMEM] * len(resident) + [whole(a.shape) for a in arrays] + [DOWN_EDGE, RIGHT_EDGE],
-        out_specs=tuple(whole(s.shape) for s in shapes),
+        in_specs=[SMEM, SMEM] + [VMEM] * len(resident) + [ANY] * 3 + [whole(pairing.shape), DOWN_EDGE, RIGHT_EDGE],
+        out_specs=(ANY, ANY) + tuple(whole(s.shape) for s in shapes[2:-1]) + (ANY,),
         out_shape=shapes,
-        scratch_shapes=SCATTER_SCRATCH,
+        scratch_shapes=SCATTER_SCRATCH
+        + [
+            pltpu.VMEM((ROWS, SITES_DEV), BF16),
+            pltpu.VMEM((ROWS, SITES_DEV), F32),
+            pltpu.VMEM((SLOTS, TILE), F32),
+            pltpu.VMEM((ROWS, SITES_DEV), F32),
+            pltpu.VMEM((ROWS, SITES_DEV), BF16),
+            pltpu.SemaphoreType.DMA((3,)),
+            pltpu.SemaphoreType.DMA((HI,)),
+            pltpu.SemaphoreType.DMA((HI,)),
+        ]
+        + STAGE_SCRATCH,
         compiler_params=params(),
         cost_estimate=COST,
         name="first",
@@ -327,11 +383,18 @@
 
 
 def second_kernel(
-    pattern_ref, left_ref, landed_ref, above_ref, below_ref, side_ref, hot_ref, high_ref,
-    v0_ref, one_ref, local_ref, pairing_ref, mom_in_ref, down_ref, right_ref,
-    two_ref, mom_ref, mask_ref, total_ref,
+    pattern_ref, left_ref, landed_ref, above_ref, below_ref, side_ref, hot_ref, across_ref,
+    v0_hbm, one_hbm, local_hbm, pairing_ref, mom_in_ref, down_ref, right_ref,
+    two_hbm, mom_ref, mask_ref, total_ref, v0_ref, one_ref, local_ref, two_ref, in_sems, two_sems,
 ):
-    scatter_into(landed_ref[left_ref[1]], hot_ref, high_ref, mask_ref, total_ref)
+    arriving = [
+        started(source, target, in_sems.at[i])
+        for i, (source, target) in enumerate(((v0_hbm, v0_ref), (one_hbm, one_ref), (local_hbm, local_ref)))
+    ]
+    scatter_into(landed_ref[left_ref[1]], hot_ref, across_ref, mask_ref, total_ref)
+    for copy in arriving:
+        copy.wait()
+    leaving = []
     mom_ref[0:2] = mom_in_ref[...]
     for tile in range(TR * TC):
         cols = slice(tile * TILE, (tile + 1) * TILE)
@@ -342,22 +405,35 @@
         two = 2.0 * (signed(hop) + pairing_ref[:, cols] * swapped(one_ref[:, cols])) - v0
         two_ref[:, cols] = two
         mom_ref[2, :, cols] = vector_mean(v0 * two)
-
-
-def second(pattern, left_flag, v0, one, landed, hot, high, local_part, pairing, mom, halo, down_hop, right_hop):
+        h, part = divmod(tile, SPAN // TILE)
+        if part == SPAN // TILE - 1:
+            leaving.append(started(span(two_ref, h), span(two_hbm, h), two_sems.at[h]))
+    for copy in leaving:
+        copy.wait()
+
+
+def second(pattern, left_flag, v0, one, landed, hot, across, local_part, pairing, mom, halo, down_hop, right_hop):
     shapes = (
         jax.ShapeDtypeStruct((ROWS, SITES_DEV), F32),
         jax.ShapeDtypeStruct((3, 4, SITES_DEV), F32),
     )
-    resident = [on_core(a) for a in (landed, *halo, hot, high)]
+    resident = [on_core(a) for a in (landed, *halo, hot, across)]
     arrays = (v0, one, local_part, pairing, mom)
     return pl.pallas_call(
         second_kernel,
         grid=(1,),
-        in_specs=[SMEM, SMEM] + [VMEM] * len(resident) + [whole(a.shape) for a in arrays] + [DOWN_EDGE, RIGHT_EDGE],
-        out_specs=tuple(whole(s.shape) for s in shapes),
+        in_specs=[SMEM, SMEM] + [VMEM] * len(resident) + [ANY] * 3 + [whole(pairing.shape), whole(mom.shape)] + [DOWN_EDGE, RIGHT_EDGE],
+        out_specs=(ANY, whole(shapes[1].shape)),
         out_shape=shapes,
-        scratch_shapes=SCATTER_SCRATCH,
+        scratch_shapes=SCATTER_SCRATCH
+        + [
+            pltpu.VMEM((ROWS, SITES_DEV), BF16),
+            pltpu.VMEM((ROWS, SITES_DEV), F32),
+            pltpu.VMEM((ROWS, SITES_DEV), F32),
+            pltpu.VMEM((ROWS, SITES_DEV), F32),
+            pltpu.SemaphoreType.DMA((3,)),
+            pltpu.SemaphoreType.DMA((HI,)),
+        ],
         compiler_params=params(),
         cost_estimate=COST,
         name="second",
@@ -405,7 +481,7 @@
         )
 
     *tables, payload = prepare(v0, link_rows, link_target, link_weight, link_count)
-    hot, high, weight = tables
+    hot, _, across, _ = tables
     spread = spread_out(payload)
     halo = halo_of(*edges(pattern, left_flag, v0, down_hop, right_hop))
     local_part = local(pattern, v0, onsite, down_hop, right_hop)
@@ -418,7 +494,7 @@
     local_part = local(pattern, x, onsite, down_hop, right_hop)
     landed, local_part, halo = lax.optimization_barrier((spread, local_part, halo))
     two, mom = second(
-        pattern, left_flag, v0, one, landed, hot, high, local_part, pairing, mom, halo, down_hop, right_hop
+        pattern, left_flag, v0, one, landed, hot, across, local_part, pairing, mom, halo, down_hop, right_hop
     )
     shape = rand_vectors.shape
     return one.reshape(shape), two.reshape(shape), mom

time: 95 us -> 100 us (1.053)
  Pallas kernels: 22.7 us -> 27.6 us
    pallas_call x1, Pallas kernels: 5.77 us -> 7.76 us  [first(): pl.pallas_call(first_kernel, grid=(1,), in_specs=[SMEM, SMEM] + [VMEM] *...]
    pallas_call x1, Pallas kernels: 3.86 us -> 5.6 us  [second(): pl.pallas_call(second_kernel, grid=(1,), in_specs=[SMEM, SMEM] + [VMEM] *...]
    pallas_call x1, Pallas kernels: 4.04 us -> 5.12 us  [prepare(): pl.pallas_call(prepare_kernel, in_specs=[ANY] + [VMEM] * 4, out_specs=(VM...]
  transfers between devices with their start and end apart: 8 -> 8, of which waited for: 4 -> 4; matrix products, arithmetic and copies ran while one was open for 1% -> 1% of each run, Pallas kernels for 10% -> 9%
where the time goes in v7:
time: 100 us; the launch traced here: 99.6 us
  starting transfers between devices  53.7 us (54%)
  Pallas kernels  27.6 us (28%)
  waiting for transfers between devices  16.9 us (17%)
    all_to_all x2, starting transfers between devices, spread_out(): lax.all_to_all(payload.reshape(2 * PEERS, CAP, 2 * ROWS), ('sheet',) + TI...  35.2 us
    ppermute x4, starting transfers between devices, passed_along(): return lax.ppermute(value, TILE_AXES, pairs)  10.9 us
    ppermute x2, waiting for transfers between devices, halo_of(): lax.ppermute(side_part, 'side', [(0, 1), (1, 0)])  8.79 us
    all_to_all x2, waiting for transfers between devices, spread_out(): lax.all_to_all(payload.reshape(2 * PEERS, CAP, 2 * ROWS), ('sheet',) + TI...  8.1 us
    pallas_call x1, Pallas kernels, first(): pl.pallas_call(first_kernel, grid=(1,), in_specs=[SMEM, SMEM] + [VMEM] *...  7.76 us
    ppermute x2, starting transfers between devices, halo_of(): lax.ppermute(side_part, 'side', [(0, 1), (1, 0)])  7.55 us
    pallas_call x2, Pallas kernels, local(): pl.pallas_call(local_kernel, in_specs=[SMEM] + [VMEM] * 4, out_shape=jax....  7.11 us
    pallas_call x1, Pallas kernels, second(): pl.pallas_call(second_kernel, grid=(1,), in_specs=[SMEM, SMEM] + [VMEM] *...  5.6 us
  transfers between devices with their start and end apart: 8, of which 4 were waited for; matrix products, arithmetic and copies ran while one was open for 1% of the time, Pallas kernels for 9%

profile of v7, /device:TPU:1, one launch (start us, length us, event | category | flops | bytes accessed | tf_op | source)
XLA Modules:
  0.0 99.6 jit_solution(7132165942717188748)
XLA Ops:
  0.6 5.1 %prepare.1 = (bf16[3072,256]{1,0:T(8,128)(2,1)S(1)}, bf16[2048,128]{1,0:T(8,128)(2,1)S(1)}, bf16[64,2048]{1,0:T(8,128)(2,1)S(1)}, f32[1024,128]{1,0:T(8,128)}, bf16[2,1024,128]{2,1,0:T(8,128)(2,1)}) custom-call(bf16[64,3072]{1,0:T(8,128)(2,1)} %bitcast.21, s32[8,128]{1,0:T(8,128)} %bitcast.36, s32[8,128]{1,0:T(8,128)} %bitcast.37, bf16[8,128]{1,0:T(8,128)(2,1)} %bitcast.38, ...), custom_call_target="tpu_custom_call" | custom-call | flops 1000000 | bytes 100000 | tf_op jit(solution)/shard_map/prepare/pallas_call | solution.py:145
  5.8 22.4 %all-to-all-start = ((bf16[256,8,128]{2,1,0:T(8,128)(2,1)}), bf16[256,8,128]{2,1,0:T(8,128)(2,1)S(1)}, u32[]{:S(2)}, u32[]{:S(2)}) async-start(bf16[256,8,128]{2,1,0:T(8,128)(2,1)} %bitcast.27), calls=%async_computation | async-start | bytes 1048576 | tf_op jit(solution)/shard_map/all_to_all | solution.py:453
  28.2 0.6 pad_add_fusion.left_ref
  28.7 2.0 %edges.1 = (bf16[64,768]{1,0:T(8,128)(2,1)}, bf16[64,768]{1,0:T(8,128)(2,1)}, bf16[64,512]{1,0:T(8,128)(2,1)}) custom-call(s32[2,24]{1,0:T(2,128)} %bitcast.31, s32[2]{0:T(128)} %pad_add_fusion.left_ref, bf16[64,3072]{1,0:T(8,128)(2,1)} %bitcast.22, bf16[24,128,128]{2,1,0:T(8,128)(2,1)} %down_ref.9, bf16[4,6,128,128]{3,2,1,0:T(8,128)(2,1)} %bitcast.18), custom_call_target="tpu_custom_call" | custom-call | flops 1000000 | bytes 100000 | tf_op jit(solution)/shard_map/edges/pallas_call | solution.py:195
  30.7 3.5 %collective-permute-start = (bf16[64,768]{1,0:T(8,128)(2,1)}, bf16[64,768]{1,0:T(8,128)(2,1)S(1)}, u32[]{:S(2)}, u32[]{:S(2)}) collective-permute-start(bf16[64,768]{1,0:T(8,128)(2,1)} %get-tuple-element.31), channel_id=1, source_target_pairs={{0,4},{4,8},{8,12},{12,16},{16,20},{20,24},{24,28},{28,32},{32,36}... | collective-permute-start | bytes 294920 | tf_op jit(solution)/shard_map/ppermute | solution.py:449
  34.2 1.9 %collective-permute-start.1 = (bf16[64,768]{1,0:T(8,128)(2,1)}, bf16[64,768]{1,0:T(8,128)(2,1)S(1)}, u32[]{:S(2)}, u32[]{:S(2)}) collective-permute-start(bf16[64,768]{1,0:T(8,128)(2,1)} %get-tuple-element.32), channel_id=1, source_target_pairs={{4,0},{8,4},{12,8},{16,12},{20,16},{24,20},{28,24},{32,28},{36,32}... | collective-permute-start | bytes 294920 | tf_op jit(solution)/shard_map/ppermute | solution.py:449
  36.2 4.0 %collective-permute-start.2 = (bf16[64,512]{1,0:T(8,128)(2,1)}, bf16[64,512]{1,0:T(8,128)(2,1)S(1)}, u32[]{:S(2)}, u32[]{:S(2)}) collective-permute-start(bf16[64,512]{1,0:T(8,128)(2,1)} %get-tuple-element.33), channel_id=1, source_target_pairs={{0,1},{1,0},{2,3},{3,2},{4,5},{5,4},{6,7},{7,6},{8,9},{9,8},{10,11... | collective-permute-start | bytes 196616 | tf_op jit(solution)/shard_map/ppermute | solution.py:480
  40.2 3.5 %local.2.local_hbm = f32[64,3072]{1,0:T(8,128)} custom-call(s32[2,24]{1,0:T(2,128)} %bitcast.32, bf16[64,3072]{1,0:T(8,128)(2,1)} %bitcast.23, bf16[24,128,128]{2,1,0:T(8,128)(2,1)} %onsite_ref.3, bf16[24,128,128]{2,1,0:T(8,128)(2,1)} %down_ref.9, bf16[24,128,128]{2,1,0:T(8,128)(2,1)} %right_ref.3), custom_call_target="tpu_custom_call" | custom-call | flops 1000000 | bytes 100000 | tf_op jit(solution)/shard_map/local/pallas_call | solution.py:375
  43.7 3.2 %collective-permute-done.2.side_ref = bf16[64,512]{1,0:T(8,128)(2,1)S(1)} collective-permute-done((bf16[64,512]{1,0:T(8,128)(2,1)}, bf16[64,512]{1,0:T(8,128)(2,1)S(1)}, u32[]{:S(2)}, u32[]{:S(2)}) %collective-permute-start.2) | collective-permute-done | bytes 65568 | tf_op jit(solution)/shard_map/ppermute | solution.py:480
  46.9 0.0 collective-permute-done.above_ref
  46.9 0.0 collective-permute-done.1.below_ref
  46.9 3.9 %all-to-all-done = bf16[256,8,128]{2,1,0:T(8,128)(2,1)S(1)} async-done(((bf16[256,8,128]{2,1,0:T(8,128)(2,1)}), bf16[256,8,128]{2,1,0:T(8,128)(2,1)S(1)}, u32[]{:S(2)}, u32[]{:S(2)}) %all-to-all-start) | async-done | bytes 524320 | tf_op jit(solution)/shard_map/all_to_all | solution.py:453
  50.8 7.8 %first.1 = (f32[64,3072]{1,0:T(8,128)}, bf16[64,3072]{1,0:T(8,128)(2,1)}, f32[2,4,3072]{2,1,0:T(4,128)}, bf16[64,768]{1,0:T(8,128)(2,1)}, bf16[64,768]{1,0:T(8,1...) custom-call(s32[2,24]{1,0:T(2,128)} %bitcast.33, s32[2]{0:T(128)} %pad_add_fusion.left_ref, ...), custom_call_target="tpu_custom_call" | custom-call | flops 1000000 | bytes 100000 | tf_op jit(solution)/shard_map/first/pallas_call | solution.py:343
  58.6 12.8 %all-to-all-start.1 = ((bf16[256,8,128]{2,1,0:T(8,128)(2,1)}), bf16[256,8,128]{2,1,0:T(8,128)(2,1)S(1)}, u32[]{:S(2)}, u32[]{:S(2)}) async-start(bf16[256,8,128]{2,1,0:T(8,128)(2,1)} %bitcast.28), calls=%async_computation.1 | async-start | bytes 1048576 | tf_op jit(solution)/shard_map/all_to_all | solution.py:453
  71.4 3.5 %collective-permute-start.3 = (bf16[64,768]{1,0:T(8,128)(2,1)}, bf16[64,768]{1,0:T(8,128)(2,1)S(1)}, u32[]{:S(2)}, u32[]{:S(2)}) collective-permute-start(bf16[64,768]{1,0:T(8,128)(2,1)} %get-tuple-element.46), channel_id=1, source_target_pairs={{0,4},{4,8},{8,12},{12,16},{16,20},{20,24},{24,28},{28,32},{32,36}... | collective-permute-start | bytes 294920 | tf_op jit(solution)/shard_map/ppermute | solution.py:449
  74.9 1.9 %collective-permute-start.4 = (bf16[64,768]{1,0:T(8,128)(2,1)}, bf16[64,768]{1,0:T(8,128)(2,1)S(1)}, u32[]{:S(2)}, u32[]{:S(2)}) collective-permute-start(bf16[64,768]{1,0:T(8,128)(2,1)} %get-tuple-element.47), channel_id=1, source_target_pairs={{4,0},{8,4},{12,8},{16,12},{20,16},{24,20},{28,24},{32,28},{36,32}... | collective-permute-start | bytes 294920 | tf_op jit(solution)/shard_map/ppermute | solution.py:449
  76.9 3.5 %collective-permute-start.5 = (bf16[64,512]{1,0:T(8,128)(2,1)}, bf16[64,512]{1,0:T(8,128)(2,1)S(1)}, u32[]{:S(2)}, u32[]{:S(2)}) collective-permute-start(bf16[64,512]{1,0:T(8,128)(2,1)} %get-tuple-element.48), channel_id=1, source_target_pairs={{0,1},{1,0},{2,3},{3,2},{4,5},{5,4},{6,7},{7,6},{8,9},{9,8},{10,11... | collective-permute-start | bytes 196616 | tf_op jit(solution)/shard_map/ppermute | solution.py:480
  80.4 3.6 %local.3.local_hbm = f32[64,3072]{1,0:T(8,128)} custom-call(s32[2,24]{1,0:T(2,128)} %bitcast.34, bf16[64,3072]{1,0:T(8,128)(2,1)} %get-tuple-element.45.x_ref, bf16[24,128,128]{2,1,0:T(8,128)(2,1)} %onsite_ref.3, bf16[24,128,128]{2,1,0:T(8,128)(2,1)} %down_ref.9, bf16[24,128,128]{2,1,0:T(8,128)(2,1)} %right_ref.3), custom_call_target="tpu_custom_call" | custom-call | flops 1000000 | bytes 100000 | tf_op jit(solution)/shard_map/local/pallas_call | solution.py:375
  84.0 5.6 %collective-permute-done.5.side_ref = bf16[64,512]{1,0:T(8,128)(2,1)S(1)} collective-permute-done((bf16[64,512]{1,0:T(8,128)(2,1)}, bf16[64,512]{1,0:T(8,128)(2,1)S(1)}, u32[]{:S(2)}, u32[]{:S(2)}) %collective-permute-start.5) | collective-permute-done | bytes 65568 | tf_op jit(solution)/shard_map/ppermute | solution.py:480
  89.6 0.0 collective-permute-done.3.above_ref
  89.6 0.0 collective-permute-done.4.below_ref
  89.6 4.2 %all-to-all-done.1 = bf16[256,8,128]{2,1,0:T(8,128)(2,1)S(1)} async-done(((bf16[256,8,128]{2,1,0:T(8,128)(2,1)}), bf16[256,8,128]{2,1,0:T(8,128)(2,1)S(1)}, u32[]{:S(2)}, u32[]{:S(2)}) %all-to-all-start.1) | async-done | bytes 524320 | tf_op jit(solution)/shard_map/all_to_all | solution.py:453
  93.8 5.6 %second.1 = (f32[64,3072]{1,0:T(8,128)}, f32[3,4,3072]{2,1,0:T(4,128)}) custom-call(s32[2,24]{1,0:T(2,128)} %bitcast.35, s32[2]{0:T(128)} %pad_add_fusion.left_ref, bf16[2,1024,128]{2,1,0:T(8,128)(2,1)S(1)} %bitcast.17, bf16[64,768]{1,0:T(8,128)(2,1)S(1)} %collective-permute-done.3.above_ref, bf16[64,768]{1,0:T(8,128)(2,1)S(1)} %collective-permute-done.4.below_ref, ...), custom_call_target="tpu_custom_call" | custom-call | flops 1000000 | bytes 100000 | tf_op jit(solution)/shard_map/second/pallas_call | solution.py:422
Async XLA Ops:
  5.8 45.0 %all-to-all-start = ((bf16[256,8,128]{2,1,0:T(8,128)(2,1)}), bf16[256,8,128]{2,1,0:T(8,128)(2,1)S(1)}, u32[]{:S(2)}, u32[]{:S(2)}) async-start(bf16[256,8,128]{2,1,0:T(8,128)(2,1)} %bitcast.27), calls=%async_computation | async-start | bytes 1048576 | tf_op jit(solution)/shard_map/all_to_all | solution.py:453
  30.7 16.2 %collective-permute-start = (bf16[64,768]{1,0:T(8,128)(2,1)}, bf16[64,768]{1,0:T(8,128)(2,1)S(1)}, u32[]{:S(2)}, u32[]{:S(2)}) collective-permute-start(bf16[64,768]{1,0:T(8,128)(2,1)} %get-tuple-element.31), channel_id=1, source_target_pairs={{0,4},{4,8},{8,12},{12,16},{16,20},{20,24},{24,28},{28,32},{32,36}... | collective-permute-start | bytes 294920 | tf_op jit(solution)/shard_map/ppermute | solution.py:449
  34.2 12.7 %collective-permute-start.1 = (bf16[64,768]{1,0:T(8,128)(2,1)}, bf16[64,768]{1,0:T(8,128)(2,1)S(1)}, u32[]{:S(2)}, u32[]{:S(2)}) collective-permute-start(bf16[64,768]{1,0:T(8,128)(2,1)} %get-tuple-element.32), channel_id=1, source_target_pairs={{4,0},{8,4},{12,8},{16,12},{20,16},{24,20},{28,24},{32,28},{36,32}... | collective-permute-start | bytes 294920 | tf_op jit(solution)/shard_map/ppermute | solution.py:449
  36.2 10.7 %collective-permute-start.2 = (bf16[64,512]{1,0:T(8,128)(2,1)}, bf16[64,512]{1,0:T(8,128)(2,1)S(1)}, u32[]{:S(2)}, u32[]{:S(2)}) collective-permute-start(bf16[64,512]{1,0:T(8,128)(2,1)} %get-tuple-element.33), channel_id=1, source_target_pairs={{0,1},{1,0},{2,3},{3,2},{4,5},{5,4},{6,7},{7,6},{8,9},{9,8},{10,11... | collective-permute-start | bytes 196616 | tf_op jit(solution)/shard_map/ppermute | solution.py:480
  58.6 35.3 %all-to-all-start.1 = ((bf16[256,8,128]{2,1,0:T(8,128)(2,1)}), bf16[256,8,128]{2,1,0:T(8,128)(2,1)S(1)}, u32[]{:S(2)}, u32[]{:S(2)}) async-start(bf16[256,8,128]{2,1,0:T(8,128)(2,1)} %bitcast.28), calls=%async_computation.1 | async-start | bytes 1048576 | tf_op jit(solution)/shard_map/all_to_all | solution.py:453
  71.4 18.2 %collective-permute-start.3 = (bf16[64,768]{1,0:T(8,128)(2,1)}, bf16[64,768]{1,0:T(8,128)(2,1)S(1)}, u32[]{:S(2)}, u32[]{:S(2)}) collective-permute-start(bf16[64,768]{1,0:T(8,128)(2,1)} %get-tuple-element.46), channel_id=1, source_target_pairs={{0,4},{4,8},{8,12},{12,16},{16,20},{20,24},{24,28},{28,32},{32,36}... | collective-permute-start | bytes 294920 | tf_op jit(solution)/shard_map/ppermute | solution.py:449
  74.9 14.7 %collective-permute-start.4 = (bf16[64,768]{1,0:T(8,128)(2,1)}, bf16[64,768]{1,0:T(8,128)(2,1)S(1)}, u32[]{:S(2)}, u32[]{:S(2)}) collective-permute-start(bf16[64,768]{1,0:T(8,128)(2,1)} %get-tuple-element.47), channel_id=1, source_target_pairs={{4,0},{8,4},{12,8},{16,12},{20,16},{24,20},{28,24},{32,28},{36,32}... | collective-permute-start | bytes 294920 | tf_op jit(solution)/shard_map/ppermute | solution.py:449
  76.9 12.7 %collective-permute-start.5 = (bf16[64,512]{1,0:T(8,128)(2,1)}, bf16[64,512]{1,0:T(8,128)(2,1)S(1)}, u32[]{:S(2)}, u32[]{:S(2)}) collective-permute-start(bf16[64,512]{1,0:T(8,128)(2,1)} %get-tuple-element.48), channel_id=1, source_target_pairs={{0,1},{1,0},{2,3},{3,2},{4,5},{5,4},{6,7},{7,6},{8,9},{9,8},{10,11... | collective-permute-start | bytes 196616 | tf_op jit(solution)/shard_map/ppermute | solution.py:480

commit v8 on v6

--- a/solution.py
+++ b/solution.py
@@ -34,23 +34,33 @@
     return pltpu.CompilerParams(vmem_limit_bytes=VMEM_LIMIT)
 
 
-def per_slot(table):
+def picked(table):
     spread = jnp.broadcast_to(table[None], (PEERS, CAP, PEERS)).reshape(SLOTS, PEERS)
     own = lax.broadcasted_iota(jnp.int32, (SLOTS, PEERS), 0) // CAP == lax.broadcasted_iota(
         jnp.int32, (SLOTS, PEERS), 1
     )
-    return dot(jnp.where(own, spread, 0.0).astype(BF16), jnp.ones((PEERS, TILE), BF16))
-
-
-def build_tables(rows, target, weight, hot_ref, high_ref, weight_ref):
+    return jnp.where(own, spread, 0.0).astype(BF16)
+
+
+def per_slot(table):
+    return dot(picked(table), jnp.ones((PEERS, TILE), BF16))
+
+
+def build_tables(rows, target, weight, hot_ref, high_ref, across_ref, weight_ref):
     lane = lax.broadcasted_iota(jnp.int32, (SLOTS, SPAN), 1).astype(F32)
     spread_weight = per_slot(weight)
     weight_ref[...] = spread_weight
     wide_weight = jnp.concatenate([spread_weight, spread_weight], axis=1)
+    rows_half = lax.broadcasted_iota(jnp.int32, (2 * PEERS, 2 * TILE), 0) < PEERS
+    both = (rows_half == (lax.broadcasted_iota(jnp.int32, (2 * PEERS, 2 * TILE), 1) < TILE)).astype(BF16)
     for end, table in ((0, rows), (1, target)):
         coarse = jnp.floor(table * (1.0 / SPAN))
-        low = per_slot(table - coarse * SPAN)
-        high_ref[end * SLOTS : (end + 1) * SLOTS, :] = per_slot(coarse)
+        low = picked(table - coarse * SPAN)
+        coarse = picked(coarse)
+        wide = dot(jnp.concatenate([low, coarse], axis=1), both)
+        low = wide[:, :TILE]
+        high_ref[end * SLOTS : (end + 1) * SLOTS, :] = wide[:, TILE:].astype(BF16)
+        across_ref[:, end * SLOTS : (end + 1) * SLOTS] = dot(jnp.ones((ROWS, PEERS), BF16), coarse, NT).astype(BF16)
         same = lane == jnp.concatenate([low, low], axis=1)
         hot_ref[2 * end * SLOTS : (2 * end + 1) * SLOTS, :] = jnp.where(same, 1.0, 0.0).astype(BF16)
         if end == 1:
@@ -63,11 +73,12 @@
     ends = []
     for end in range(2):
         hot = hot_ref[2 * end * SLOTS + start : 2 * end * SLOTS + start + chunk, :]
-        high = high_ref[end * SLOTS + start : end * SLOTS + start + chunk, :] - half
+        high = high_ref[end * SLOTS + start : end * SLOTS + start + chunk, :].astype(F32) - half
         total = jnp.zeros((chunk, TILE), F32)
-        for q in range(HI // 2):
-            found = dot(hot, jnp.concatenate([parts[2 * q], parts[2 * q + 1]], axis=0), NT)
-            total = jnp.where(high == 2.0 * q, found, total)
+        for q in range(HI // 4):
+            found = dot(hot, jnp.concatenate(parts[4 * q : 4 * q + 4], axis=0), NT)
+            total = jnp.where(high == 4.0 * q, found[:, :TILE], total)
+            total = jnp.where(high == 4.0 * q + 2.0, found[:, TILE:], total)
         ends.append(total + pltpu.roll(total, ROWS, 1))
     return jnp.where(lane < ROWS, ends[0], ends[1])
 
@@ -78,7 +89,7 @@
     return jnp.where(lane < ROWS, field.astype(F32), field.astype(F32) * weight).astype(BF16)
 
 
-CHUNK = 256
+CHUNK = 512
 
 
 def gather_payload(x_ref, hot_ref, high_ref, weight_ref, out_ref):
@@ -91,19 +102,20 @@
 
 
 def prepare_kernel(
-    x_ref, rows_ref, target_ref, weight_ref, count_ref, hot_ref, high_ref, spread_ref, out_ref
+    x_ref, rows_ref, target_ref, weight_ref, count_ref, hot_ref, high_ref, across_ref, spread_ref, out_ref
 ):
     live = lax.broadcasted_iota(jnp.int32, (CAP, PEERS), 0) < count_ref[...]
     weight = jnp.where(live, weight_ref[...].astype(F32), 0.0)
     build_tables(
-        rows_ref[...].astype(F32), target_ref[...].astype(F32), weight, hot_ref, high_ref, spread_ref
+        rows_ref[...].astype(F32), target_ref[...].astype(F32), weight, hot_ref, high_ref, across_ref, spread_ref
     )
     gather_payload(x_ref, hot_ref, high_ref, spread_ref, out_ref)
 
 
 TABLE_SHAPES = (
     pltpu.VMEM((3 * SLOTS, SPAN), BF16),
-    pltpu.VMEM((2 * SLOTS, TILE), F32),
+    pltpu.VMEM((2 * SLOTS, TILE), BF16),
+    pltpu.VMEM((ROWS, 2 * SLOTS), BF16),
     jax.ShapeDtypeStruct((SLOTS, TILE), F32),
 )
 
@@ -238,16 +250,13 @@
 SCATTER_SCRATCH = [pltpu.VMEM((HI * ROWS, 2 * SLOTS), BF16), pltpu.VMEM((HI * ROWS, SPAN), F32)]
 
 
-def scatter_into(landed, hot_ref, high_ref, mask_ref, total_ref):
-    turned = landed.astype(F32).T.astype(BF16)
-    high_send = high_ref[0:SLOTS, :].T.astype(BF16)[:ROWS]
-    high_recv = high_ref[SLOTS : 2 * SLOTS, :].T.astype(BF16)[:ROWS]
-    zero = jnp.zeros((ROWS, SLOTS), BF16)
+def scatter_into(landed, hot_ref, across_ref, mask_ref, total_ref):
+    turned = landed.T
+    ends = jnp.concatenate([turned[ROWS:], turned[:ROWS]], axis=1)
+    zero = jnp.zeros_like(ends)
     for h in range(HI):
-        rows = slice(h * ROWS, (h + 1) * ROWS)
-        mask_ref[rows, 0:SLOTS] = jnp.where(high_send == BF16(h), turned[ROWS:], zero)
-        mask_ref[rows, SLOTS : 2 * SLOTS] = jnp.where(high_recv == BF16(h), turned[:ROWS], zero)
-    group = 4
+        mask_ref[h * ROWS : (h + 1) * ROWS, :] = jnp.where(across_ref[...] == BF16(h), ends, zero)
+    group = 2
     for start in range(0, HI, group):
         total_ref[start * ROWS : (start + group) * ROWS, :] = dot(
             mask_ref[start * ROWS : (start + group) * ROWS, :], hot_ref[0 : 2 * SLOTS, :]
@@ -266,11 +275,11 @@
 
 
 def first_kernel(
-    pattern_ref, left_ref, landed_ref, above_ref, below_ref, side_ref, hot_ref, high_ref,
-    v0_ref, weight_ref, local_ref, pairing_ref, down_ref, right_ref,
+    pattern_ref, left_ref, landed_ref, above_ref, below_ref, side_ref, hot_ref, high_ref, across_ref,
+    v0_ref, local_ref, weight_ref, pairing_ref, down_ref, right_ref,
     one_ref, x_ref, mom_ref, top_ref, lower_ref, beside_ref, out_ref, mask_ref, total_ref,
 ):
-    scatter_into(landed_ref[left_ref[1]], hot_ref, high_ref, mask_ref, total_ref)
+    scatter_into(landed_ref[left_ref[1]], hot_ref, across_ref, mask_ref, total_ref)
     for tile in range(TR * TC):
         cols = slice(tile * TILE, (tile + 1) * TILE)
         hop = whole_hop(
@@ -292,9 +301,9 @@
         jax.ShapeDtypeStruct((ROWS, SITES_DEV), BF16),
         jax.ShapeDtypeStruct((2, 4, SITES_DEV), F32),
     ) + EDGE_SHAPES + (jax.ShapeDtypeStruct((2, SLOTS, 2 * ROWS), BF16),)
-    hot, high, weight = tables
-    resident = [on_core(a) for a in (landed, *halo, hot, high)]
-    arrays = (v0, weight, local_part, pairing)
+    hot, high, across, weight = tables
+    resident = [on_core(a) for a in (landed, *halo, hot, high, across)]
+    arrays = (v0, local_part, weight, pairing)
     return pl.pallas_call(
         first_kernel,
         grid=(1,),
@@ -327,11 +336,11 @@
 
 
 def second_kernel(
-    pattern_ref, left_ref, landed_ref, above_ref, below_ref, side_ref, hot_ref, high_ref,
+    pattern_ref, left_ref, landed_ref, above_ref, below_ref, side_ref, hot_ref, across_ref,
     v0_ref, one_ref, local_ref, pairing_ref, mom_in_ref, down_ref, right_ref,
     two_ref, mom_ref, mask_ref, total_ref,
 ):
-    scatter_into(landed_ref[left_ref[1]], hot_ref, high_ref, mask_ref, total_ref)
+    scatter_into(landed_ref[left_ref[1]], hot_ref, across_ref, mask_ref, total_ref)
     mom_ref[0:2] = mom_in_ref[...]
     for tile in range(TR * TC):
         cols = slice(tile * TILE, (tile + 1) * TILE)
@@ -344,12 +353,12 @@
         mom_ref[2, :, cols] = vector_mean(v0 * two)
 
 
-def second(pattern, left_flag, v0, one, landed, hot, high, local_part, pairing, mom, halo, down_hop, right_hop):
+def second(pattern, left_flag, v0, one, landed, hot, across, local_part, pairing, mom, halo, down_hop, right_hop):
     shapes = (
         jax.ShapeDtypeStruct((ROWS, SITES_DEV), F32),
         jax.ShapeDtypeStruct((3, 4, SITES_DEV), F32),
     )
-    resident = [on_core(a) for a in (landed, *halo, hot, high)]
+    resident = [on_core(a) for a in (landed, *halo, hot, across)]
     arrays = (v0, one, local_part, pairing, mom)
     return pl.pallas_call(
         second_kernel,
@@ -405,7 +414,7 @@
         )
 
     *tables, payload = prepare(v0, link_rows, link_target, link_weight, link_count)
-    hot, high, weight = tables
+    hot, _, across, _ = tables
     spread = spread_out(payload)
     halo = halo_of(*edges(pattern, left_flag, v0, down_hop, right_hop))
     local_part = local(pattern, v0, onsite, down_hop, right_hop)
@@ -418,7 +427,7 @@
     local_part = local(pattern, x, onsite, down_hop, right_hop)
     landed, local_part, halo = lax.optimization_barrier((spread, local_part, halo))
     two, mom = second(
-        pattern, left_flag, v0, one, landed, hot, high, local_part, pairing, mom, halo, down_hop, right_hop
+        pattern, left_flag, v0, one, landed, hot, across, local_part, pairing, mom, halo, down_hop, right_hop
     )
     shape = rand_vectors.shape
     return one.reshape(shape), two.reshape(shape), mom

time: 95 us -> 93.5 us (0.984)
  Pallas kernels: 22.7 us -> 21.3 us
where the time goes in v8:
time: 93.5 us; the launch traced here: 92.9 us
  starting transfers between devices  53.5 us (57%)
  Pallas kernels  21.3 us (23%)
  waiting for transfers between devices  16.9 us (18%)
    all_to_all x2, starting transfers between devices, spread_out(): lax.all_to_all(payload.reshape(2 * PEERS, CAP, 2 * ROWS), ('sheet',) + TI...  35 us
    ppermute x4, starting transfers between devices, passed_along(): return lax.ppermute(value, TILE_AXES, pairs)  10.9 us
    ppermute x2, waiting for transfers between devices, halo_of(): lax.ppermute(side_part, 'side', [(0, 1), (1, 0)])  8.83 us
    all_to_all x2, waiting for transfers between devices, spread_out(): lax.all_to_all(payload.reshape(2 * PEERS, CAP, 2 * ROWS), ('sheet',) + TI...  8.05 us
    ppermute x2, starting transfers between devices, halo_of(): lax.ppermute(side_part, 'side', [(0, 1), (1, 0)])  7.56 us
    pallas_call x2, Pallas kernels, local(): pl.pallas_call(local_kernel, in_specs=[SMEM] + [VMEM] * 4, out_shape=jax....  7.11 us
    pallas_call x1, Pallas kernels, first(): pl.pallas_call(first_kernel, grid=(1,), in_specs=[SMEM, SMEM] + [VMEM] *...  4.94 us
    pallas_call x1, Pallas kernels, second(): pl.pallas_call(second_kernel, grid=(1,), in_specs=[SMEM, SMEM] + [VMEM] *...  3.82 us
  transfers between devices with their start and end apart: 8, of which 4 were waited for; matrix products, arithmetic and copies ran while one was open for 1% of the time, Pallas kernels for 10%

profile of v8, /device:TPU:1, one launch (start us, length us, event | category | flops | bytes accessed | tf_op | source)
XLA Modules:
  0.0 92.9 jit_solution(10796406550093942753)
XLA Ops:
  0.6 3.4 %prepare.1 = (bf16[3072,256]{1,0:T(8,128)(2,1)S(1)}, bf16[2048,128]{1,0:T(8,128)(2,1)S(1)}, bf16[64,2048]{1,0:T(8,128)(2,1)S(1)}, f32[1024,128]{1,0:T(8,128)}, bf16[2,1024,128]{2,1,0:T(8,128)(2,1)}) custom-call(bf16[64,3072]{1,0:T(8,128)(2,1)} %bitcast.21, s32[8,128]{1,0:T(8,128)} %bitcast.36, s32[8,128]{1,0:T(8,128)} %bitcast.37, bf16[8,128]{1,0:T(8,128)(2,1)} %bitcast.38, ...), custom_call_target="tpu_custom_call" | custom-call | flops 1000000 | bytes 100000 | tf_op jit(solution)/shard_map/prepare/pallas_call | solution.py:124
  4.0 22.4 %all-to-all-start = ((bf16[256,8,128]{2,1,0:T(8,128)(2,1)}), bf16[256,8,128]{2,1,0:T(8,128)(2,1)S(1)}, u32[]{:S(2)}, u32[]{:S(2)}) async-start(bf16[256,8,128]{2,1,0:T(8,128)(2,1)} %bitcast.27), calls=%async_computation | async-start | bytes 1048576 | tf_op jit(solution)/shard_map/all_to_all | solution.py:386
  26.4 0.6 pad_add_fusion.left_ref
  27.0 2.0 %edges.1 = (bf16[64,768]{1,0:T(8,128)(2,1)}, bf16[64,768]{1,0:T(8,128)(2,1)}, bf16[64,512]{1,0:T(8,128)(2,1)}) custom-call(s32[2,24]{1,0:T(2,128)} %bitcast.31, s32[2]{0:T(128)} %pad_add_fusion.left_ref, bf16[64,3072]{1,0:T(8,128)(2,1)} %bitcast.22, bf16[24,128,128]{2,1,0:T(8,128)(2,1)} %down_ref.9, bf16[4,6,128,128]{3,2,1,0:T(8,128)(2,1)} %bitcast.18), custom_call_target="tpu_custom_call" | custom-call | flops 1000000 | bytes 100000 | tf_op jit(solution)/shard_map/edges/pallas_call | solution.py:173
  29.0 3.5 %collective-permute-start = (bf16[64,768]{1,0:T(8,128)(2,1)}, bf16[64,768]{1,0:T(8,128)(2,1)S(1)}, u32[]{:S(2)}, u32[]{:S(2)}) collective-permute-start(bf16[64,768]{1,0:T(8,128)(2,1)} %get-tuple-element.31), channel_id=1, source_target_pairs={{0,4},{4,8},{8,12},{12,16},{16,20},{20,24},{24,28},{28,32},{32,36}... | collective-permute-start | bytes 294920 | tf_op jit(solution)/shard_map/ppermute | solution.py:382
  32.5 1.9 %collective-permute-start.1 = (bf16[64,768]{1,0:T(8,128)(2,1)}, bf16[64,768]{1,0:T(8,128)(2,1)S(1)}, u32[]{:S(2)}, u32[]{:S(2)}) collective-permute-start(bf16[64,768]{1,0:T(8,128)(2,1)} %get-tuple-element.32), channel_id=1, source_target_pairs={{4,0},{8,4},{12,8},{16,12},{20,16},{24,20},{28,24},{32,28},{36,32}... | collective-permute-start | bytes 294920 | tf_op jit(solution)/shard_map/ppermute | solution.py:382
  34.4 4.0 %collective-permute-start.2 = (bf16[64,512]{1,0:T(8,128)(2,1)}, bf16[64,512]{1,0:T(8,128)(2,1)S(1)}, u32[]{:S(2)}, u32[]{:S(2)}) collective-permute-start(bf16[64,512]{1,0:T(8,128)(2,1)} %get-tuple-element.33), channel_id=1, source_target_pairs={{0,1},{1,0},{2,3},{3,2},{4,5},{5,4},{6,7},{7,6},{8,9},{9,8},{10,11... | collective-permute-start | bytes 196616 | tf_op jit(solution)/shard_map/ppermute | solution.py:413
  38.5 3.5 %local.2.local_ref = f32[64,3072]{1,0:T(8,128)} custom-call(s32[2,24]{1,0:T(2,128)} %bitcast.32, bf16[64,3072]{1,0:T(8,128)(2,1)} %bitcast.23, bf16[24,128,128]{2,1,0:T(8,128)(2,1)} %onsite_ref.3, bf16[24,128,128]{2,1,0:T(8,128)(2,1)} %down_ref.9, bf16[24,128,128]{2,1,0:T(8,128)(2,1)} %right_ref.3), custom_call_target="tpu_custom_call" | custom-call | flops 1000000 | bytes 100000 | tf_op jit(solution)/shard_map/local/pallas_call | solution.py:328
  42.0 3.2 %collective-permute-done.2.side_ref = bf16[64,512]{1,0:T(8,128)(2,1)S(1)} collective-permute-done((bf16[64,512]{1,0:T(8,128)(2,1)}, bf16[64,512]{1,0:T(8,128)(2,1)S(1)}, u32[]{:S(2)}, u32[]{:S(2)}) %collective-permute-start.2) | collective-permute-done | bytes 65568 | tf_op jit(solution)/shard_map/ppermute | solution.py:413
  45.2 0.0 collective-permute-done.above_ref
  45.2 0.0 collective-permute-done.1.below_ref
  45.2 3.9 %all-to-all-done = bf16[256,8,128]{2,1,0:T(8,128)(2,1)S(1)} async-done(((bf16[256,8,128]{2,1,0:T(8,128)(2,1)}), bf16[256,8,128]{2,1,0:T(8,128)(2,1)S(1)}, u32[]{:S(2)}, u32[]{:S(2)}) %all-to-all-start) | async-done | bytes 524320 | tf_op jit(solution)/shard_map/all_to_all | solution.py:386
  49.1 4.9 %first.1 = (f32[64,3072]{1,0:T(8,128)}, bf16[64,3072]{1,0:T(8,128)(2,1)}, f32[2,4,3072]{2,1,0:T(4,128)}, bf16[64,768]{1,0:T(8,128)(2,1)}, bf16[64,768]{1,0:T(8,1...) custom-call(s32[2,24]{1,0:T(2,128)} %bitcast.33, s32[2]{0:T(128)} %pad_add_fusion.left_ref, ...), custom_call_target="tpu_custom_call" | custom-call | flops 1000000 | bytes 100000 | tf_op jit(solution)/shard_map/first/pallas_call | solution.py:307
  54.0 12.6 %all-to-all-start.1 = ((bf16[256,8,128]{2,1,0:T(8,128)(2,1)}), bf16[256,8,128]{2,1,0:T(8,128)(2,1)S(1)}, u32[]{:S(2)}, u32[]{:S(2)}) async-start(bf16[256,8,128]{2,1,0:T(8,128)(2,1)} %bitcast.28), calls=%async_computation.1 | async-start | bytes 1048576 | tf_op jit(solution)/shard_map/all_to_all | solution.py:386
  66.6 3.5 %collective-permute-start.3 = (bf16[64,768]{1,0:T(8,128)(2,1)}, bf16[64,768]{1,0:T(8,128)(2,1)S(1)}, u32[]{:S(2)}, u32[]{:S(2)}) collective-permute-start(bf16[64,768]{1,0:T(8,128)(2,1)} %get-tuple-element.46), channel_id=1, source_target_pairs={{0,4},{4,8},{8,12},{12,16},{16,20},{20,24},{24,28},{28,32},{32,36}... | collective-permute-start | bytes 294920 | tf_op jit(solution)/shard_map/ppermute | solution.py:382
  70.2 1.9 %collective-permute-start.4 = (bf16[64,768]{1,0:T(8,128)(2,1)}, bf16[64,768]{1,0:T(8,128)(2,1)S(1)}, u32[]{:S(2)}, u32[]{:S(2)}) collective-permute-start(bf16[64,768]{1,0:T(8,128)(2,1)} %get-tuple-element.47), channel_id=1, source_target_pairs={{4,0},{8,4},{12,8},{16,12},{20,16},{24,20},{28,24},{32,28},{36,32}... | collective-permute-start | bytes 294920 | tf_op jit(solution)/shard_map/ppermute | solution.py:382
  72.1 3.6 %collective-permute-start.5 = (bf16[64,512]{1,0:T(8,128)(2,1)}, bf16[64,512]{1,0:T(8,128)(2,1)S(1)}, u32[]{:S(2)}, u32[]{:S(2)}) collective-permute-start(bf16[64,512]{1,0:T(8,128)(2,1)} %get-tuple-element.48), channel_id=1, source_target_pairs={{0,1},{1,0},{2,3},{3,2},{4,5},{5,4},{6,7},{7,6},{8,9},{9,8},{10,11... | collective-permute-start | bytes 196616 | tf_op jit(solution)/shard_map/ppermute | solution.py:413
  75.7 3.6 %local.3.local_ref = f32[64,3072]{1,0:T(8,128)} custom-call(s32[2,24]{1,0:T(2,128)} %bitcast.34, bf16[64,3072]{1,0:T(8,128)(2,1)} %get-tuple-element.45.x_ref, bf16[24,128,128]{2,1,0:T(8,128)(2,1)} %onsite_ref.3, bf16[24,128,128]{2,1,0:T(8,128)(2,1)} %down_ref.9, bf16[24,128,128]{2,1,0:T(8,128)(2,1)} %right_ref.3), custom_call_target="tpu_custom_call" | custom-call | flops 1000000 | bytes 100000 | tf_op jit(solution)/shard_map/local/pallas_call | solution.py:328
  79.2 5.6 %collective-permute-done.5.side_ref = bf16[64,512]{1,0:T(8,128)(2,1)S(1)} collective-permute-done((bf16[64,512]{1,0:T(8,128)(2,1)}, bf16[64,512]{1,0:T(8,128)(2,1)S(1)}, u32[]{:S(2)}, u32[]{:S(2)}) %collective-permute-start.5) | collective-permute-done | bytes 65568 | tf_op jit(solution)/shard_map/ppermute | solution.py:413
  84.9 0.0 collective-permute-done.3.above_ref
  84.9 0.0 collective-permute-done.4.below_ref
  84.9 4.2 %all-to-all-done.1 = bf16[256,8,128]{2,1,0:T(8,128)(2,1)S(1)} async-done(((bf16[256,8,128]{2,1,0:T(8,128)(2,1)}), bf16[256,8,128]{2,1,0:T(8,128)(2,1)S(1)}, u32[]{:S(2)}, u32[]{:S(2)}) %all-to-all-start.1) | async-done | bytes 524320 | tf_op jit(solution)/shard_map/all_to_all | solution.py:386
  89.1 3.8 %second.1 = (f32[64,3072]{1,0:T(8,128)}, f32[3,4,3072]{2,1,0:T(4,128)}) custom-call(s32[2,24]{1,0:T(2,128)} %bitcast.35, s32[2]{0:T(128)} %pad_add_fusion.left_ref, bf16[2,1024,128]{2,1,0:T(8,128)(2,1)S(1)} %bitcast.17, bf16[64,768]{1,0:T(8,128)(2,1)S(1)} %collective-permute-done.3.above_ref, bf16[64,768]{1,0:T(8,128)(2,1)S(1)} %collective-permute-done.4.below_ref, ...), custom_call_target="tpu_custom_call" | custom-call | flops 1000000 | bytes 100000 | tf_op jit(solution)/shard_map/second/pallas_call | solution.py:363
Async XLA Ops:
  4.0 45.0 %all-to-all-start = ((bf16[256,8,128]{2,1,0:T(8,128)(2,1)}), bf16[256,8,128]{2,1,0:T(8,128)(2,1)S(1)}, u32[]{:S(2)}, u32[]{:S(2)}) async-start(bf16[256,8,128]{2,1,0:T(8,128)(2,1)} %bitcast.27), calls=%async_computation | async-start | bytes 1048576 | tf_op jit(solution)/shard_map/all_to_all | solution.py:386
  29.0 16.2 %collective-permute-start = (bf16[64,768]{1,0:T(8,128)(2,1)}, bf16[64,768]{1,0:T(8,128)(2,1)S(1)}, u32[]{:S(2)}, u32[]{:S(2)}) collective-permute-start(bf16[64,768]{1,0:T(8,128)(2,1)} %get-tuple-element.31), channel_id=1, source_target_pairs={{0,4},{4,8},{8,12},{12,16},{16,20},{20,24},{24,28},{28,32},{32,36}... | collective-permute-start | bytes 294920 | tf_op jit(solution)/shard_map/ppermute | solution.py:382
  32.5 12.7 %collective-permute-start.1 = (bf16[64,768]{1,0:T(8,128)(2,1)}, bf16[64,768]{1,0:T(8,128)(2,1)S(1)}, u32[]{:S(2)}, u32[]{:S(2)}) collective-permute-start(bf16[64,768]{1,0:T(8,128)(2,1)} %get-tuple-element.32), channel_id=1, source_target_pairs={{4,0},{8,4},{12,8},{16,12},{20,16},{24,20},{28,24},{32,28},{36,32}... | collective-permute-start | bytes 294920 | tf_op jit(solution)/shard_map/ppermute | solution.py:382
  34.4 10.8 %collective-permute-start.2 = (bf16[64,512]{1,0:T(8,128)(2,1)}, bf16[64,512]{1,0:T(8,128)(2,1)S(1)}, u32[]{:S(2)}, u32[]{:S(2)}) collective-permute-start(bf16[64,512]{1,0:T(8,128)(2,1)} %get-tuple-element.33), channel_id=1, source_target_pairs={{0,1},{1,0},{2,3},{3,2},{4,5},{5,4},{6,7},{7,6},{8,9},{9,8},{10,11... | collective-permute-start | bytes 196616 | tf_op jit(solution)/shard_map/ppermute | solution.py:413
  54.0 35.1 %all-to-all-start.1 = ((bf16[256,8,128]{2,1,0:T(8,128)(2,1)}), bf16[256,8,128]{2,1,0:T(8,128)(2,1)S(1)}, u32[]{:S(2)}, u32[]{:S(2)}) async-start(bf16[256,8,128]{2,1,0:T(8,128)(2,1)} %bitcast.28), calls=%async_computation.1 | async-start | bytes 1048576 | tf_op jit(solution)/shard_map/all_to_all | solution.py:386
  66.6 18.2 %collective-permute-start.3 = (bf16[64,768]{1,0:T(8,128)(2,1)}, bf16[64,768]{1,0:T(8,128)(2,1)S(1)}, u32[]{:S(2)}, u32[]{:S(2)}) collective-permute-start(bf16[64,768]{1,0:T(8,128)(2,1)} %get-tuple-element.46), channel_id=1, source_target_pairs={{0,4},{4,8},{8,12},{12,16},{16,20},{20,24},{24,28},{28,32},{32,36}... | collective-permute-start | bytes 294920 | tf_op jit(solution)/shard_map/ppermute | solution.py:382
  70.2 14.7 %collective-permute-start.4 = (bf16[64,768]{1,0:T(8,128)(2,1)}, bf16[64,768]{1,0:T(8,128)(2,1)S(1)}, u32[]{:S(2)}, u32[]{:S(2)}) collective-permute-start(bf16[64,768]{1,0:T(8,128)(2,1)} %get-tuple-element.47), channel_id=1, source_target_pairs={{4,0},{8,4},{12,8},{16,12},{20,16},{24,20},{28,24},{32,28},{36,32}... | collective-permute-start | bytes 294920 | tf_op jit(solution)/shard_map/ppermute | solution.py:382
  72.1 12.8 %collective-permute-start.5 = (bf16[64,512]{1,0:T(8,128)(2,1)}, bf16[64,512]{1,0:T(8,128)(2,1)S(1)}, u32[]{:S(2)}, u32[]{:S(2)}) collective-permute-start(bf16[64,512]{1,0:T(8,128)(2,1)} %get-tuple-element.48), channel_id=1, source_target_pairs={{0,1},{1,0},{2,3},{3,2},{4,5},{5,4},{6,7},{7,6},{8,9},{9,8},{10,11... | collective-permute-start | bytes 196616 | tf_op jit(solution)/shard_map/ppermute | solution.py:413

commit v9 on v8

--- a/solution.py
+++ b/solution.py
@@ -101,33 +101,12 @@
         out_ref[1, start : start + CHUNK, :] = payload
 
 
-def prepare_kernel(
-    x_ref, rows_ref, target_ref, weight_ref, count_ref, hot_ref, high_ref, across_ref, spread_ref, out_ref
-):
-    live = lax.broadcasted_iota(jnp.int32, (CAP, PEERS), 0) < count_ref[...]
-    weight = jnp.where(live, weight_ref[...].astype(F32), 0.0)
-    build_tables(
-        rows_ref[...].astype(F32), target_ref[...].astype(F32), weight, hot_ref, high_ref, across_ref, spread_ref
-    )
-    gather_payload(x_ref, hot_ref, high_ref, spread_ref, out_ref)
-
-
 TABLE_SHAPES = (
     pltpu.VMEM((3 * SLOTS, SPAN), BF16),
     pltpu.VMEM((2 * SLOTS, TILE), BF16),
     pltpu.VMEM((ROWS, 2 * SLOTS), BF16),
     jax.ShapeDtypeStruct((SLOTS, TILE), F32),
 )
-
-
-def prepare(x, link_rows, link_target, link_weight, link_count):
-    return pl.pallas_call(
-        prepare_kernel,
-        out_shape=TABLE_SHAPES + (jax.ShapeDtypeStruct((2, SLOTS, 2 * ROWS), BF16),),
-        compiler_params=params(),
-        cost_estimate=COST,
-        name="prepare",
-    )(x, link_rows.T, link_target.T, link_weight.T, link_count.reshape(1, PEERS))
 
 
 def write_edges(pattern_ref, left_ref, x_ref, down_ref, right_ref, down_base, top_ref, below_ref, side_ref):
@@ -137,17 +116,13 @@
         keep = pattern_ref[0, tile].astype(F32)
         product = keep * dot(x_ref[:, tile * TILE : (tile + 1) * TILE], down_ref[down_base + k])
         below_ref[:, k * TILE : (k + 1) * TILE] = product.astype(BF16)
-    is_left = left_ref[0] == 1
+    is_left = (left_ref[0] & 1) == 1
     for r in range(TR):
         last = r * TC + TC - 1
         keep = pattern_ref[1, last].astype(F32)
         product = keep * dot(x_ref[:, last * TILE : (last + 1) * TILE], right_ref[r, 0])
         first_tile = x_ref[:, r * TC * TILE : (r * TC + 1) * TILE]
         side_ref[:, r * TILE : (r + 1) * TILE] = jnp.where(is_left, product.astype(BF16), first_tile)
-
-
-def edges_kernel(pattern_ref, left_ref, x_ref, down_ref, right_ref, top_ref, below_ref, side_ref):
-    write_edges(pattern_ref, left_ref, x_ref, down_ref, right_ref, 0, top_ref, below_ref, side_ref)
 
 
 EDGE_SHAPES = (
@@ -169,17 +144,33 @@
     return pltpu.with_memory_space_constraint(value, pltpu.VMEM)
 
 
-def edges(pattern, left_flag, x, down_hop, right_hop):
+def prepare_kernel(
+    pattern_ref, left_ref, x_ref, rows_ref, target_ref, weight_ref, count_ref, down_ref, right_ref,
+    hot_ref, high_ref, across_ref, spread_ref, top_ref, below_ref, side_ref, out_ref,
+):
+    live = lax.broadcasted_iota(jnp.int32, (CAP, PEERS), 0) < count_ref[...]
+    weight = jnp.where(live, weight_ref[...].astype(F32), 0.0)
+    build_tables(
+        rows_ref[...].astype(F32), target_ref[...].astype(F32), weight, hot_ref, high_ref, across_ref, spread_ref
+    )
+    gather_payload(x_ref, hot_ref, high_ref, spread_ref, out_ref)
+    write_edges(pattern_ref, left_ref, x_ref, down_ref, right_ref, 0, top_ref, below_ref, side_ref)
+
+
+def prepare(pattern, left_flag, x, link_rows, link_target, link_weight, link_count, down_hop, right_hop):
+    arrays = (x, link_rows.T, link_target.T, link_weight.T, link_count.reshape(1, PEERS))
+    shapes = TABLE_SHAPES + EDGE_SHAPES + (jax.ShapeDtypeStruct((2, SLOTS, 2 * ROWS), BF16),)
+    resident = len(TABLE_SHAPES) - 1
     return pl.pallas_call(
-        edges_kernel,
+        prepare_kernel,
         grid=(1,),
-        in_specs=[SMEM, SMEM, whole((ROWS, SITES_DEV)), DOWN_EDGE, RIGHT_EDGE],
-        out_specs=tuple(whole(s.shape) for s in EDGE_SHAPES),
-        out_shape=EDGE_SHAPES,
+        in_specs=[SMEM, SMEM] + [whole(a.shape) for a in arrays] + [DOWN_EDGE, RIGHT_EDGE],
+        out_specs=(VMEM,) * resident + tuple(whole(s.shape) for s in shapes[resident:]),
+        out_shape=shapes,
         compiler_params=params(),
         cost_estimate=COST,
-        name="edges",
-    )(pattern, left_flag, x, down_hop, right_hop.reshape(TR, TC, TILE, TILE))
+        name="prepare",
+    )(pattern, left_flag, *arrays, down_hop, right_hop.reshape(TR, TC, TILE, TILE))
 
 
 def kept(pattern_ref, which, tile, value):
@@ -268,7 +259,7 @@
     hop = local_ref[:, tile * TILE : (tile + 1) * TILE]
     hop = hop + total_ref[h * ROWS : (h + 1) * ROWS, part * TILE : (part + 1) * TILE]
     halo = halo_tile(
-        pattern_ref, left_ref[0] == 1, lambda k: down_ref[k], lambda r: right_ref[r, 0],
+        pattern_ref, (left_ref[0] & 1) == 1, lambda k: down_ref[k], lambda r: right_ref[r, 0],
         above_ref, below_ref, side_ref, tile,
     )
     return hop if halo is None else hop + halo
@@ -279,7 +270,7 @@
     v0_ref, local_ref, weight_ref, pairing_ref, down_ref, right_ref,
     one_ref, x_ref, mom_ref, top_ref, lower_ref, beside_ref, out_ref, mask_ref, total_ref,
 ):
-    scatter_into(landed_ref[left_ref[1]], hot_ref, across_ref, mask_ref, total_ref)
+    scatter_into(landed_ref[left_ref[0] >> 1], hot_ref, across_ref, mask_ref, total_ref)
     for tile in range(TR * TC):
         cols = slice(tile * TILE, (tile + 1) * TILE)
         hop = whole_hop(
@@ -340,7 +331,7 @@
     v0_ref, one_ref, local_ref, pairing_ref, mom_in_ref, down_ref, right_ref,
     two_ref, mom_ref, mask_ref, total_ref,
 ):
-    scatter_into(landed_ref[left_ref[1]], hot_ref, across_ref, mask_ref, total_ref)
+    scatter_into(landed_ref[left_ref[0] >> 1], hot_ref, across_ref, mask_ref, total_ref)
     mom_ref[0:2] = mom_in_ref[...]
     for tile in range(TR * TC):
         cols = slice(tile * TILE, (tile + 1) * TILE)
@@ -404,7 +395,7 @@
     v0 = rand_vectors.reshape(ROWS, SITES_DEV)
     pairing = pairing.reshape(1, SITES_DEV)
     pattern = pattern.T
-    left_flag = jnp.stack([1 - lax.axis_index("side"), 1 - lax.axis_index("sheet")]).astype(jnp.int32)
+    left_flag = (3 - lax.axis_index("side") - 2 * lax.axis_index("sheet")).astype(jnp.int32).reshape(1)
 
     def halo_of(top, below_part, side_part):
         return (
@@ -413,10 +404,13 @@
             lax.ppermute(side_part, "side", [(0, 1), (1, 0)]),
         )
 
-    *tables, payload = prepare(v0, link_rows, link_target, link_weight, link_count)
+    made = prepare(
+        pattern, left_flag, v0, link_rows, link_target, link_weight, link_count, down_hop, right_hop
+    )
+    tables, edge_parts, payload = made[:4], made[4:7], made[7]
     hot, _, across, _ = tables
     spread = spread_out(payload)
-    halo = halo_of(*edges(pattern, left_flag, v0, down_hop, right_hop))
+    halo = halo_of(*edge_parts)
     local_part = local(pattern, v0, onsite, down_hop, right_hop)
     landed, local_part, halo = lax.optimization_barrier((spread, local_part, halo))
     one, x, mom, *edge_parts, payload = first(

time: 93.5 us -> 91.4 us (0.978)
  waiting for transfers between devices: 16.9 us -> 19.7 us
  starting transfers between devices: 53.5 us -> 50.9 us
  Pallas kernels: 21.3 us -> 19.6 us
    all_to_all x2, starting transfers between devices: 35 us -> 32.6 us  [spread_out(): lax.all_to_all(payload.reshape(2 * PEERS, CAP, 2 * ROWS), ('sheet',) + TI...]
    ppermute x2, waiting for transfers between devices: 8.83 us -> 11.3 us  [halo_of(): lax.ppermute(side_part, 'side', [(0, 1), (1, 0)])]
    pallas_call x2 -> x1, Pallas kernels: 5.39 us -> 3.76 us  [prepare(): pl.pallas_call(prepare_kernel, grid=(1,), in_specs=[SMEM, SMEM] + [whole(...]
  transfers between devices with their start and end apart: 8 -> 8, of which waited for: 4 -> 4; matrix products, arithmetic and copies ran while one was open for 1% -> 0% of each run, Pallas kernels for 10% -> 8%
where the time goes in v9:
time: 91.4 us; the launch traced here: 90.9 us
  starting transfers between devices  50.9 us (56%)
  waiting for transfers between devices  19.7 us (22%)
  Pallas kernels  19.6 us (21%)
    all_to_all x2, starting transfers between devices, spread_out(): lax.all_to_all(payload.reshape(2 * PEERS, CAP, 2 * ROWS), ('sheet',) + TI...  32.6 us
    ppermute x2, waiting for transfers between devices, halo_of(): lax.ppermute(side_part, 'side', [(0, 1), (1, 0)])  11.3 us
    ppermute x4, starting transfers between devices, passed_along(): return lax.ppermute(value, TILE_AXES, pairs)  10.9 us
    all_to_all x2, waiting for transfers between devices, spread_out(): lax.all_to_all(payload.reshape(2 * PEERS, CAP, 2 * ROWS), ('sheet',) + TI...  8.44 us
    ppermute x2, starting transfers between devices, halo_of(): lax.ppermute(side_part, 'side', [(0, 1), (1, 0)])  7.37 us
    pallas_call x2, Pallas kernels, local(): pl.pallas_call(local_kernel, in_specs=[SMEM] + [VMEM] * 4, out_shape=jax....  7.09 us
    pallas_call x1, Pallas kernels, first(): pl.pallas_call(first_kernel, grid=(1,), in_specs=[SMEM, SMEM] + [VMEM] *...  4.94 us
    pallas_call x1, Pallas kernels, second(): pl.pallas_call(second_kernel, grid=(1,), in_specs=[SMEM, SMEM] + [VMEM] *...  3.81 us
  transfers between devices with their start and end apart: 8, of which 4 were waited for; matrix products, arithmetic and copies ran while one was open for 0% of the time, Pallas kernels for 8%

profile of v9, /device:TPU:1, one launch (start us, length us, event | category | flops | bytes accessed | tf_op | source)
XLA Modules:
  0.0 90.9 jit_solution(10505485077528436402)
XLA Ops:
  0.6 3.8 %prepare.1 = (bf16[3072,256]{1,0:T(8,128)(2,1)S(1)}, bf16[2048,128]{1,0:T(8,128)(2,1)S(1)}, bf16[64,2048]{1,0:T(8,128)(2,1)S(1)}, f32[1024,128]{1,0:T(8,128)}, b...) custom-call(s32[2,24]{1,0:T(2,128)} %bitcast.29, ...), custom_call_target="tpu_custom_call" | custom-call | flops 1000000 | bytes 100000 | tf_op jit(solution)/shard_map/prepare/pallas_call | solution.py:164
  4.4 22.4 %all-to-all-start = ((bf16[256,8,128]{2,1,0:T(8,128)(2,1)}), bf16[256,8,128]{2,1,0:T(8,128)(2,1)S(1)}, u32[]{:S(2)}, u32[]{:S(2)}) async-start(bf16[256,8,128]{2,1,0:T(8,128)(2,1)} %bitcast.26), calls=%async_computation | async-start | bytes 1048576 | tf_op jit(solution)/shard_map/all_to_all | solution.py:377
  26.8 3.5 %collective-permute-start = (bf16[64,768]{1,0:T(8,128)(2,1)}, bf16[64,768]{1,0:T(8,128)(2,1)S(1)}, u32[]{:S(2)}, u32[]{:S(2)}) collective-permute-start(bf16[64,768]{1,0:T(8,128)(2,1)} %get-tuple-element.31), channel_id=1, source_target_pairs={{0,4},{4,8},{8,12},{12,16},{16,20},{20,24},{24,28},{28,32},{32,36}... | collective-permute-start | bytes 294920 | tf_op jit(solution)/shard_map/ppermute | solution.py:373
  30.3 1.9 %collective-permute-start.1 = (bf16[64,768]{1,0:T(8,128)(2,1)}, bf16[64,768]{1,0:T(8,128)(2,1)S(1)}, u32[]{:S(2)}, u32[]{:S(2)}) collective-permute-start(bf16[64,768]{1,0:T(8,128)(2,1)} %get-tuple-element.32), channel_id=1, source_target_pairs={{4,0},{8,4},{12,8},{16,12},{20,16},{24,20},{28,24},{32,28},{36,32}... | collective-permute-start | bytes 294920 | tf_op jit(solution)/shard_map/ppermute | solution.py:373
  32.2 4.0 %collective-permute-start.2 = (bf16[64,512]{1,0:T(8,128)(2,1)}, bf16[64,512]{1,0:T(8,128)(2,1)S(1)}, u32[]{:S(2)}, u32[]{:S(2)}) collective-permute-start(bf16[64,512]{1,0:T(8,128)(2,1)} %get-tuple-element.33), channel_id=1, source_target_pairs={{0,1},{1,0},{2,3},{3,2},{4,5},{5,4},{6,7},{7,6},{8,9},{9,8},{10,11... | collective-permute-start | bytes 196616 | tf_op jit(solution)/shard_map/ppermute | solution.py:404
  36.2 3.5 %local.2.local_ref = f32[64,3072]{1,0:T(8,128)} custom-call(s32[2,24]{1,0:T(2,128)} %bitcast.30, bf16[64,3072]{1,0:T(8,128)(2,1)} %bitcast.21, bf16[24,128,128]{2,1,0:T(8,128)(2,1)} %onsite_ref.3, bf16[24,128,128]{2,1,0:T(8,128)(2,1)} %down_ref.9, bf16[24,128,128]{2,1,0:T(8,128)(2,1)} %right_ref.3), custom_call_target="tpu_custom_call" | custom-call | flops 1000000 | bytes 100000 | tf_op jit(solution)/shard_map/local/pallas_call | solution.py:319
  39.8 6.0 %collective-permute-done.2.side_ref = bf16[64,512]{1,0:T(8,128)(2,1)S(1)} collective-permute-done((bf16[64,512]{1,0:T(8,128)(2,1)}, bf16[64,512]{1,0:T(8,128)(2,1)S(1)}, u32[]{:S(2)}, u32[]{:S(2)}) %collective-permute-start.2) | collective-permute-done | bytes 65568 | tf_op jit(solution)/shard_map/ppermute | solution.py:404
  45.7 0.0 collective-permute-done.above_ref
  45.8 0.0 collective-permute-done.1.below_ref
  45.8 3.7 %all-to-all-done = bf16[256,8,128]{2,1,0:T(8,128)(2,1)S(1)} async-done(((bf16[256,8,128]{2,1,0:T(8,128)(2,1)}), bf16[256,8,128]{2,1,0:T(8,128)(2,1)S(1)}, u32[]{:S(2)}, u32[]{:S(2)}) %all-to-all-start) | async-done | bytes 524320 | tf_op jit(solution)/shard_map/all_to_all | solution.py:377
  49.5 4.9 %first.1 = (f32[64,3072]{1,0:T(8,128)}, bf16[64,3072]{1,0:T(8,128)(2,1)}, f32[2,4,3072]{2,1,0:T(4,128)}, bf16[64,768]{1,0:T(8,128)(2,1)}, bf16[64,768]{1,0:T(8,1...) custom-call(s32[2,24]{1,0:T(2,128)} %bitcast.31, s32[1]{0:T(128)} %bitcast.1.left_ref, ...), custom_call_target="tpu_custom_call" | custom-call | flops 1000000 | bytes 100000 | tf_op jit(solution)/shard_map/first/pallas_call | solution.py:298
  54.4 10.2 %all-to-all-start.1 = ((bf16[256,8,128]{2,1,0:T(8,128)(2,1)}), bf16[256,8,128]{2,1,0:T(8,128)(2,1)S(1)}, u32[]{:S(2)}, u32[]{:S(2)}) async-start(bf16[256,8,128]{2,1,0:T(8,128)(2,1)} %bitcast.25), calls=%async_computation.1 | async-start | bytes 1048576 | tf_op jit(solution)/shard_map/all_to_all | solution.py:377
  64.6 3.5 %collective-permute-start.3 = (bf16[64,768]{1,0:T(8,128)(2,1)}, bf16[64,768]{1,0:T(8,128)(2,1)S(1)}, u32[]{:S(2)}, u32[]{:S(2)}) collective-permute-start(bf16[64,768]{1,0:T(8,128)(2,1)} %get-tuple-element.46), channel_id=1, source_target_pairs={{0,4},{4,8},{8,12},{12,16},{16,20},{20,24},{24,28},{28,32},{32,36}... | collective-permute-start | bytes 294920 | tf_op jit(solution)/shard_map/ppermute | solution.py:373
  68.2 1.9 %collective-permute-start.4 = (bf16[64,768]{1,0:T(8,128)(2,1)}, bf16[64,768]{1,0:T(8,128)(2,1)S(1)}, u32[]{:S(2)}, u32[]{:S(2)}) collective-permute-start(bf16[64,768]{1,0:T(8,128)(2,1)} %get-tuple-element.47), channel_id=1, source_target_pairs={{4,0},{8,4},{12,8},{16,12},{20,16},{24,20},{28,24},{32,28},{36,32}... | collective-permute-start | bytes 294920 | tf_op jit(solution)/shard_map/ppermute | solution.py:373
  70.1 3.4 %collective-permute-start.5 = (bf16[64,512]{1,0:T(8,128)(2,1)}, bf16[64,512]{1,0:T(8,128)(2,1)S(1)}, u32[]{:S(2)}, u32[]{:S(2)}) collective-permute-start(bf16[64,512]{1,0:T(8,128)(2,1)} %get-tuple-element.48), channel_id=1, source_target_pairs={{0,1},{1,0},{2,3},{3,2},{4,5},{5,4},{6,7},{7,6},{8,9},{9,8},{10,11... | collective-permute-start | bytes 196616 | tf_op jit(solution)/shard_map/ppermute | solution.py:404
  73.5 3.6 %local.3.local_ref = f32[64,3072]{1,0:T(8,128)} custom-call(s32[2,24]{1,0:T(2,128)} %bitcast.32, bf16[64,3072]{1,0:T(8,128)(2,1)} %get-tuple-element.45.x_ref, bf16[24,128,128]{2,1,0:T(8,128)(2,1)} %onsite_ref.3, bf16[24,128,128]{2,1,0:T(8,128)(2,1)} %down_ref.9, bf16[24,128,128]{2,1,0:T(8,128)(2,1)} %right_ref.3), custom_call_target="tpu_custom_call" | custom-call | flops 1000000 | bytes 100000 | tf_op jit(solution)/shard_map/local/pallas_call | solution.py:319
  77.0 5.3 %collective-permute-done.5.side_ref = bf16[64,512]{1,0:T(8,128)(2,1)S(1)} collective-permute-done((bf16[64,512]{1,0:T(8,128)(2,1)}, bf16[64,512]{1,0:T(8,128)(2,1)S(1)}, u32[]{:S(2)}, u32[]{:S(2)}) %collective-permute-start.5) | collective-permute-done | bytes 65568 | tf_op jit(solution)/shard_map/ppermute | solution.py:404
  82.3 0.0 collective-permute-done.3.above_ref
  82.3 0.0 collective-permute-done.4.below_ref
  82.3 4.7 %all-to-all-done.1 = bf16[256,8,128]{2,1,0:T(8,128)(2,1)S(1)} async-done(((bf16[256,8,128]{2,1,0:T(8,128)(2,1)}), bf16[256,8,128]{2,1,0:T(8,128)(2,1)S(1)}, u32[]{:S(2)}, u32[]{:S(2)}) %all-to-all-start.1) | async-done | bytes 524320 | tf_op jit(solution)/shard_map/all_to_all | solution.py:377
  87.1 3.8 %second.1 = (f32[64,3072]{1,0:T(8,128)}, f32[3,4,3072]{2,1,0:T(4,128)}) custom-call(s32[2,24]{1,0:T(2,128)} %bitcast.33, s32[1]{0:T(128)} %bitcast.1.left_ref, bf16[2,1024,128]{2,1,0:T(8,128)(2,1)S(1)} %bitcast.16, bf16[64,768]{1,0:T(8,128)(2,1)S(1)} %collective-permute-done.3.above_ref, bf16[64,768]{1,0:T(8,128)(2,1)S(1)} %collective-permute-done.4.below_ref, ...), custom_call_target="tpu_custom_call" | custom-call | flops 1000000 | bytes 100000 | tf_op jit(solution)/shard_map/second/pallas_call | solution.py:354
Async XLA Ops:
  4.4 45.1 %all-to-all-start = ((bf16[256,8,128]{2,1,0:T(8,128)(2,1)}), bf16[256,8,128]{2,1,0:T(8,128)(2,1)S(1)}, u32[]{:S(2)}, u32[]{:S(2)}) async-start(bf16[256,8,128]{2,1,0:T(8,128)(2,1)} %bitcast.26), calls=%async_computation | async-start | bytes 1048576 | tf_op jit(solution)/shard_map/all_to_all | solution.py:377
  26.8 19.0 %collective-permute-start = (bf16[64,768]{1,0:T(8,128)(2,1)}, bf16[64,768]{1,0:T(8,128)(2,1)S(1)}, u32[]{:S(2)}, u32[]{:S(2)}) collective-permute-start(bf16[64,768]{1,0:T(8,128)(2,1)} %get-tuple-element.31), channel_id=1, source_target_pairs={{0,4},{4,8},{8,12},{12,16},{16,20},{20,24},{24,28},{28,32},{32,36}... | collective-permute-start | bytes 294920 | tf_op jit(solution)/shard_map/ppermute | solution.py:373
  30.3 15.4 %collective-permute-start.1 = (bf16[64,768]{1,0:T(8,128)(2,1)}, bf16[64,768]{1,0:T(8,128)(2,1)S(1)}, u32[]{:S(2)}, u32[]{:S(2)}) collective-permute-start(bf16[64,768]{1,0:T(8,128)(2,1)} %get-tuple-element.32), channel_id=1, source_target_pairs={{4,0},{8,4},{12,8},{16,12},{20,16},{24,20},{28,24},{32,28},{36,32}... | collective-permute-start | bytes 294920 | tf_op jit(solution)/shard_map/ppermute | solution.py:373
  32.2 13.5 %collective-permute-start.2 = (bf16[64,512]{1,0:T(8,128)(2,1)}, bf16[64,512]{1,0:T(8,128)(2,1)S(1)}, u32[]{:S(2)}, u32[]{:S(2)}) collective-permute-start(bf16[64,512]{1,0:T(8,128)(2,1)} %get-tuple-element.33), channel_id=1, source_target_pairs={{0,1},{1,0},{2,3},{3,2},{4,5},{5,4},{6,7},{7,6},{8,9},{9,8},{10,11... | collective-permute-start | bytes 196616 | tf_op jit(solution)/shard_map/ppermute | solution.py:404
  54.4 32.6 %all-to-all-start.1 = ((bf16[256,8,128]{2,1,0:T(8,128)(2,1)}), bf16[256,8,128]{2,1,0:T(8,128)(2,1)S(1)}, u32[]{:S(2)}, u32[]{:S(2)}) async-start(bf16[256,8,128]{2,1,0:T(8,128)(2,1)} %bitcast.25), calls=%async_computation.1 | async-start | bytes 1048576 | tf_op jit(solution)/shard_map/all_to_all | solution.py:377
  64.6 17.7 %collective-permute-start.3 = (bf16[64,768]{1,0:T(8,128)(2,1)}, bf16[64,768]{1,0:T(8,128)(2,1)S(1)}, u32[]{:S(2)}, u32[]{:S(2)}) collective-permute-start(bf16[64,768]{1,0:T(8,128)(2,1)} %get-tuple-element.46), channel_id=1, source_target_pairs={{0,4},{4,8},{8,12},{12,16},{16,20},{20,24},{24,28},{28,32},{32,36}... | collective-permute-start | bytes 294920 | tf_op jit(solution)/shard_map/ppermute | solution.py:373
  68.2 14.2 %collective-permute-start.4 = (bf16[64,768]{1,0:T(8,128)(2,1)}, bf16[64,768]{1,0:T(8,128)(2,1)S(1)}, u32[]{:S(2)}, u32[]{:S(2)}) collective-permute-start(bf16[64,768]{1,0:T(8,128)(2,1)} %get-tuple-element.47), channel_id=1, source_target_pairs={{4,0},{8,4},{12,8},{16,12},{20,16},{24,20},{28,24},{32,28},{36,32}... | collective-permute-start | bytes 294920 | tf_op jit(solution)/shard_map/ppermute | solution.py:373
  70.1 12.2 %collective-permute-start.5 = (bf16[64,512]{1,0:T(8,128)(2,1)}, bf16[64,512]{1,0:T(8,128)(2,1)S(1)}, u32[]{:S(2)}, u32[]{:S(2)}) collective-permute-start(bf16[64,512]{1,0:T(8,128)(2,1)} %get-tuple-element.48), channel_id=1, source_target_pairs={{0,1},{1,0},{2,3},{3,2},{4,5},{5,4},{6,7},{7,6},{8,9},{9,8},{10,11... | collective-permute-start | bytes 196616 | tf_op jit(solution)/shard_map/ppermute | solution.py:404

commit v10 on v9

--- a/solution.py
+++ b/solution.py
@@ -247,7 +247,7 @@
     zero = jnp.zeros_like(ends)
     for h in range(HI):
         mask_ref[h * ROWS : (h + 1) * ROWS, :] = jnp.where(across_ref[...] == BF16(h), ends, zero)
-    group = 2
+    group = 1
     for start in range(0, HI, group):
         total_ref[start * ROWS : (start + group) * ROWS, :] = dot(
             mask_ref[start * ROWS : (start + group) * ROWS, :], hot_ref[0 : 2 * SLOTS, :]

time: 91.4 us -> 93.5 us (1.023)
  Pallas kernels: 19.6 us -> 21.6 us
    pallas_call x1, Pallas kernels: 4.94 us -> 6.26 us  [first(): pl.pallas_call(first_kernel, grid=(1,), in_specs=[SMEM, SMEM] + [VMEM] *...]
where the time goes in v10:
time: 93.5 us; the launch traced here: 92.9 us
  starting transfers between devices  50.9 us (54%)
  Pallas kernels  21.6 us (23%)
  waiting for transfers between devices  19.7 us (21%)
    all_to_all x2, starting transfers between devices, spread_out(): lax.all_to_all(payload.reshape(2 * PEERS, CAP, 2 * ROWS), ('sheet',) + TI...  32.6 us
    ppermute x2, waiting for transfers between devices, halo_of(): lax.ppermute(side_part, 'side', [(0, 1), (1, 0)])  11.3 us
    ppermute x4, starting transfers between devices, passed_along(): return lax.ppermute(value, TILE_AXES, pairs)  10.9 us
    all_to_all x2, waiting for transfers between devices, spread_out(): lax.all_to_all(payload.reshape(2 * PEERS, CAP, 2 * ROWS), ('sheet',) + TI...  8.44 us
    ppermute x2, starting transfers between devices, halo_of(): lax.ppermute(side_part, 'side', [(0, 1), (1, 0)])  7.37 us
    pallas_call x2, Pallas kernels, local(): pl.pallas_call(local_kernel, in_specs=[SMEM] + [VMEM] * 4, out_shape=jax....  7.09 us
    pallas_call x1, Pallas kernels, first(): pl.pallas_call(first_kernel, grid=(1,), in_specs=[SMEM, SMEM] + [VMEM] *...  6.26 us
    pallas_call x1, Pallas kernels, second(): pl.pallas_call(second_kernel, grid=(1,), in_specs=[SMEM, SMEM] + [VMEM] *...  4.53 us
  transfers between devices with their start and end apart: 8, of which 4 were waited for; matrix products, arithmetic and copies ran while one was open for 0% of the time, Pallas kernels for 8%

profile of v10, /device:TPU:1, one launch (start us, length us, event | category | flops | bytes accessed | tf_op | source)
XLA Modules:
  0.0 92.9 jit_solution(8521199059184743372)
XLA Ops:
  0.6 3.8 %prepare.1 = (bf16[3072,256]{1,0:T(8,128)(2,1)S(1)}, bf16[2048,128]{1,0:T(8,128)(2,1)S(1)}, bf16[64,2048]{1,0:T(8,128)(2,1)S(1)}, f32[1024,128]{1,0:T(8,128)}, b...) custom-call(s32[2,24]{1,0:T(2,128)} %bitcast.29, ...), custom_call_target="tpu_custom_call" | custom-call | flops 1000000 | bytes 100000 | tf_op jit(solution)/shard_map/prepare/pallas_call | solution.py:164
  4.4 22.4 %all-to-all-start = ((bf16[256,8,128]{2,1,0:T(8,128)(2,1)}), bf16[256,8,128]{2,1,0:T(8,128)(2,1)S(1)}, u32[]{:S(2)}, u32[]{:S(2)}) async-start(bf16[256,8,128]{2,1,0:T(8,128)(2,1)} %bitcast.26), calls=%async_computation | async-start | bytes 1048576 | tf_op jit(solution)/shard_map/all_to_all | solution.py:377
  26.8 3.5 %collective-permute-start = (bf16[64,768]{1,0:T(8,128)(2,1)}, bf16[64,768]{1,0:T(8,128)(2,1)S(1)}, u32[]{:S(2)}, u32[]{:S(2)}) collective-permute-start(bf16[64,768]{1,0:T(8,128)(2,1)} %get-tuple-element.31), channel_id=1, source_target_pairs={{0,4},{4,8},{8,12},{12,16},{16,20},{20,24},{24,28},{28,32},{32,36}... | collective-permute-start | bytes 294920 | tf_op jit(solution)/shard_map/ppermute | solution.py:373
  30.3 1.9 %collective-permute-start.1 = (bf16[64,768]{1,0:T(8,128)(2,1)}, bf16[64,768]{1,0:T(8,128)(2,1)S(1)}, u32[]{:S(2)}, u32[]{:S(2)}) collective-permute-start(bf16[64,768]{1,0:T(8,128)(2,1)} %get-tuple-element.32), channel_id=1, source_target_pairs={{4,0},{8,4},{12,8},{16,12},{20,16},{24,20},{28,24},{32,28},{36,32}... | collective-permute-start | bytes 294920 | tf_op jit(solution)/shard_map/ppermute | solution.py:373
  32.2 4.0 %collective-permute-start.2 = (bf16[64,512]{1,0:T(8,128)(2,1)}, bf16[64,512]{1,0:T(8,128)(2,1)S(1)}, u32[]{:S(2)}, u32[]{:S(2)}) collective-permute-start(bf16[64,512]{1,0:T(8,128)(2,1)} %get-tuple-element.33), channel_id=1, source_target_pairs={{0,1},{1,0},{2,3},{3,2},{4,5},{5,4},{6,7},{7,6},{8,9},{9,8},{10,11... | collective-permute-start | bytes 196616 | tf_op jit(solution)/shard_map/ppermute | solution.py:404
  36.2 3.5 %local.2.local_ref = f32[64,3072]{1,0:T(8,128)} custom-call(s32[2,24]{1,0:T(2,128)} %bitcast.30, bf16[64,3072]{1,0:T(8,128)(2,1)} %bitcast.21, bf16[24,128,128]{2,1,0:T(8,128)(2,1)} %onsite_ref.3, bf16[24,128,128]{2,1,0:T(8,128)(2,1)} %down_ref.9, bf16[24,128,128]{2,1,0:T(8,128)(2,1)} %right_ref.3), custom_call_target="tpu_custom_call" | custom-call | flops 1000000 | bytes 100000 | tf_op jit(solution)/shard_map/local/pallas_call | solution.py:319
  39.8 6.0 %collective-permute-done.2.side_ref = bf16[64,512]{1,0:T(8,128)(2,1)S(1)} collective-permute-done((bf16[64,512]{1,0:T(8,128)(2,1)}, bf16[64,512]{1,0:T(8,128)(2,1)S(1)}, u32[]{:S(2)}, u32[]{:S(2)}) %collective-permute-start.2) | collective-permute-done | bytes 65568 | tf_op jit(solution)/shard_map/ppermute | solution.py:404
  45.7 0.0 collective-permute-done.above_ref
  45.8 0.0 collective-permute-done.1.below_ref
  45.8 3.7 %all-to-all-done = bf16[256,8,128]{2,1,0:T(8,128)(2,1)S(1)} async-done(((bf16[256,8,128]{2,1,0:T(8,128)(2,1)}), bf16[256,8,128]{2,1,0:T(8,128)(2,1)S(1)}, u32[]{:S(2)}, u32[]{:S(2)}) %all-to-all-start) | async-done | bytes 524320 | tf_op jit(solution)/shard_map/all_to_all | solution.py:377
  49.5 6.3 %first.1 = (f32[64,3072]{1,0:T(8,128)}, bf16[64,3072]{1,0:T(8,128)(2,1)}, f32[2,4,3072]{2,1,0:T(4,128)}, bf16[64,768]{1,0:T(8,128)(2,1)}, bf16[64,768]{1,0:T(8,1...) custom-call(s32[2,24]{1,0:T(2,128)} %bitcast.31, s32[1]{0:T(128)} %bitcast.1.left_ref, ...), custom_call_target="tpu_custom_call" | custom-call | flops 1000000 | bytes 100000 | tf_op jit(solution)/shard_map/first/pallas_call | solution.py:298
  55.7 10.2 %all-to-all-start.1 = ((bf16[256,8,128]{2,1,0:T(8,128)(2,1)}), bf16[256,8,128]{2,1,0:T(8,128)(2,1)S(1)}, u32[]{:S(2)}, u32[]{:S(2)}) async-start(bf16[256,8,128]{2,1,0:T(8,128)(2,1)} %bitcast.25), calls=%async_computation.1 | async-start | bytes 1048576 | tf_op jit(solution)/shard_map/all_to_all | solution.py:377
  65.9 3.5 %collective-permute-start.3 = (bf16[64,768]{1,0:T(8,128)(2,1)}, bf16[64,768]{1,0:T(8,128)(2,1)S(1)}, u32[]{:S(2)}, u32[]{:S(2)}) collective-permute-start(bf16[64,768]{1,0:T(8,128)(2,1)} %get-tuple-element.46), channel_id=1, source_target_pairs={{0,4},{4,8},{8,12},{12,16},{16,20},{20,24},{24,28},{28,32},{32,36}... | collective-permute-start | bytes 294920 | tf_op jit(solution)/shard_map/ppermute | solution.py:373
  69.5 1.9 %collective-permute-start.4 = (bf16[64,768]{1,0:T(8,128)(2,1)}, bf16[64,768]{1,0:T(8,128)(2,1)S(1)}, u32[]{:S(2)}, u32[]{:S(2)}) collective-permute-start(bf16[64,768]{1,0:T(8,128)(2,1)} %get-tuple-element.47), channel_id=1, source_target_pairs={{4,0},{8,4},{12,8},{16,12},{20,16},{24,20},{28,24},{32,28},{36,32}... | collective-permute-start | bytes 294920 | tf_op jit(solution)/shard_map/ppermute | solution.py:373
  71.4 3.4 %collective-permute-start.5 = (bf16[64,512]{1,0:T(8,128)(2,1)}, bf16[64,512]{1,0:T(8,128)(2,1)S(1)}, u32[]{:S(2)}, u32[]{:S(2)}) collective-permute-start(bf16[64,512]{1,0:T(8,128)(2,1)} %get-tuple-element.48), channel_id=1, source_target_pairs={{0,1},{1,0},{2,3},{3,2},{4,5},{5,4},{6,7},{7,6},{8,9},{9,8},{10,11... | collective-permute-start | bytes 196616 | tf_op jit(solution)/shard_map/ppermute | solution.py:404
  74.8 3.5 %local.3.local_ref = f32[64,3072]{1,0:T(8,128)} custom-call(s32[2,24]{1,0:T(2,128)} %bitcast.32, bf16[64,3072]{1,0:T(8,128)(2,1)} %get-tuple-element.45.x_ref, bf16[24,128,128]{2,1,0:T(8,128)(2,1)} %onsite_ref.3, bf16[24,128,128]{2,1,0:T(8,128)(2,1)} %down_ref.9, bf16[24,128,128]{2,1,0:T(8,128)(2,1)} %right_ref.3), custom_call_target="tpu_custom_call" | custom-call | flops 1000000 | bytes 100000 | tf_op jit(solution)/shard_map/local/pallas_call | solution.py:319
  78.3 5.3 %collective-permute-done.5.side_ref = bf16[64,512]{1,0:T(8,128)(2,1)S(1)} collective-permute-done((bf16[64,512]{1,0:T(8,128)(2,1)}, bf16[64,512]{1,0:T(8,128)(2,1)S(1)}, u32[]{:S(2)}, u32[]{:S(2)}) %collective-permute-start.5) | collective-permute-done | bytes 65568 | tf_op jit(solution)/shard_map/ppermute | solution.py:404
  83.6 0.0 collective-permute-done.3.above_ref
  83.6 0.0 collective-permute-done.4.below_ref
  83.6 4.7 %all-to-all-done.1 = bf16[256,8,128]{2,1,0:T(8,128)(2,1)S(1)} async-done(((bf16[256,8,128]{2,1,0:T(8,128)(2,1)}), bf16[256,8,128]{2,1,0:T(8,128)(2,1)S(1)}, u32[]{:S(2)}, u32[]{:S(2)}) %all-to-all-start.1) | async-done | bytes 524320 | tf_op jit(solution)/shard_map/all_to_all | solution.py:377
  88.4 4.5 %second.1 = (f32[64,3072]{1,0:T(8,128)}, f32[3,4,3072]{2,1,0:T(4,128)}) custom-call(s32[2,24]{1,0:T(2,128)} %bitcast.33, s32[1]{0:T(128)} %bitcast.1.left_ref, bf16[2,1024,128]{2,1,0:T(8,128)(2,1)S(1)} %bitcast.16, bf16[64,768]{1,0:T(8,128)(2,1)S(1)} %collective-permute-done.3.above_ref, bf16[64,768]{1,0:T(8,128)(2,1)S(1)} %collective-permute-done.4.below_ref, ...), custom_call_target="tpu_custom_call" | custom-call | flops 1000000 | bytes 100000 | tf_op jit(solution)/shard_map/second/pallas_call | solution.py:354
Async XLA Ops:
  4.4 45.1 %all-to-all-start = ((bf16[256,8,128]{2,1,0:T(8,128)(2,1)}), bf16[256,8,128]{2,1,0:T(8,128)(2,1)S(1)}, u32[]{:S(2)}, u32[]{:S(2)}) async-start(bf16[256,8,128]{2,1,0:T(8,128)(2,1)} %bitcast.26), calls=%async_computation | async-start | bytes 1048576 | tf_op jit(solution)/shard_map/all_to_all | solution.py:377
  26.8 19.0 %collective-permute-start = (bf16[64,768]{1,0:T(8,128)(2,1)}, bf16[64,768]{1,0:T(8,128)(2,1)S(1)}, u32[]{:S(2)}, u32[]{:S(2)}) collective-permute-start(bf16[64,768]{1,0:T(8,128)(2,1)} %get-tuple-element.31), channel_id=1, source_target_pairs={{0,4},{4,8},{8,12},{12,16},{16,20},{20,24},{24,28},{28,32},{32,36}... | collective-permute-start | bytes 294920 | tf_op jit(solution)/shard_map/ppermute | solution.py:373
  30.3 15.4 %collective-permute-start.1 = (bf16[64,768]{1,0:T(8,128)(2,1)}, bf16[64,768]{1,0:T(8,128)(2,1)S(1)}, u32[]{:S(2)}, u32[]{:S(2)}) collective-permute-start(bf16[64,768]{1,0:T(8,128)(2,1)} %get-tuple-element.32), channel_id=1, source_target_pairs={{4,0},{8,4},{12,8},{16,12},{20,16},{24,20},{28,24},{32,28},{36,32}... | collective-permute-start | bytes 294920 | tf_op jit(solution)/shard_map/ppermute | solution.py:373
  32.2 13.5 %collective-permute-start.2 = (bf16[64,512]{1,0:T(8,128)(2,1)}, bf16[64,512]{1,0:T(8,128)(2,1)S(1)}, u32[]{:S(2)}, u32[]{:S(2)}) collective-permute-start(bf16[64,512]{1,0:T(8,128)(2,1)} %get-tuple-element.33), channel_id=1, source_target_pairs={{0,1},{1,0},{2,3},{3,2},{4,5},{5,4},{6,7},{7,6},{8,9},{9,8},{10,11... | collective-permute-start | bytes 196616 | tf_op jit(solution)/shard_map/ppermute | solution.py:404
  55.7 32.6 %all-to-all-start.1 = ((bf16[256,8,128]{2,1,0:T(8,128)(2,1)}), bf16[256,8,128]{2,1,0:T(8,128)(2,1)S(1)}, u32[]{:S(2)}, u32[]{:S(2)}) async-start(bf16[256,8,128]{2,1,0:T(8,128)(2,1)} %bitcast.25), calls=%async_computation.1 | async-start | bytes 1048576 | tf_op jit(solution)/shard_map/all_to_all | solution.py:377
  65.9 17.7 %collective-permute-start.3 = (bf16[64,768]{1,0:T(8,128)(2,1)}, bf16[64,768]{1,0:T(8,128)(2,1)S(1)}, u32[]{:S(2)}, u32[]{:S(2)}) collective-permute-start(bf16[64,768]{1,0:T(8,128)(2,1)} %get-tuple-element.46), channel_id=1, source_target_pairs={{0,4},{4,8},{8,12},{12,16},{16,20},{20,24},{24,28},{28,32},{32,36}... | collective-permute-start | bytes 294920 | tf_op jit(solution)/shard_map/ppermute | solution.py:373
  69.5 14.2 %collective-permute-start.4 = (bf16[64,768]{1,0:T(8,128)(2,1)}, bf16[64,768]{1,0:T(8,128)(2,1)S(1)}, u32[]{:S(2)}, u32[]{:S(2)}) collective-permute-start(bf16[64,768]{1,0:T(8,128)(2,1)} %get-tuple-element.47), channel_id=1, source_target_pairs={{4,0},{8,4},{12,8},{16,12},{20,16},{24,20},{28,24},{32,28},{36,32}... | collective-permute-start | bytes 294920 | tf_op jit(solution)/shard_map/ppermute | solution.py:373
  71.4 12.2 %collective-permute-start.5 = (bf16[64,512]{1,0:T(8,128)(2,1)}, bf16[64,512]{1,0:T(8,128)(2,1)S(1)}, u32[]{:S(2)}, u32[]{:S(2)}) collective-permute-start(bf16[64,512]{1,0:T(8,128)(2,1)} %get-tuple-element.48), channel_id=1, source_target_pairs={{0,1},{1,0},{2,3},{3,2},{4,5},{5,4},{6,7},{7,6},{8,9},{9,8},{10,11... | collective-permute-start | bytes 196616 | tf_op jit(solution)/shard_map/ppermute | solution.py:404
